TPU v7x, 32 devices: a whole 2x2x4 slice. The times are simulated.
32 devices in a mesh: ckpt: 4 (over x, core), tensor: 8 (over z, y).
Axes of the slice: x: 2, y: 2, z: 4, core: 2. Of those that a mesh axis runs over, the one named last changes fastest.
Arguments:
- delta: bfloat16 [4, 2, 2048, 16384], P('ckpt', None, None, 'tensor'), may hold values from -0.03125 to 0.03125
- drop_mask: int32 [4, 2, 16, 128], P('ckpt', None, None, 'tensor'), may hold values 0 or 1
- scale_num: int32 [4], P('ckpt'), may hold values from 4 to 39
- base: bfloat16 [2, 2048, 16384], P(None, 'ckpt', 'tensor'), may hold values from -0.046875 to 0.046875
- tokens: bfloat16 [256, 16384], P(('tensor', 'ckpt')), may hold values from -6 to 6
Outputs:
- hidden: bfloat16 [256, 2048], P('tensor', 'ckpt')
Inputs may be any that keep to these rules, and one draw needn't show every extreme that they name: drop_mask holds only 0 and 1. A checkpoint's scale is scale_num / 16.
All inputs are finite; a program needn't handle non-finite values. No bound on the sum of `drop_mask` on one device may be relied on, other than what follows from the above.
Results may differ from a plain program's by a relative error of at most 0.015.
Values may be sent and summed in bfloat16 or wider, within the bound.
No kernel may reach another device: no remote copies, remote signals or barrier semaphores. Data moves between devices by JAX's collectives and lax.ppermute only.
A program may use at most 192 MiB of HBM per device.

v0:
```python
import jax
import jax.numpy as jnp
from jax import lax
from jax.sharding import PartitionSpec as P

BLOCK = 128
DEN = 16


def local(delta, drop_mask, scale_num, base, tokens):
    slab_loc = delta.shape[2]
    width_loc = delta.shape[3]
    factor = drop_mask[0].astype(jnp.float32) * (scale_num[0].astype(jnp.float32) / DEN)
    shaped = delta[0].reshape(2, slab_loc // BLOCK, BLOCK, width_loc // BLOCK, BLOCK)
    term = (shaped.astype(jnp.float32) * factor[:, :, None, :, None]).reshape(
        2, slab_loc, width_loc
    )
    term = term.astype(jnp.bfloat16)
    summed = lax.psum_scatter(term, "ckpt", scatter_dimension=1, tiled=True).astype(jnp.float32)
    merged = (base.astype(jnp.float32) + summed).astype(jnp.bfloat16)
    row_block = lax.all_gather(tokens, "ckpt", axis=0, tiled=True)
    products = jnp.einsum(
        "td,msd->tms",
        row_block,
        lax.all_gather(merged, "tensor", axis=2, tiled=True),
        preferred_element_type=jnp.float32,
    )
    return (jax.nn.silu(products[:, 0]) * products[:, 1]).astype(jnp.bfloat16)


def solution(mesh):
    in_specs = (
        P("ckpt", None, None, "tensor"),
        P("ckpt", None, None, "tensor"),
        P("ckpt"),
        P(None, "ckpt", "tensor"),
        P(("tensor", "ckpt"), None),
    )
    out_specs = P("tensor", "ckpt")
    return jax.shard_map(local, mesh=mesh, in_specs=in_specs, out_specs=out_specs, check_vma=False)
```

profile of v0, /device:TPU:0, one launch (start us, length us, event | category | flops | bytes accessed | tf_op | source)
XLA Modules:
  0.0 886.9 jit_solution(1097242008520929067)
XLA Ops:
  6.5 0.0 reduce-scatter.2.cloned.1.call-start
  7.2 0.7 multiply_bitcast_fusion
  7.9 11.1 %mul.34 = f32[2,16,128,16,128]{4,3,2,1,0:T(8,128)} broadcast(f32[2,16,16]{2,1,0:T(8,128)S(1)} %multiply_bitcast_fusion), dimensions={0,1,3} | broadcast | bytes 33556480 | tf_op jit(solution)/shard_map/mul | solution.py:15
  19.0 35.5 %mul.35 = f32[2,2048,2048]{2,1,0:T(8,128)} reshape(f32[2,16,128,16,128]{4,3,2,1,0:T(8,128)} %mul.34) | data formatting | bytes 67108864 | tf_op jit(solution)/shard_map/mul | solution.py:15
  54.5 22.3 %fusion = bf16[2,2048,2048]{2,1,0:T(8,128)(2,1)} fusion(f32[2,2048,2048]{2,1,0:T(8,128)} %mul.35, bf16[1,2,2048,2048]{3,2,1,0:T(8,128)(2,1)} %param.5), kind=kLoop, calls=%fused_computation.1 | loop fusion | flops 25165824 | bytes 67108864 | tf_op jit(solution)/shard_map/convert_element_type | solution.py:18
  76.7 0.0 reduce-scatter.2.cloned.1.call-update
  76.7 0.0 all-gather.5.cloned.1.call-start
  76.8 0.7 all-gather.5.cloned.1.call-update
  77.5 0.0 all-gather.3.cloned.1.call-start
  77.5 128.2 %reduce-scatter.2.cloned.1.call-done = bf16[2,512,2048]{2,1,0:T(8,128)(2,1)} async-done(((bf16[2,2048,2048]{2,1,0:T(8,128)(2,1)}), bf16[2,512,2048]{2,1,0:T(8,128)(2,1)}) %reduce-scatter.2.cloned.1.call-update) | async-done | bytes 4194320 | tf_op jit(solution)/shard_map/reduce_scatter | solution.py:19
  205.7 7.8 add_convert_fusion
  213.5 0.0 all-gather.3.cloned.1.call-update
  213.6 10.6 %all-gather.5.cloned.1.call-done = bf16[32,16384]{1,0:T(8,128)(2,1)} async-done(((bf16[8,16384]{1,0:T(8,128)(2,1)}), bf16[32,16384]{1,0:T(8,128)(2,1)}) %all-gather.5.cloned.1.call-update) | async-done | bytes 1048592 | tf_op jit(solution)/shard_map/all_gather | solution.py:21
  224.1 639.4 %all-gather.3.cloned.1.call-done = bf16[2,512,16384]{2,1,0:T(8,128)(2,1)} async-done(((bf16[2,512,2048]{2,1,0:T(8,128)(2,1)}), bf16[2,512,16384]{2,1,0:T(8,128)(2,1)}) %all-gather.3.cloned.1.call-update) | async-done | bytes 33554448 | tf_op jit(solution)/shard_map/all_gather | solution.py:25
  863.5 16.2 %convolution_bitcast_fusion = f32[32,2,512]{2,0,1:T(8,128)S(1)} fusion(bf16[2,512,16384]{2,1,0:T(8,128)(2,1)} %all-gather.3.cloned.1.call-done, bf16[32,16384]{1,0:T(8,128)(2,1)} %all-gather.5.cloned.1.call-done), kind=kOutput, calls=%fused_computation.3 | convolution fusion | flops 1073741824 | bytes 34734080 | tf_op jit(solution)/shard_map/td,msd->tms/dot_general | solution.py:22
  879.7 0.7 fusion.3
Async XLA Ops:
  6.5 199.2 %reduce-scatter.2.cloned.1.call-start = ((), (), s32[]{:S(2)}) async-start(), calls=%async_computation.1 | async-start | bytes 20971520 | tf_op jit(solution)/shard_map/reduce_scatter | solution.py:19
  76.7 147.4 %all-gather.5.cloned.1.call-start = ((), (), s32[]{:S(2)}) async-start(), calls=%async_computation.3 | async-start | bytes 1310720 | tf_op jit(solution)/shard_map/all_gather | solution.py:21
  77.5 786.0 %all-gather.3.cloned.1.call-start = ((), (), s32[]{:S(2)}) async-start(), calls=%async_computation.2 | async-start | bytes 37748736 | tf_op jit(solution)/shard_map/all_gather | solution.py:25
Sparse Core Ops, SparseCore 0:
  76.9 128.8 reduce-scatter.1
  207.4 16.7 all-gather.4
  225.8 637.7 all-gather.2
where the time goes:
time: 888 us; the launch traced here: 887 us
  waiting for transfers between devices  779 us (88%)
  local copies, waits for them, and re-layouts  46.5 us (5%)
  other arithmetic  31.4 us (4%)
  matrix products  16.2 us (2%)
  between operations  13.8 us (2%)
    all_gather x1, waiting for transfers between devices, local(): lax.all_gather(merged, 'tensor', axis=2, tiled=True)  639 us
    reduce_scatter x1, waiting for transfers between devices, local(): lax.psum_scatter(term, 'ckpt', scatter_dimension=1, tiled=True)  128 us
    mul x2, local copies, waits for them, and re-layouts, local(): shaped.astype(jnp.float32) * factor[:, :, None, :, None]  46.5 us
    convert_element_type x1, other arithmetic, local(): term = term.astype(jnp.bfloat16)  22.3 us
  transfers between devices with their start and end apart: 3, of which 3 were waited for; matrix products, arithmetic and copies ran while one was open for 1% of the time, Pallas kernels for 0%

commit v1 on v0

v1 whole, which is shorter than its diff:
```python
import functools

import jax
import jax.numpy as jnp
from jax import lax
from jax.experimental import pallas as pl
from jax.experimental.pallas import tpu as pltpu
from jax.sharding import PartitionSpec as P

BLOCK = 128
DEN = 16
CORES = 2
MIB = 1 << 20


def masked_rows(mask_ref, delta_ref, kept, m, row_block):
    for i in range(kept.shape[0] // BLOCK):
        for j in range(kept.shape[1] // BLOCK):
            keep = mask_ref[m, row_block * (kept.shape[0] // BLOCK) + i, j] != 0
            here = (slice(i * BLOCK, (i + 1) * BLOCK), slice(j * BLOCK, (j + 1) * BLOCK))
            piece = delta_ref[0, here[0], here[1]]
            kept[here] = jnp.where(keep, piece, jnp.zeros_like(piece))


def dot_rows(tokens, weights):
    return lax.dot_general(
        tokens, weights, (((1,), (1,)), ((), ())), preferred_element_type=jnp.float32
    )


def partial_kernel(with_base, rows, place_ref, scale_ref, mask_ref, own_ref, sib_ref, delta_ref, *rest):
    if with_base:
        base_ref, out_ref, held, kept = rest
    else:
        out_ref, held, kept = rest
    row, core = place_ref[0], place_ref[1]
    target = place_ref[2]
    step, m = pl.program_id(0), pl.program_id(1)

    @pl.when((step == 0) & (m == 0))
    def _():
        half = own_ref.shape[0]
        held[:half] = own_ref[...]
        held[half:] = sib_ref[...]

    masked_rows(mask_ref, delta_ref, kept, m, step * CORES + target)
    scale = scale_ref[0].astype(jnp.float32) / DEN

    def put(total):
        groups = out_ref.shape[1]
        split = total.reshape(CORES, -1, groups, rows, total.shape[-1])
        span = split.shape[1] * rows
        for side, at in ((0, core), (1, 1 - core)):
            for g in range(groups):
                piece = split[side, :, g].reshape(span, -1).astype(out_ref.dtype)
                out_ref[0, g, pl.ds(pl.multiple_of(at * span, span), span), :] = piece

    product = scale * dot_rows(held[...], kept[...])
    if with_base:

        @pl.when(step == row)
        def _():
            put(product + dot_rows(held[...], base_ref[0]))

        @pl.when(step != row)
        def _():
            put(product)

    else:
        put(product)


def partials(place, scale_num, mask, own, sib, delta, base, slab_own, groups, rows):
    width = delta.shape[2]
    owners = delta.shape[1] // slab_own // CORES
    span = 2 * own.shape[0] // groups
    whole = lambda *_: (0, 0)
    in_specs = [
        pl.BlockSpec(own.shape, whole),
        pl.BlockSpec(sib.shape, whole),
        pl.BlockSpec((1, slab_own, width), lambda x, m, place, *_: (m, x * CORES + place[2], 0)),
    ]
    operands = [own, sib, delta]
    if base is not None:
        in_specs.append(pl.BlockSpec((1, slab_own, width), lambda x, m, *_: (m, 0, 0)))
        operands.append(base)
    out_dtype = jnp.bfloat16 if base is None else jnp.float32
    flops = 2 * 2 * own.shape[0] * width * 2 * slab_own * owners
    return pl.pallas_call(
        functools.partial(partial_kernel, base is not None, rows),
        out_shape=jax.ShapeDtypeStruct((owners, groups, span, 2 * slab_own), out_dtype),
        grid_spec=pltpu.PrefetchScalarGridSpec(
            num_scalar_prefetch=3,
            grid=(owners, 2),
            in_specs=in_specs,
            out_specs=pl.BlockSpec((1, groups, span, slab_own), lambda x, m, *_: (x, 0, 0, m)),
            scratch_shapes=[
                pltpu.VMEM((2 * own.shape[0], width), jnp.bfloat16),
                pltpu.VMEM((slab_own, width), jnp.bfloat16),
            ],
        ),
        compiler_params=pltpu.CompilerParams(vmem_limit_bytes=40 * MIB),
        cost_estimate=pl.CostEstimate(
            flops=flops, bytes_accessed=2 * slab_own * owners * width * 2, transcendentals=0
        ),
    )(place, scale_num, mask, *operands)


def finish_kernel(rows, part_ref, out_ref, total):
    step = pl.program_id(0)
    here = jnp.sum(part_ref[...].astype(jnp.float32), axis=0)

    @pl.when(step == 0)
    def _():
        total[...] = here

    @pl.when(step != 0)
    def _():
        total[...] += here

    @pl.when(step == pl.num_programs(0) - 1)
    def _():
        slab_own = out_ref.shape[1]
        gate, up = total[:, :slab_own], total[:, slab_own:]
        value = gate / (1 + jnp.exp(-gate)) * up
        split = value.reshape(CORES, -1, rows, slab_own)
        pieces = [split[core, x] for x in range(split.shape[1]) for core in range(CORES)]
        out_ref[...] = jnp.concatenate(pieces, axis=0).astype(out_ref.dtype)


def finish(parts, rows):
    sources, span, both = parts.shape
    block = min(sources, 16)
    return pl.pallas_call(
        functools.partial(finish_kernel, rows),
        out_shape=jax.ShapeDtypeStruct((span, both // 2), jnp.bfloat16),
        grid=(sources // block,),
        in_specs=[pl.BlockSpec((block, span, both), lambda i: (i, 0, 0))],
        out_specs=pl.BlockSpec((span, both // 2), lambda i: (0, 0)),
        scratch_shapes=[pltpu.VMEM((span, both), jnp.float32)],
        compiler_params=pltpu.CompilerParams(vmem_limit_bytes=32 * MIB),
        cost_estimate=pl.CostEstimate(
            flops=parts.size, bytes_accessed=2 * parts.size, transcendentals=span * both // 2
        ),
    )(parts)


def solution(mesh):
    ckpts, groups = mesh.shape["ckpt"], mesh.shape["tensor"]
    owners = ckpts // CORES
    both = ("ckpt", "tensor")
    same_core = [
        [(x * CORES + core) * groups + t for x in range(owners) for t in range(groups)]
        for core in range(CORES)
    ]
    swap = [(i, i ^ 1) for i in range(ckpts)]

    def local(delta, drop_mask, scale_num, base, tokens):
        rows, width = tokens.shape
        width //= groups
        slab_own = base.shape[1]
        me = lax.axis_index("ckpt")
        row, core = me // CORES, me % CORES

        cut = tokens.reshape(rows, groups, width).transpose(1, 0, 2)
        send = jnp.broadcast_to(cut[None], (owners, groups, rows, width)).reshape(-1, rows, width)
        own = lax.all_to_all(send, both, 0, 0, axis_index_groups=same_core, tiled=True)
        own = own.reshape(owners * groups * rows, width)
        sib = lax.ppermute(own, "ckpt", swap)

        place = jnp.stack([row, core, 1 - core]).astype(jnp.int32)
        theirs = partials(
            place, scale_num, drop_mask[0], own, sib, delta[0], None, slab_own, groups, rows
        )
        arrived = lax.ppermute(theirs, "ckpt", swap)
        place = jnp.stack([row, core, core]).astype(jnp.int32)
        ours = partials(
            place, scale_num, drop_mask[0], own, sib, delta[0], base, slab_own, groups, rows
        )
        chip = (ours + arrived.astype(jnp.float32)).astype(jnp.bfloat16)
        chip = chip.reshape(owners * groups, -1, 2 * slab_own)
        parts = lax.all_to_all(chip, both, 0, 0, axis_index_groups=same_core, tiled=True)
        return finish(parts, rows)

    in_specs = (
        P("ckpt", None, None, "tensor"),
        P("ckpt", None, None, "tensor"),
        P("ckpt"),
        P(None, "ckpt", "tensor"),
        P(("tensor", "ckpt"), None),
    )
    out_specs = P("tensor", "ckpt")
    return jax.shard_map(local, mesh=mesh, in_specs=in_specs, out_specs=out_specs, check_vma=False)
```

time: 888 us -> 74.5 us (0.08)
  waiting for transfers between devices: 779 us -> 1.18 us
  blocking collectives: 0 us -> 53.5 us
  local copies, waits for them, and re-layouts: 46.5 us -> 1.72 us
  other arithmetic: 31.4 us -> 0.52 us
  Pallas kernels: 0 us -> 16.3 us
  matrix products: 16.2 us -> 0 us
  between operations: 13.8 us -> 0.7 us
    all_gather x2 -> x0, waiting for transfers between devices: 650 us -> none  [the longest x1 639 us: local(): lax.all_gather(merged, 'tensor', axis=2, tiled=True)]
    reduce_scatter x1 -> x0, waiting for transfers between devices: 128 us -> none  [local(): lax.psum_scatter(term, 'ckpt', scatter_dimension=1, tiled=True)]
    all_to_all x0 -> x2, blocking collectives: none -> 53.5 us  [the longest x1 30.1 us: local(): lax.all_to_all(chip, both, 0, 0, axis_index_groups=same_core, tiled=True)]
    mul x2 -> x0, local copies, waits for them, and re-layouts: 46.5 us -> none  [local(): shaped.astype(jnp.float32) * factor[:, :, None, :, None]]
    convert_element_type x3 -> x1, other arithmetic: 30.7 us -> 0.37 us  [local(): chip = (ours + arrived.astype(jnp.float32)).astype(jnp.bfloat16)]
    pallas_call x0 -> x3, Pallas kernels: none -> 16.3 us  [the longest x2 15.5 us: partials(): pl.pallas_call(functools.partial(partial_kernel, base is not None, rows),...]
    dot_general x1 -> x0, matrix products: 16.2 us -> none  [local(): jnp.einsum('td,msd->tms', row_block, lax.all_gather(merged, 'tensor', axi...]
  transfers between devices with their start and end apart: 3 -> 2, of which waited for: 3 -> 1; matrix products, arithmetic and copies ran while one was open for 1% -> 0% of each run, Pallas kernels for 0% -> 11%
where the time goes in v1:
time: 74.5 us; the launch traced here: 74.1 us
  blocking collectives  53.5 us (72%)
  Pallas kernels  16.3 us (22%)
  local copies, waits for them, and re-layouts  1.72 us (2%)
  waiting for transfers between devices  1.18 us (2%)
    all_to_all x1, blocking collectives, local(): lax.all_to_all(chip, both, 0, 0, axis_index_groups=same_core, tiled=True)  30.1 us
    all_to_all x1, blocking collectives, local(): lax.all_to_all(send, both, 0, 0, axis_index_groups=same_core, tiled=True)  23.4 us
    pallas_call x2, Pallas kernels, partials(): pl.pallas_call(functools.partial(partial_kernel, base is not None, rows),...  15.5 us
  transfers between devices with their start and end apart: 2, of which 1 were waited for; matrix products, arithmetic and copies ran while one was open for 0% of the time, Pallas kernels for 11%

profile of v1, /device:TPU:0, one launch (start us, length us, event | category | flops | bytes accessed | tf_op | source)
XLA Modules:
  0.0 74.1 jit_solution(2792514302433760669)
XLA Ops:
  0.0 1.0 %broadcast_in_dim.2 = bf16[2,8,8,2048]{3,2,1,0:T(8,128)(2,1)S(1)} broadcast(bf16[8,8,2048]{2,1,0:T(8,128)(2,1)} %bitcast.20), dimensions={1,2,3} | broadcast | bytes 786432 | tf_op jit(solution)/shard_map/broadcast_in_dim | solution.py:166
  1.0 23.4 %all_to_all.10 = bf16[16,8,2048]{2,1,0:T(8,128)(2,1)S(1)} all-to-all(bf16[16,8,2048]{2,1,0:T(8,128)(2,1)S(1)} %bitcast.19), channel_id=1, replica_groups={{0,1,2,3,4,5,6,7,16,17,18,19,20,21,22,23},{8,9,10,11,12,13,14,15,24,25,..., dimensions={0} | all-to-all | bytes 1048576 | tf_op jit(solution)/shard_map/all_to_all | solution.py:167
  24.4 0.0 collective-permute-start
  25.0 0.1 pad_add_fusion.2.place_ref
  25.1 1.2 %collective-permute-done.sib_ref = bf16[128,2048]{1,0:T(8,128)(2,1)S(1)} collective-permute-done((bf16[128,2048]{1,0:T(8,128)(2,1)S(1)}, bf16[128,2048]{1,0:T(8,128)(2,1)S(1)}, u32[]{:S(2)}, u32[]{:S(2)}) %collective-permute-start) | collective-permute-done | bytes 524320 | tf_op jit(solution)/shard_map/ppermute | solution.py:169
  26.3 0.0 copy-start.1
  26.3 0.7 copy-done.1
  27.0 0.0 copy-start
  27.0 0.0 copy-start.2
  27.0 7.3 %shard_map.56 = bf16[2,8,32,1024]{3,2,1,0:T(8,128)(2,1)S(1)} custom-call(s32[3]{0:T(128)S(1)} %pad_add_fusion.2.place_ref, s32[1]{0:T(128)S(6)} %copy.6.scale_ref, s32[2,16,16]{2,1,0:T(8,128)S(1)} %bitcast.14, bf16[128,2048]{1,0:T(8,128)(2,1)S(1)} %bitcast.12, bf16[128,2048]{1,0:T(8,128)(2,1)S(1)} %collective-permute-done.sib_ref, ...), custom_call_target="tpu_custom_call" | custom-call | flops 2147483648 | bytes 8388608 | tf_op jit(solution)/shard_map/pallas_call | solution.py:89
  34.3 0.2 collective-permute-start.1
  34.5 0.1 pad_add_fusion.place_ref
  34.5 0.0 copy-done
  34.5 0.0 copy-done.2
  34.5 8.3 %shard_map.55 = f32[2,8,32,1024]{3,2,1,0:T(8,128)S(1)} custom-call(s32[3]{0:T(128)S(1)} %pad_add_fusion.place_ref, s32[1]{0:T(128)S(6)} %copy.6.scale_ref, s32[2,16,16]{2,1,0:T(8,128)S(1)} %bitcast.15, bf16[128,2048]{1,0:T(8,128)(2,1)S(1)} %bitcast.13, bf16[128,2048]{1,0:T(8,128)(2,1)S(1)} %collective-permute-done.sib_ref, bf16[2,2048,2048]{2,1,0:T(8,128)(2,1)} %bitcast.17, ...), custom_call_target="tpu_custom_call" | custom-call | flops 2147483648 | bytes 8388608 | tf_op jit(solution)/shard_map/pallas_call | solution.py:89
  42.8 0.0 collective-permute-done.1
  42.8 0.4 add_convert_fusion
  43.2 30.1 %all_to_all.11.part_ref = bf16[16,32,1024]{2,1,0:T(8,128)(2,1)S(1)} all-to-all(bf16[16,32,1024]{2,1,0:T(8,128)(2,1)S(1)} %bitcast.18), channel_id=1, replica_groups={{0,1,2,3,4,5,6,7,16,17,18,19,20,21,22,23},{8,9,10,11,12,13,14,15,24,25,..., dimensions={0} | all-to-all | bytes 2097152 | tf_op jit(solution)/shard_map/all_to_all | solution.py:182
  73.3 0.8 %shard_map.57 = bf16[32,512]{1,0:T(8,128)(2,1)} custom-call(bf16[16,32,1024]{2,1,0:T(8,128)(2,1)S(1)} %all_to_all.11.part_ref), custom_call_target="tpu_custom_call" | custom-call | flops 524288 | bytes 1048576 | tf_op jit(solution)/shard_map/pallas_call | solution.py:134
Async XLA Ops:
  24.4 1.9 %collective-permute-start = (bf16[128,2048]{1,0:T(8,128)(2,1)S(1)}, bf16[128,2048]{1,0:T(8,128)(2,1)S(1)}, u32[]{:S(2)}, u32[]{:S(2)}) collective-permute-start(bf16[128,2048]{1,0:T(8,128)(2,1)S(1)} %bitcast.11), channel_id=1, source_target_pairs={{0,8},{8,0},{16,24},{24,16},{1,9},{9,1},{17,25},{25,17},{2,10},{10... | collective-permute-start | bytes 1572872 | tf_op jit(solution)/shard_map/ppermute | solution.py:169
  26.3 0.7 copy-start.1
  27.0 7.6 %copy-start = (bf16[2,512,2048]{2,1,0:T(8,128)(2,1)S(1)}, bf16[2,512,2048]{2,1,0:T(8,128)(2,1)}, u32[]{:S(2)}) copy-start(bf16[2,512,2048]{2,1,0:T(8,128)(2,1)} %rest_0_.1) | copy-start | bytes 12582916
  27.0 7.6 %copy-start.2 = (s32[1,2,16,16]{3,2,1,0:T(8,128)S(1)}, s32[1,2,16,16]{3,2,1,0:T(8,128)}, u32[]{:S(2)}) copy-start(s32[1,2,16,16]{3,2,1,0:T(8,128)} %param.6) | copy-start | bytes 6148
  34.3 8.6 %collective-permute-start.1 = (bf16[2,8,32,1024]{3,2,1,0:T(8,128)(2,1)S(1)}, bf16[2,8,32,1024]{3,2,1,0:T(8,128)(2,1)S(1)}, u32[]{:S(2)}, u32[]{:S(2)}) collective-permute-start(bf16[2,8,32,1024]{3,2,1,0:T(8,128)(2,1)S(1)} %shard_map.56), channel_id=1, source_target_pairs={{0,8},{8,0},{16,24},{24,16},{1,9},{9,1},{17,25},{25,17},{2,10},{10... | collective-permute-start | bytes 3145736 | tf_op jit(solution)/shard_map/ppermute | solution.py:175

commit v2 on v1

--- a/solution.py
+++ b/solution.py
@@ -11,6 +11,272 @@
 DEN = 16
 CORES = 2
 MIB = 1 << 20
+VMEM = pl.BlockSpec(memory_space=pltpu.VMEM)
+SMEM = pl.BlockSpec(memory_space=pltpu.SMEM)
+HBM = pl.BlockSpec(memory_space=pltpu.HBM)
+
+
+def dot_rows(tokens, weights):
+    return lax.dot_general(
+        tokens, weights, (((1,), (1,)), ((), ())), preferred_element_type=jnp.float32
+    )
+
+
+def silu_times(gate, up):
+    return gate / (1 + jnp.exp(-gate)) * up
+
+
+def gather_held(held, pieces):
+    for i, piece in enumerate(pieces):
+        span = piece.shape[0]
+        held[i * span : (i + 1) * span] = piece[...]
+
+
+def drop_blocks(mask_ref, kept, part, m, first):
+    rows, width = kept.shape[1:]
+    for i in range(rows // BLOCK):
+        for j in range(width // BLOCK):
+            here = (part, slice(i * BLOCK, (i + 1) * BLOCK), slice(j * BLOCK, (j + 1) * BLOCK))
+            piece = kept[here]
+            keep = mask_ref[m, first * (rows // BLOCK) + i, j] != 0
+            kept[here] = jnp.where(keep, piece, jnp.zeros_like(piece))
+
+
+def put(view, total, core):
+    groups, rows = view.shape[-5 if len(view.shape) == 5 else 0], view.shape[-2]
+    split = total.reshape(-1, CORES, groups, rows, total.shape[-1])
+    for x in range(split.shape[0]):
+        for side in range(CORES):
+            at = core if side == 0 else 1 - core
+            for g in range(groups):
+                here = (g, at) if len(view.shape) == 4 else (g, x, at)
+                view[here] = split[x, side, g].astype(view.dtype)
+
+
+def half_of(ref, m):
+    size = ref.shape[-1] // 2
+    return ref.at[(slice(None),) * (len(ref.shape) - 1) + (slice(m * size, (m + 1) * size),)]
+
+
+def fetch(delta, kept, sems, owners, chunks):
+    slab_own = kept.shape[1]
+    span = slab_own // chunks
+    copies = []
+    for part, (m, owner) in enumerate(owners):
+        for h in range(chunks):
+            rows = pl.ds(pl.multiple_of(owner * slab_own + h * span, span), span)
+            copy = pltpu.make_async_copy(
+                delta.at[m, rows, :], kept.at[part, pl.ds(h * span, span), :], sems.at[part, h]
+            )
+            copy.start()
+            copies.append(copy)
+    return copies
+
+
+def owners_of(chip, core):
+    return [(m, chip * CORES + core) for m in range(2)]
+
+
+def wait_for(copies, part, chunks):
+    for copy in copies[part * chunks : (part + 1) * chunks]:
+        copy.wait()
+
+
+def early_kernel(
+    place, scale_num, mask_hbm, own, sib, delta, theirs, ours, kept, held, mask, sems, mask_sem
+):
+    chip, core = place[0], place[1]
+    chunks = sems.shape[1]
+    mask_copy = pltpu.make_async_copy(mask_hbm, mask, mask_sem)
+    mask_copy.start()
+    owners = owners_of(1 - chip, 1 - core) + owners_of(1 - chip, core)
+    copies = fetch(delta, kept, sems, owners, chunks)
+    gather_held(held, (own, sib))
+    scale = scale_num[0].astype(jnp.float32) / DEN
+    mask_copy.wait()
+    for part, (m, owner) in enumerate(owners):
+        wait_for(copies, part, chunks)
+        drop_blocks(mask, kept, part, m, owner)
+        total = scale * dot_rows(held[...], kept[part])
+        put(half_of(theirs if part < 2 else ours, m), total, core)
+
+
+def later_kernel(
+    place, scale_num, mask_hbm, own, sib, far_own, far_sib, kept, delta, theirs, ours, theirs_home,
+    home, held, mask, sems, mask_sem,
+):
+    chip, core = place[0], place[1]
+    chunks = sems.shape[1]
+    half = held.shape[0] // 2
+    mask_copy = pltpu.make_async_copy(mask_hbm, mask, mask_sem)
+    mask_copy.start()
+    owners = owners_of(chip, 1 - core)
+    copies = fetch(delta, home, sems, owners, chunks)
+    gather_held(held, (own, sib, far_own, far_sib))
+    scale = scale_num[0].astype(jnp.float32) / DEN
+    for part in range(4):
+        total = scale * dot_rows(held[half:], kept[part])
+        put(half_of(theirs if part < 2 else ours, part % 2), total, core)
+    mask_copy.wait()
+    for part, (m, owner) in enumerate(owners):
+        wait_for(copies, part, chunks)
+        drop_blocks(mask, home, part, m, owner)
+        put(half_of(theirs_home, m), scale * dot_rows(held[...], home[part]), core)
+
+
+def home_kernel(
+    place, scale_num, mask_hbm, own, sib, far_own, far_sib, delta, base, ours,
+    kept, kept_base, held, mask, sems, base_sems, mask_sem,
+):
+    chip, core = place[0], place[1]
+    chunks = sems.shape[1]
+    mask_copy = pltpu.make_async_copy(mask_hbm, mask, mask_sem)
+    mask_copy.start()
+    owners = owners_of(chip, core)
+    copies = fetch(delta, kept, sems, owners, chunks)
+    base_copies = fetch(base, kept_base, base_sems, [(0, 0), (1, 0)], chunks)
+    gather_held(held, (own, sib, far_own, far_sib))
+    scale = scale_num[0].astype(jnp.float32) / DEN
+    mask_copy.wait()
+    for part, (m, owner) in enumerate(owners):
+        wait_for(copies, part, chunks)
+        drop_blocks(mask, kept, part, m, owner)
+        total = scale * dot_rows(held[...], kept[part])
+        wait_for(base_copies, part, chunks)
+        put(half_of(ours, m), total + dot_rows(held[...], kept_base[m]), core)
+
+
+def call(kernel, outs, scratch, in_specs, operands, flops, traffic):
+    return pl.pallas_call(
+        kernel,
+        out_shape=outs,
+        in_specs=in_specs,
+        out_specs=[VMEM] * len(outs),
+        scratch_shapes=scratch,
+        compiler_params=pltpu.CompilerParams(vmem_limit_bytes=50 * MIB),
+        cost_estimate=pl.CostEstimate(flops=flops // 8, bytes_accessed=traffic // 8, transcendentals=0),
+    )(*operands)
+
+
+def join_kernel(ours, arrived, out):
+    out[...] = (ours[...] + arrived[...].astype(jnp.float32)).astype(out.dtype)
+
+
+def join_home_kernel(ours, arrived, near, far, out):
+    for x, other in enumerate((near, far)):
+        total = ours[:, x] + arrived[:, x].astype(jnp.float32) + other[...].astype(jnp.float32)
+        out[:, x] = total.astype(out.dtype)
+
+
+def last_kernel(place, parts, out, total):
+    chip, core = place[0], place[1]
+    rows = parts.shape[-2]
+    slab_own = out.shape[1]
+    for x in range(2):
+        at = chip if x == 0 else 1 - chip
+        for c in range(CORES):
+            both = jnp.sum(parts[:, x, c].astype(jnp.float32), axis=0)
+            value = silu_times(both[:, :slab_own], both[:, slab_own:])
+            total[pl.ds(pl.multiple_of((at * CORES + c) * rows, rows), rows), :] = value
+    out[...] = total[...].astype(out.dtype)
+
+
+def local_pair(delta, drop_mask, scale_num, base, tokens, *, groups):
+    rows, width = tokens.shape[0], tokens.shape[1] // groups
+    slab_own = base.shape[1]
+    f32, bf16 = jnp.float32, jnp.bfloat16
+    me = lax.axis_index("ckpt")
+    place = jnp.stack([me >> 1, me & 1]).astype(jnp.int32)
+    mask, delta = drop_mask[0], delta[0]
+    core_swap = functools.partial(lax.ppermute, axis_name="ckpt", perm=[(i, i ^ 1) for i in range(4)])
+    chip_swap = functools.partial(lax.ppermute, axis_name="ckpt", perm=[(i, i ^ 2) for i in range(4)])
+
+    cut = tokens.reshape(rows, groups, width).transpose(1, 0, 2)
+    own = lax.all_to_all(cut, "tensor", 0, 0, tiled=True).reshape(groups * rows, width)
+    far_own = chip_swap(own)
+    sib = core_swap(own)
+
+    half = groups * rows * CORES
+    chunks = 2
+    part = jax.ShapeDtypeStruct
+    pair = (groups, CORES, rows, 2 * slab_own)
+    four = (groups, 2, CORES, rows, 2 * slab_own)
+    weights = (4, slab_own, width)
+    size = 4 * slab_own * width
+    theirs, ours, kept = call(
+        early_kernel,
+        [part(pair, bf16), part(pair, f32), part(weights, bf16)],
+        [
+            pltpu.VMEM((half, width), bf16),
+            pltpu.SMEM(mask.shape, mask.dtype),
+            pltpu.SemaphoreType.DMA((4, chunks)),
+            pltpu.SemaphoreType.DMA(()),
+        ],
+        [SMEM, SMEM, HBM, VMEM, VMEM, HBM],
+        (place, scale_num, mask, own, sib, delta),
+        2 * half * size,
+        2 * size,
+    )
+    near = core_swap(theirs)
+    far_own, theirs = lax.optimization_barrier((far_own, theirs))
+    far_sib = core_swap(far_own)
+    simple = lambda kernel, shape, *xs: pl.pallas_call(
+        kernel,
+        out_shape=part(shape, bf16),
+        in_specs=[VMEM] * len(xs),
+        out_specs=VMEM,
+        compiler_params=pltpu.CompilerParams(vmem_limit_bytes=16 * MIB),
+        cost_estimate=pl.CostEstimate(flops=xs[0].size, bytes_accessed=8 * xs[0].size, transcendentals=0),
+    )(*xs)
+    first, far_sib = lax.optimization_barrier((simple(join_kernel, pair, ours, near), far_sib))
+    over_first = chip_swap(first)
+    theirs, ours, theirs_home = call(
+        later_kernel,
+        [part(pair, bf16), part(pair, f32), part(four, bf16)],
+        [
+            pltpu.VMEM((2, slab_own, width), bf16),
+            pltpu.VMEM((2 * half, width), bf16),
+            pltpu.SMEM(mask.shape, mask.dtype),
+            pltpu.SemaphoreType.DMA((2, chunks)),
+            pltpu.SemaphoreType.DMA(()),
+        ],
+        [SMEM, SMEM, HBM, VMEM, VMEM, VMEM, VMEM, VMEM, HBM],
+        (place, scale_num, mask, own, sib, far_own, far_sib, kept, delta),
+        4 * half * size,
+        2 * size,
+    )
+    theirs, theirs_home, over_first = lax.optimization_barrier((theirs, theirs_home, over_first))
+    second = simple(join_kernel, pair, ours, core_swap(theirs))
+    near_home = core_swap(theirs_home)
+    second, own = lax.optimization_barrier((second, own))
+    over_second = chip_swap(second)
+    (ours,) = call(
+        home_kernel,
+        [part(four, f32)],
+        [
+            pltpu.VMEM((2, slab_own, width), bf16),
+            pltpu.VMEM((2, slab_own, width), bf16),
+            pltpu.VMEM((2 * half, width), bf16),
+            pltpu.SMEM(mask.shape, mask.dtype),
+            pltpu.SemaphoreType.DMA((2, chunks)),
+            pltpu.SemaphoreType.DMA((2, chunks)),
+            pltpu.SemaphoreType.DMA(()),
+        ],
+        [SMEM, SMEM, HBM, VMEM, VMEM, VMEM, VMEM, HBM, HBM],
+        (place, scale_num, mask, own, sib, far_own, far_sib, delta, base),
+        4 * half * size,
+        2 * size,
+    )
+    whole = simple(join_home_kernel, four, ours, near_home, over_second, over_first)
+    parts = lax.all_to_all(whole, "tensor", 0, 0, tiled=True)
+    return pl.pallas_call(
+        last_kernel,
+        out_shape=part((2 * CORES * rows, slab_own), bf16),
+        in_specs=[SMEM, VMEM],
+        out_specs=VMEM,
+        scratch_shapes=[pltpu.VMEM((2 * CORES * rows, slab_own), f32)],
+        compiler_params=pltpu.CompilerParams(vmem_limit_bytes=16 * MIB),
+    )(place, parts)
 
 
 def masked_rows(mask_ref, delta_ref, kept, m, row_block):
@@ -20,12 +286,6 @@
             here = (slice(i * BLOCK, (i + 1) * BLOCK), slice(j * BLOCK, (j + 1) * BLOCK))
             piece = delta_ref[0, here[0], here[1]]
             kept[here] = jnp.where(keep, piece, jnp.zeros_like(piece))
-
-
-def dot_rows(tokens, weights):
-    return lax.dot_general(
-        tokens, weights, (((1,), (1,)), ((), ())), preferred_element_type=jnp.float32
-    )
 
 
 def partial_kernel(with_base, rows, place_ref, scale_ref, mask_ref, own_ref, sib_ref, delta_ref, *rest):
@@ -46,7 +306,7 @@
     masked_rows(mask_ref, delta_ref, kept, m, step * CORES + target)
     scale = scale_ref[0].astype(jnp.float32) / DEN
 
-    def put(total):
+    def store(total):
         groups = out_ref.shape[1]
         split = total.reshape(CORES, -1, groups, rows, total.shape[-1])
         span = split.shape[1] * rows
@@ -60,14 +320,14 @@
 
         @pl.when(step == row)
         def _():
-            put(product + dot_rows(held[...], base_ref[0]))
+            store(product + dot_rows(held[...], base_ref[0]))
 
         @pl.when(step != row)
         def _():
-            put(product)
+            store(product)
 
     else:
-        put(product)
+        store(product)
 
 
 def partials(place, scale_num, mask, own, sib, delta, base, slab_own, groups, rows):
@@ -121,8 +381,7 @@
     @pl.when(step == pl.num_programs(0) - 1)
     def _():
         slab_own = out_ref.shape[1]
-        gate, up = total[:, :slab_own], total[:, slab_own:]
-        value = gate / (1 + jnp.exp(-gate)) * up
+        value = silu_times(total[:, :slab_own], total[:, slab_own:])
         split = value.reshape(CORES, -1, rows, slab_own)
         pieces = [split[core, x] for x in range(split.shape[1]) for core in range(CORES)]
         out_ref[...] = jnp.concatenate(pieces, axis=0).astype(out_ref.dtype)
@@ -145,8 +404,7 @@
     )(parts)
 
 
-def solution(mesh):
-    ckpts, groups = mesh.shape["ckpt"], mesh.shape["tensor"]
+def local_any(delta, drop_mask, scale_num, base, tokens, *, ckpts, groups):
     owners = ckpts // CORES
     both = ("ckpt", "tensor")
     same_core = [
@@ -154,34 +412,36 @@
         for core in range(CORES)
     ]
     swap = [(i, i ^ 1) for i in range(ckpts)]
-
-    def local(delta, drop_mask, scale_num, base, tokens):
-        rows, width = tokens.shape
-        width //= groups
-        slab_own = base.shape[1]
-        me = lax.axis_index("ckpt")
-        row, core = me // CORES, me % CORES
-
-        cut = tokens.reshape(rows, groups, width).transpose(1, 0, 2)
-        send = jnp.broadcast_to(cut[None], (owners, groups, rows, width)).reshape(-1, rows, width)
-        own = lax.all_to_all(send, both, 0, 0, axis_index_groups=same_core, tiled=True)
-        own = own.reshape(owners * groups * rows, width)
-        sib = lax.ppermute(own, "ckpt", swap)
-
-        place = jnp.stack([row, core, 1 - core]).astype(jnp.int32)
-        theirs = partials(
-            place, scale_num, drop_mask[0], own, sib, delta[0], None, slab_own, groups, rows
-        )
-        arrived = lax.ppermute(theirs, "ckpt", swap)
-        place = jnp.stack([row, core, core]).astype(jnp.int32)
-        ours = partials(
-            place, scale_num, drop_mask[0], own, sib, delta[0], base, slab_own, groups, rows
-        )
-        chip = (ours + arrived.astype(jnp.float32)).astype(jnp.bfloat16)
-        chip = chip.reshape(owners * groups, -1, 2 * slab_own)
-        parts = lax.all_to_all(chip, both, 0, 0, axis_index_groups=same_core, tiled=True)
-        return finish(parts, rows)
-
+    rows, width = tokens.shape
+    width //= groups
+    slab_own = base.shape[1]
+    me = lax.axis_index("ckpt")
+    row, core = me // CORES, me % CORES
+
+    cut = tokens.reshape(rows, groups, width).transpose(1, 0, 2)
+    send = jnp.broadcast_to(cut[None], (owners, groups, rows, width)).reshape(-1, rows, width)
+    own = lax.all_to_all(send, both, 0, 0, axis_index_groups=same_core, tiled=True)
+    own = own.reshape(owners * groups * rows, width)
+    sib = lax.ppermute(own, "ckpt", swap)
+
+    common = (own, sib, delta[0])
+    place = jnp.stack([row, core, 1 - core]).astype(jnp.int32)
+    theirs = partials(place, scale_num, drop_mask[0], *common, None, slab_own, groups, rows)
+    arrived = lax.ppermute(theirs, "ckpt", swap)
+    place = jnp.stack([row, core, core]).astype(jnp.int32)
+    ours = partials(place, scale_num, drop_mask[0], *common, base, slab_own, groups, rows)
+    chip = (ours + arrived.astype(jnp.float32)).astype(jnp.bfloat16)
+    chip = chip.reshape(owners * groups, -1, 2 * slab_own)
+    parts = lax.all_to_all(chip, both, 0, 0, axis_index_groups=same_core, tiled=True)
+    return finish(parts, rows)
+
+
+def solution(mesh):
+    ckpts, groups = mesh.shape["ckpt"], mesh.shape["tensor"]
+    if ckpts == 2 * CORES:
+        local = functools.partial(local_pair, groups=groups)
+    else:
+        local = functools.partial(local_any, ckpts=ckpts, groups=groups)
     in_specs = (
         P("ckpt", None, None, "tensor"),
         P("ckpt", None, None, "tensor"),

time: 74.5 us -> 68.1 us (0.914)
  blocking collectives: 53.5 us -> 33.5 us
  Pallas kernels: 16.3 us -> 24.2 us
  starting transfers between devices: 0.2 us -> 4.73 us
  waiting for transfers between devices: 1.18 us -> 3.75 us
  local copies, waits for them, and re-layouts: 1.72 us -> 0.72 us
    all_to_all x2, blocking collectives: 53.5 us -> 33.5 us  [the longest x1 17.3 us: local_pair(): parts = lax.all_to_all(whole, 'tensor', 0, 0, tiled=True)]
    pallas_call x3 -> x7, Pallas kernels: 16.3 us -> 24.2 us  [the longest x3 22.7 us: call(): pl.pallas_call(kernel, out_shape=outs, in_specs=in_specs, out_specs=[VMEM...]
    ppermute x2 -> x8, starting transfers between devices: 0.2 us -> 4.73 us  [the longest x1 1.49 us: local_pair(): far_own = chip_swap(own)]
    ppermute x2 -> x8, waiting for transfers between devices: 1.18 us -> 3.75 us  [the longest x1 1.37 us: local_pair(): over_second = chip_swap(second)]
    broadcast_in_dim x1 -> x0, local copies, waits for them, and re-layouts: 0.99 us -> none  [local(): jnp.broadcast_to(cut[None], (owners, groups, rows, width))]
  transfers between devices with their start and end apart: 2 -> 8, of which waited for: 1 -> 4; matrix products, arithmetic and copies ran while one was open for 0% -> 0% of each run, Pallas kernels for 11% -> 34%
where the time goes in v2:
time: 68.1 us; the launch traced here: 67.7 us
  blocking collectives  33.5 us (49%)
  Pallas kernels  24.2 us (36%)
  starting transfers between devices  4.73 us (7%)
  waiting for transfers between devices  3.75 us (6%)
  local copies, waits for them, and re-layouts  0.72 us (1%)
  between operations  0.71 us (1%)
    pallas_call x3, Pallas kernels, call(): pl.pallas_call(kernel, out_shape=outs, in_specs=in_specs, out_specs=[VMEM...  22.7 us
    all_to_all x1, blocking collectives, local_pair(): parts = lax.all_to_all(whole, 'tensor', 0, 0, tiled=True)  17.3 us
    all_to_all x1, blocking collectives, local_pair(): lax.all_to_all(cut, 'tensor', 0, 0, tiled=True)  16.2 us
    ppermute x1, starting transfers between devices, local_pair(): far_own = chip_swap(own)  1.49 us
    ppermute x1, waiting for transfers between devices, local_pair(): over_second = chip_swap(second)  1.37 us
  transfers between devices with their start and end apart: 8, of which 4 were waited for; matrix products, arithmetic and copies ran while one was open for 0% of the time, Pallas kernels for 34%

profile of v2, /device:TPU:0, one launch (start us, length us, event | category | flops | bytes accessed | tf_op | source)
XLA Modules:
  0.0 67.7 jit_solution(10632748353307231110)
XLA Ops:
  0.0 16.2 %all_to_all.10 = bf16[8,8,2048]{2,1,0:T(8,128)(2,1)S(1)} all-to-all(bf16[8,8,2048]{2,1,0:T(8,128)(2,1)} %bitcast.19), channel_id=1, replica_groups=mesh['ckpt'=4,'tensor'=8] {'tensor'}, dimensions={0} | all-to-all | bytes 524288 | tf_op jit(solution)/shard_map/all_to_all | solution.py:195
  16.2 0.0 collective-permute-start
  16.2 1.5 %collective-permute-start.1 = (bf16[64,2048]{1,0:T(8,128)(2,1)S(1)}, bf16[64,2048]{1,0:T(8,128)(2,1)S(1)}, u32[]{:S(2)}, u32[]{:S(2)}) collective-permute-start(bf16[64,2048]{1,0:T(8,128)(2,1)S(1)} %bitcast.9), channel_id=1, source_target_pairs={{0,16},{8,24},{16,0},{24,8},{1,17},{9,25},{17,1},{25,9},{2,18},{10... | collective-permute-start | bytes 786440 | tf_op jit(solution)/shard_map/ppermute | solution.py:196
  18.3 0.1 pad_add_fusion.place
  18.4 0.0 collective-permute-done.sib
  18.4 0.0 copy-start
  18.4 0.7 %copy-done = s32[1,2,16,16]{3,2,1,0:T(8,128)S(1)} copy-done((s32[1,2,16,16]{3,2,1,0:T(8,128)S(1)}, s32[1,2,16,16]{3,2,1,0:T(8,128)}, u32[]{:S(2)}) %copy-start) | copy-done | bytes 2072
  19.1 8.9 %shard_map.55 = (bf16[8,2,8,1024]{3,2,1,0:T(8,128)(2,1)S(1)}, f32[8,2,8,1024]{3,2,1,0:T(8,128)S(1)}, bf16[4,512,2048]{2,1,0:T(8,128)(2,1)}) custom-call(s32[2]{0:T(128)S(1)} %pad_add_fusion.place, s32[1]{0:T(128)S(6)} %copy.6.scale_num, s32[2,16,16]{2,1,0:T(8,128)S(1)} %bitcast.13, bf16[64,2048]{1,0:T(8,128)(2,1)S(1)} %bitcast.10, ...), custom_call_target="tpu_custom_call" | custom-call | flops 134217728 | bytes 1048576 | tf_op jit(solution)/shard_map/pallas_call | solution.py:150
  28.0 0.3 collective-permute-start.2
  28.3 0.0 collective-permute-done.1.far_own
  28.3 0.3 collective-permute-start.3
  28.6 1.0 %collective-permute-done.2.arrived = bf16[8,2,8,1024]{3,2,1,0:T(8,128)(2,1)S(1)} collective-permute-done((bf16[8,2,8,1024]{3,2,1,0:T(8,128)(2,1)S(1)}, bf16[8,2,8,1024]{3,2,1,0:T(8,128)(2,1)S(1)}, u32[]{:S(2)}, u32[]{:S(2)}) %collective-permute-start.2) | collective-permute-done | bytes 262176 | tf_op jit(solution)/shard_map/ppermute | solution.py:220
  29.7 0.3 collective-permute-done.3.far_sib
  30.0 0.8 %collective-permute-start.4 = (bf16[8,2,8,1024]{3,2,1,0:T(8,128)(2,1)S(1)}, bf16[8,2,8,1024]{3,2,1,0:T(8,128)(2,1)S(1)}, u32[]{:S(2)}, u32[]{:S(2)}) collective-permute-start(bf16[8,2,8,1024]{3,2,1,0:T(8,128)(2,1)S(1)} %shard_map.56), channel_id=1, source_target_pairs={{0,16},{8,24},{16,0},{24,8},{1,17},{9,25},{17,1},{25,9},{2,18},{10... | collective-permute-start | bytes 786440 | tf_op jit(solution)/shard_map/ppermute | solution.py:232
  30.8 8.1 %shard_map.57 = (bf16[8,2,8,1024]{3,2,1,0:T(8,128)(2,1)S(1)}, f32[8,2,8,1024]{3,2,1,0:T(8,128)S(1)}, bf16[8,2,2,8,1024]{4,3,2,1,0:T(8,128)(2,1)S(1)}) custom-call(s32[2]{0:T(128)S(1)} %pad_add_fusion.place, s32[1]{0:T(128)S(6)} %copy.6.scale_num, s32[2,16,16]{2,1,0:T(8,128)S(1)} %bitcast.14, bf16[64,2048]{1,0:T(8,128)(2,1)S(1)} %bitcast.11, ...), custom_call_target="tpu_custom_call" | custom-call | flops 268435456 | bytes 1048576 | tf_op jit(solution)/shard_map/pallas_call | solution.py:150
  38.9 0.0 collective-permute-done.4.far
  38.9 0.1 collective-permute-start.5
  39.0 0.5 collective-permute-start.6
  39.5 1.0 %collective-permute-done.5.arrived = bf16[8,2,8,1024]{3,2,1,0:T(8,128)(2,1)S(1)} collective-permute-done((bf16[8,2,8,1024]{3,2,1,0:T(8,128)(2,1)S(1)}, bf16[8,2,8,1024]{3,2,1,0:T(8,128)(2,1)S(1)}, u32[]{:S(2)}, u32[]{:S(2)}) %collective-permute-start.5) | collective-permute-done | bytes 262176 | tf_op jit(solution)/shard_map/ppermute | solution.py:249
  40.5 1.3 %collective-permute-start.7 = (bf16[8,2,8,1024]{3,2,1,0:T(8,128)(2,1)S(1)}, bf16[8,2,8,1024]{3,2,1,0:T(8,128)(2,1)S(1)}, u32[]{:S(2)}, u32[]{:S(2)}) collective-permute-start(bf16[8,2,8,1024]{3,2,1,0:T(8,128)(2,1)S(1)} %shard_map.58), channel_id=1, source_target_pairs={{0,16},{8,24},{16,0},{24,8},{1,17},{9,25},{17,1},{25,9},{2,18},{10... | collective-permute-start | bytes 786440 | tf_op jit(solution)/shard_map/ppermute | solution.py:252
  41.8 5.7 %shard_map.59.ours = f32[8,2,2,8,1024]{4,3,2,1,0:T(8,128)S(1)} custom-call(s32[2]{0:T(128)S(1)} %pad_add_fusion.place, s32[1]{0:T(128)S(6)} %copy.6.scale_num, s32[2,16,16]{2,1,0:T(8,128)S(1)} %bitcast.15, bf16[64,2048]{1,0:T(8,128)(2,1)S(1)} %bitcast.12, bf16[64,2048]{1,0:T(8,128)(2,1)S(1)} %collective-permute-done.sib, ...), custom_call_target="tpu_custom_call" | custom-call | flops 268435456 | bytes 1048576 | tf_op jit(solution)/shard_map/pallas_call | solution.py:150
  47.6 1.4 %collective-permute-done.7.near = bf16[8,2,8,1024]{3,2,1,0:T(8,128)(2,1)S(1)} collective-permute-done((bf16[8,2,8,1024]{3,2,1,0:T(8,128)(2,1)S(1)}, bf16[8,2,8,1024]{3,2,1,0:T(8,128)(2,1)S(1)}, u32[]{:S(2)}, u32[]{:S(2)}) %collective-permute-start.7) | collective-permute-done | bytes 262176 | tf_op jit(solution)/shard_map/ppermute | solution.py:252
  49.0 0.0 collective-permute-done.6.arrived
  49.0 0.2 shard_map.60
  49.1 17.3 %all_to_all.11.parts = bf16[8,2,2,8,1024]{4,3,2,1,0:T(8,128)(2,1)S(1)} all-to-all(bf16[8,2,2,8,1024]{4,3,2,1,0:T(8,128)(2,1)S(1)} %shard_map.60), channel_id=1, replica_groups=mesh['ckpt'=4,'tensor'=8] {'tensor'}, dimensions={0} | all-to-all | bytes 1048576 | tf_op jit(solution)/shard_map/all_to_all | solution.py:271
  66.5 1.3 %shard_map.61 = bf16[32,512]{1,0:T(8,128)(2,1)} custom-call(s32[2]{0:T(128)S(1)} %pad_add_fusion.place, bf16[8,2,2,8,1024]{4,3,2,1,0:T(8,128)(2,1)S(1)} %all_to_all.11.parts), custom_call_target="tpu_custom_call" | custom-call | tf_op jit(solution)/shard_map/pallas_call | solution.py:272
  (2 shorter events, 0.1 us)
Async XLA Ops:
  16.2 2.2 %collective-permute-start = (bf16[64,2048]{1,0:T(8,128)(2,1)S(1)}, bf16[64,2048]{1,0:T(8,128)(2,1)S(1)}, u32[]{:S(2)}, u32[]{:S(2)}) collective-permute-start(bf16[64,2048]{1,0:T(8,128)(2,1)S(1)} %bitcast.8), channel_id=1, source_target_pairs={{0,8},{8,0},{16,24},{24,16},{1,9},{9,1},{17,25},{25,17},{2,10},{10... | collective-permute-start | bytes 786440 | tf_op jit(solution)/shard_map/ppermute | solution.py:197
  16.2 12.1 %collective-permute-start.1 = (bf16[64,2048]{1,0:T(8,128)(2,1)S(1)}, bf16[64,2048]{1,0:T(8,128)(2,1)S(1)}, u32[]{:S(2)}, u32[]{:S(2)}) collective-permute-start(bf16[64,2048]{1,0:T(8,128)(2,1)S(1)} %bitcast.9), channel_id=1, source_target_pairs={{0,16},{8,24},{16,0},{24,8},{1,17},{9,25},{17,1},{25,9},{2,18},{10... | collective-permute-start | bytes 786440 | tf_op jit(solution)/shard_map/ppermute | solution.py:196
  18.4 0.7 %copy-start = (s32[1,2,16,16]{3,2,1,0:T(8,128)S(1)}, s32[1,2,16,16]{3,2,1,0:T(8,128)}, u32[]{:S(2)}) copy-start(s32[1,2,16,16]{3,2,1,0:T(8,128)} %param.6) | copy-start | bytes 6148
  28.0 1.6 %collective-permute-start.2 = (bf16[8,2,8,1024]{3,2,1,0:T(8,128)(2,1)S(1)}, bf16[8,2,8,1024]{3,2,1,0:T(8,128)(2,1)S(1)}, u32[]{:S(2)}, u32[]{:S(2)}) collective-permute-start(bf16[8,2,8,1024]{3,2,1,0:T(8,128)(2,1)S(1)} %get-tuple-element.19), channel_id=1, source_target_pairs={{0,8},{8,0},{16,24},{24,16},{1,9},{9,1},{17,25},{25,17},{2,10},{10... | collective-permute-start | bytes 786440 | tf_op jit(solution)/shard_map/ppermute | solution.py:220
  28.3 1.7 %collective-permute-start.3 = (bf16[64,2048]{1,0:T(8,128)(2,1)S(1)}, bf16[64,2048]{1,0:T(8,128)(2,1)S(1)}, u32[]{:S(2)}, u32[]{:S(2)}) collective-permute-start(bf16[64,2048]{1,0:T(8,128)(2,1)S(1)} %collective-permute-done.1.far_own), channel_id=1, source_target_pairs={{0,8},{8,0},{16,24},{24,16},{1,9},{9,1},{17,25},{25,17},{2,10},{10... | collective-permute-start | bytes 786440 | tf_op jit(solution)/shard_map/ppermute | solution.py:222
  30.0 8.9 %collective-permute-start.4 = (bf16[8,2,8,1024]{3,2,1,0:T(8,128)(2,1)S(1)}, bf16[8,2,8,1024]{3,2,1,0:T(8,128)(2,1)S(1)}, u32[]{:S(2)}, u32[]{:S(2)}) collective-permute-start(bf16[8,2,8,1024]{3,2,1,0:T(8,128)(2,1)S(1)} %shard_map.56), channel_id=1, source_target_pairs={{0,16},{8,24},{16,0},{24,8},{1,17},{9,25},{17,1},{25,9},{2,18},{10... | collective-permute-start | bytes 786440 | tf_op jit(solution)/shard_map/ppermute | solution.py:232
  38.9 1.6 %collective-permute-start.5 = (bf16[8,2,8,1024]{3,2,1,0:T(8,128)(2,1)S(1)}, bf16[8,2,8,1024]{3,2,1,0:T(8,128)(2,1)S(1)}, u32[]{:S(2)}, u32[]{:S(2)}) collective-permute-start(bf16[8,2,8,1024]{3,2,1,0:T(8,128)(2,1)S(1)} %get-tuple-element.28), channel_id=1, source_target_pairs={{0,8},{8,0},{16,24},{24,16},{1,9},{9,1},{17,25},{25,17},{2,10},{10... | collective-permute-start | bytes 786440 | tf_op jit(solution)/shard_map/ppermute | solution.py:249
  39.0 10.0 %collective-permute-start.6 = (bf16[8,2,2,8,1024]{4,3,2,1,0:T(8,128)(2,1)S(1)}, bf16[8,2,2,8,1024]{4,3,2,1,0:T(8,128)(2,1)S(1)}, u32[]{:S(2)}, u32[]{:S(2)}) collective-permute-start(bf16[8,2,2,8,1024]{4,3,2,1,0:T(8,128)(2,1)S(1)} %get-tuple-element.30), channel_id=1, source_target_pairs={{0,8},{8,0},{16,24},{24,16},{1,9},{9,1},{17,25},{25,17},{2,10},{10... | collective-permute-start | bytes 1572872 | tf_op jit(solution)/shard_map/ppermute | solution.py:250
  40.5 8.4 %collective-permute-start.7 = (bf16[8,2,8,1024]{3,2,1,0:T(8,128)(2,1)S(1)}, bf16[8,2,8,1024]{3,2,1,0:T(8,128)(2,1)S(1)}, u32[]{:S(2)}, u32[]{:S(2)}) collective-permute-start(bf16[8,2,8,1024]{3,2,1,0:T(8,128)(2,1)S(1)} %shard_map.58), channel_id=1, source_target_pairs={{0,16},{8,24},{16,0},{24,8},{1,17},{9,25},{17,1},{25,9},{2,18},{10... | collective-permute-start | bytes 786440 | tf_op jit(solution)/shard_map/ppermute | solution.py:252

commit v3 on v2

--- a/solution.py
+++ b/solution.py
@@ -32,14 +32,17 @@
         held[i * span : (i + 1) * span] = piece[...]
 
 
-def drop_blocks(mask_ref, kept, part, m, first):
-    rows, width = kept.shape[1:]
+def kept_blocks(mask_ref, weights, m, owner):
+    rows, width = weights.shape
+    strips = []
     for i in range(rows // BLOCK):
+        strip = []
         for j in range(width // BLOCK):
-            here = (part, slice(i * BLOCK, (i + 1) * BLOCK), slice(j * BLOCK, (j + 1) * BLOCK))
-            piece = kept[here]
-            keep = mask_ref[m, first * (rows // BLOCK) + i, j] != 0
-            kept[here] = jnp.where(keep, piece, jnp.zeros_like(piece))
+            piece = weights[i * BLOCK : (i + 1) * BLOCK, j * BLOCK : (j + 1) * BLOCK]
+            keep = mask_ref[m, owner * (rows // BLOCK) + i, j] != 0
+            strip.append(jnp.where(keep, piece, jnp.zeros_like(piece)))
+        strips.append(jnp.concatenate(strip, axis=1))
+    return jnp.concatenate(strips, axis=0)
 
 
 def put(view, total, core):
@@ -83,7 +86,7 @@
 
 
 def early_kernel(
-    place, scale_num, mask_hbm, own, sib, delta, theirs, ours, kept, held, mask, sems, mask_sem
+    place, scale_num, mask_hbm, own, sib, delta, theirs, kept, held, mask, sems, mask_sem
 ):
     chip, core = place[0], place[1]
     chunks = sems.shape[1]
@@ -94,56 +97,60 @@
     gather_held(held, (own, sib))
     scale = scale_num[0].astype(jnp.float32) / DEN
     mask_copy.wait()
-    for part, (m, owner) in enumerate(owners):
+    for part, (m, owner) in enumerate(owners[:2]):
         wait_for(copies, part, chunks)
-        drop_blocks(mask, kept, part, m, owner)
-        total = scale * dot_rows(held[...], kept[part])
-        put(half_of(theirs if part < 2 else ours, m), total, core)
+        total = scale * dot_rows(held[...], kept_blocks(mask, kept.at[part], m, owner))
+        put(half_of(theirs, m), total, core)
+    for part in (2, 3):
+        wait_for(copies, part, chunks)
+
+
+def early_rest_kernel(place, scale_num, mask, own, sib, kept, ours, held):
+    chip, core = place[0], place[1]
+    gather_held(held, (own, sib))
+    scale = scale_num[0].astype(jnp.float32) / DEN
+    for part, (m, owner) in enumerate(owners_of(1 - chip, core)):
+        total = scale * dot_rows(held[...], kept_blocks(mask, kept.at[2 + part], m, owner))
+        put(half_of(ours, m), total, core)
 
 
 def later_kernel(
-    place, scale_num, mask_hbm, own, sib, far_own, far_sib, kept, delta, theirs, ours, theirs_home,
-    home, held, mask, sems, mask_sem,
+    place, scale_num, mask, own, sib, far_own, far_sib, kept, delta, theirs, ours, theirs_home,
+    home, held, sems,
 ):
     chip, core = place[0], place[1]
     chunks = sems.shape[1]
     half = held.shape[0] // 2
-    mask_copy = pltpu.make_async_copy(mask_hbm, mask, mask_sem)
-    mask_copy.start()
-    owners = owners_of(chip, 1 - core)
-    copies = fetch(delta, home, sems, owners, chunks)
+    home_owners = owners_of(chip, 1 - core)
+    copies = fetch(delta, home, sems, home_owners, chunks)
     gather_held(held, (own, sib, far_own, far_sib))
     scale = scale_num[0].astype(jnp.float32) / DEN
-    for part in range(4):
-        total = scale * dot_rows(held[half:], kept[part])
-        put(half_of(theirs if part < 2 else ours, part % 2), total, core)
-    mask_copy.wait()
+    owners = owners_of(1 - chip, 1 - core) + owners_of(1 - chip, core)
     for part, (m, owner) in enumerate(owners):
+        total = scale * dot_rows(held[half:], kept_blocks(mask, kept.at[part], m, owner))
+        put(half_of(theirs if part < 2 else ours, m), total, core)
+    for part, (m, owner) in enumerate(home_owners):
         wait_for(copies, part, chunks)
-        drop_blocks(mask, home, part, m, owner)
-        put(half_of(theirs_home, m), scale * dot_rows(held[...], home[part]), core)
+        total = scale * dot_rows(held[...], kept_blocks(mask, home.at[part], m, owner))
+        put(half_of(theirs_home, m), total, core)
 
 
 def home_kernel(
-    place, scale_num, mask_hbm, own, sib, far_own, far_sib, delta, base, ours,
-    kept, kept_base, held, mask, sems, base_sems, mask_sem,
+    place, scale_num, mask, own, sib, far_own, far_sib, delta, base, ours,
+    kept, kept_base, held, sems, base_sems,
 ):
     chip, core = place[0], place[1]
     chunks = sems.shape[1]
-    mask_copy = pltpu.make_async_copy(mask_hbm, mask, mask_sem)
-    mask_copy.start()
     owners = owners_of(chip, core)
     copies = fetch(delta, kept, sems, owners, chunks)
     base_copies = fetch(base, kept_base, base_sems, [(0, 0), (1, 0)], chunks)
     gather_held(held, (own, sib, far_own, far_sib))
     scale = scale_num[0].astype(jnp.float32) / DEN
-    mask_copy.wait()
     for part, (m, owner) in enumerate(owners):
         wait_for(copies, part, chunks)
-        drop_blocks(mask, kept, part, m, owner)
-        total = scale * dot_rows(held[...], kept[part])
+        total = scale * dot_rows(held[...], kept_blocks(mask, kept.at[part], m, owner))
         wait_for(base_copies, part, chunks)
-        put(half_of(ours, m), total + dot_rows(held[...], kept_base[m]), core)
+        put(half_of(ours, m), total + dot_rows(held[...], kept_base[part]), core)
 
 
 def call(kernel, outs, scratch, in_specs, operands, flops, traffic):
@@ -188,6 +195,7 @@
     me = lax.axis_index("ckpt")
     place = jnp.stack([me >> 1, me & 1]).astype(jnp.int32)
     mask, delta = drop_mask[0], delta[0]
+    mask_hbm = pltpu.with_memory_space_constraint(mask, pltpu.HBM)
     core_swap = functools.partial(lax.ppermute, axis_name="ckpt", perm=[(i, i ^ 1) for i in range(4)])
     chip_swap = functools.partial(lax.ppermute, axis_name="ckpt", perm=[(i, i ^ 2) for i in range(4)])
 
@@ -203,9 +211,9 @@
     four = (groups, 2, CORES, rows, 2 * slab_own)
     weights = (4, slab_own, width)
     size = 4 * slab_own * width
-    theirs, ours, kept = call(
+    theirs, kept = call(
         early_kernel,
-        [part(pair, bf16), part(pair, f32), part(weights, bf16)],
+        [part(pair, bf16), part(weights, bf16)],
         [
             pltpu.VMEM((half, width), bf16),
             pltpu.SMEM(mask.shape, mask.dtype),
@@ -213,12 +221,21 @@
             pltpu.SemaphoreType.DMA(()),
         ],
         [SMEM, SMEM, HBM, VMEM, VMEM, HBM],
-        (place, scale_num, mask, own, sib, delta),
-        2 * half * size,
+        (place, scale_num, mask_hbm, own, sib, delta),
+        half * size,
         2 * size,
     )
     near = core_swap(theirs)
-    far_own, theirs = lax.optimization_barrier((far_own, theirs))
+    (ours,) = call(
+        early_rest_kernel,
+        [part(pair, f32)],
+        [pltpu.VMEM((half, width), bf16)],
+        [SMEM, SMEM, SMEM, VMEM, VMEM, VMEM],
+        (place, scale_num, mask, own, sib, kept),
+        half * size,
+        size,
+    )
+    far_own, ours = lax.optimization_barrier((far_own, ours))
     far_sib = core_swap(far_own)
     simple = lambda kernel, shape, *xs: pl.pallas_call(
         kernel,
@@ -236,11 +253,9 @@
         [
             pltpu.VMEM((2, slab_own, width), bf16),
             pltpu.VMEM((2 * half, width), bf16),
-            pltpu.SMEM(mask.shape, mask.dtype),
             pltpu.SemaphoreType.DMA((2, chunks)),
-            pltpu.SemaphoreType.DMA(()),
         ],
-        [SMEM, SMEM, HBM, VMEM, VMEM, VMEM, VMEM, VMEM, HBM],
+        [SMEM, SMEM, SMEM, VMEM, VMEM, VMEM, VMEM, VMEM, HBM],
         (place, scale_num, mask, own, sib, far_own, far_sib, kept, delta),
         4 * half * size,
         2 * size,
@@ -257,12 +272,10 @@
             pltpu.VMEM((2, slab_own, width), bf16),
             pltpu.VMEM((2, slab_own, width), bf16),
             pltpu.VMEM((2 * half, width), bf16),
-            pltpu.SMEM(mask.shape, mask.dtype),
             pltpu.SemaphoreType.DMA((2, chunks)),
             pltpu.SemaphoreType.DMA((2, chunks)),
-            pltpu.SemaphoreType.DMA(()),
         ],
-        [SMEM, SMEM, HBM, VMEM, VMEM, VMEM, VMEM, HBM, HBM],
+        [SMEM, SMEM, SMEM, VMEM, VMEM, VMEM, VMEM, HBM, HBM],
         (place, scale_num, mask, own, sib, far_own, far_sib, delta, base),
         4 * half * size,
         2 * size,

time: 68.1 us -> 71.6 us (1.051)
  Pallas kernels: 24.2 us -> 28.6 us
    pallas_call x3 -> x4, Pallas kernels: 22.7 us -> 27.1 us  [call(): pl.pallas_call(kernel, out_shape=outs, in_specs=in_specs, out_specs=[VMEM...]
    ppermute x1, waiting for transfers between devices: 1.02 us -> 0.01 us  [local_pair(): near = core_swap(theirs)]
    ppermute x1, waiting for transfers between devices: 0.32 us -> 1.2 us  [local_pair(): far_sib = core_swap(far_own)]
  transfers between devices with their start and end apart: 8 -> 8, of which waited for: 4 -> 3; matrix products, arithmetic and copies ran while one was open for 0% -> 0% of each run, Pallas kernels for 34% -> 38%
where the time goes in v3:
time: 71.6 us; the launch traced here: 71.3 us
  blocking collectives  33.5 us (47%)
  Pallas kernels  28.6 us (40%)
  starting transfers between devices  4.81 us (7%)
  waiting for transfers between devices  3.54 us (5%)
  between operations  0.72 us (1%)
    pallas_call x4, Pallas kernels, call(): pl.pallas_call(kernel, out_shape=outs, in_specs=in_specs, out_specs=[VMEM...  27.1 us
    all_to_all x1, blocking collectives, local_pair(): parts = lax.all_to_all(whole, 'tensor', 0, 0, tiled=True)  17.3 us
    all_to_all x1, blocking collectives, local_pair(): lax.all_to_all(cut, 'tensor', 0, 0, tiled=True)  16.2 us
    ppermute x1, starting transfers between devices, local_pair(): far_own = chip_swap(own)  1.49 us
  transfers between devices with their start and end apart: 8, of which 3 were waited for; matrix products, arithmetic and copies ran while one was open for 0% of the time, Pallas kernels for 38%

profile of v3, /device:TPU:0, one launch (start us, length us, event | category | flops | bytes accessed | tf_op | source)
XLA Modules:
  0.0 71.3 jit_solution(538234821726188915)
XLA Ops:
  0.0 16.2 %all_to_all.10 = bf16[8,8,2048]{2,1,0:T(8,128)(2,1)S(1)} all-to-all(bf16[8,8,2048]{2,1,0:T(8,128)(2,1)} %bitcast.21), channel_id=1, replica_groups=mesh['ckpt'=4,'tensor'=8] {'tensor'}, dimensions={0} | all-to-all | bytes 524288 | tf_op jit(solution)/shard_map/all_to_all | solution.py:203
  16.2 0.0 collective-permute-start
  16.2 1.5 %collective-permute-start.1 = (bf16[64,2048]{1,0:T(8,128)(2,1)S(1)}, bf16[64,2048]{1,0:T(8,128)(2,1)S(1)}, u32[]{:S(2)}, u32[]{:S(2)}) collective-permute-start(bf16[64,2048]{1,0:T(8,128)(2,1)S(1)} %bitcast.9), channel_id=1, source_target_pairs={{0,16},{8,24},{16,0},{24,8},{1,17},{9,25},{17,1},{25,9},{2,18},{10... | collective-permute-start | bytes 786440 | tf_op jit(solution)/shard_map/ppermute | solution.py:204
  18.3 0.1 pad_add_fusion.place
  18.4 0.0 collective-permute-done.sib
  18.4 0.0 copy-start
  18.4 7.3 %shard_map.55 = (bf16[8,2,8,1024]{3,2,1,0:T(8,128)(2,1)S(1)}, bf16[4,512,2048]{2,1,0:T(8,128)(2,1)}) custom-call(s32[2]{0:T(128)S(1)} %pad_add_fusion.place, s32[1]{0:T(128)S(6)} %copy.6.scale_num, s32[2,16,16]{2,1,0:T(8,128)} %bitcast.14, bf16[64,2048]{1,0:T(8,128)(2,1)S(1)} %bitcast.10, bf16[64,2048]{1,0:T(8,128)(2,1)S(1)} %collective-permute-done.sib, ...), custom_call_target="tpu_custom_call" | custom-call | flops 67108864 | bytes 1048576 | tf_op jit(solution)/shard_map/pallas_call | solution.py:157
  25.7 0.3 collective-permute-start.2
  26.0 0.0 copy-done
  26.0 4.9 %shard_map.56.ours = f32[8,2,8,1024]{3,2,1,0:T(8,128)S(1)} custom-call(s32[2]{0:T(128)S(1)} %pad_add_fusion.place, s32[1]{0:T(128)S(6)} %copy.6.scale_num, s32[2,16,16]{2,1,0:T(8,128)S(1)} %bitcast.15, bf16[64,2048]{1,0:T(8,128)(2,1)S(1)} %bitcast.11, bf16[64,2048]{1,0:T(8,128)(2,1)S(1)} %collective-permute-done.sib, ...), custom_call_target="tpu_custom_call" | custom-call | flops 67108864 | bytes 524288 | tf_op jit(solution)/shard_map/pallas_call | solution.py:157
  30.9 0.0 collective-permute-done.1.far_own
  30.9 0.3 collective-permute-start.3
  31.3 0.0 collective-permute-done.2.arrived
  31.3 1.2 %collective-permute-done.3.far_sib = bf16[64,2048]{1,0:T(8,128)(2,1)S(1)} collective-permute-done((bf16[64,2048]{1,0:T(8,128)(2,1)S(1)}, bf16[64,2048]{1,0:T(8,128)(2,1)S(1)}, u32[]{:S(2)}, u32[]{:S(2)}) %collective-permute-start.3) | collective-permute-done | bytes 262176 | tf_op jit(solution)/shard_map/ppermute | solution.py:239
  32.5 0.7 %collective-permute-start.4 = (bf16[8,2,8,1024]{3,2,1,0:T(8,128)(2,1)S(1)}, bf16[8,2,8,1024]{3,2,1,0:T(8,128)(2,1)S(1)}, u32[]{:S(2)}, u32[]{:S(2)}) collective-permute-start(bf16[8,2,8,1024]{3,2,1,0:T(8,128)(2,1)S(1)} %shard_map.57), channel_id=1, source_target_pairs={{0,16},{8,24},{16,0},{24,8},{1,17},{9,25},{17,1},{25,9},{2,18},{10... | collective-permute-start | bytes 786440 | tf_op jit(solution)/shard_map/ppermute | solution.py:249
  33.2 9.2 %shard_map.58 = (bf16[8,2,8,1024]{3,2,1,0:T(8,128)(2,1)S(1)}, f32[8,2,8,1024]{3,2,1,0:T(8,128)S(1)}, bf16[8,2,2,8,1024]{4,3,2,1,0:T(8,128)(2,1)S(1)}) custom-call(s32[2]{0:T(128)S(1)} %pad_add_fusion.place, s32[1]{0:T(128)S(6)} %copy.6.scale_num, s32[2,16,16]{2,1,0:T(8,128)S(1)} %bitcast.16, bf16[64,2048]{1,0:T(8,128)(2,1)S(1)} %bitcast.12, ...), custom_call_target="tpu_custom_call" | custom-call | flops 268435456 | bytes 1048576 | tf_op jit(solution)/shard_map/pallas_call | solution.py:157
  42.4 0.0 collective-permute-done.4.far
  42.4 0.1 collective-permute-start.5
  42.6 0.4 collective-permute-start.6
  43.0 1.0 %collective-permute-done.5.arrived = bf16[8,2,8,1024]{3,2,1,0:T(8,128)(2,1)S(1)} collective-permute-done((bf16[8,2,8,1024]{3,2,1,0:T(8,128)(2,1)S(1)}, bf16[8,2,8,1024]{3,2,1,0:T(8,128)(2,1)S(1)}, u32[]{:S(2)}, u32[]{:S(2)}) %collective-permute-start.5) | collective-permute-done | bytes 262176 | tf_op jit(solution)/shard_map/ppermute | solution.py:264
  44.1 1.4 %collective-permute-start.7 = (bf16[8,2,8,1024]{3,2,1,0:T(8,128)(2,1)S(1)}, bf16[8,2,8,1024]{3,2,1,0:T(8,128)(2,1)S(1)}, u32[]{:S(2)}, u32[]{:S(2)}) collective-permute-start(bf16[8,2,8,1024]{3,2,1,0:T(8,128)(2,1)S(1)} %shard_map.59), channel_id=1, source_target_pairs={{0,16},{8,24},{16,0},{24,8},{1,17},{9,25},{17,1},{25,9},{2,18},{10... | collective-permute-start | bytes 786440 | tf_op jit(solution)/shard_map/ppermute | solution.py:267
  45.5 5.7 %shard_map.60.ours = f32[8,2,2,8,1024]{4,3,2,1,0:T(8,128)S(1)} custom-call(s32[2]{0:T(128)S(1)} %pad_add_fusion.place, s32[1]{0:T(128)S(6)} %copy.6.scale_num, s32[2,16,16]{2,1,0:T(8,128)S(1)} %bitcast.17, bf16[64,2048]{1,0:T(8,128)(2,1)S(1)} %bitcast.13, bf16[64,2048]{1,0:T(8,128)(2,1)S(1)} %collective-permute-done.sib, ...), custom_call_target="tpu_custom_call" | custom-call | flops 268435456 | bytes 1048576 | tf_op jit(solution)/shard_map/pallas_call | solution.py:157
  51.2 1.3 %collective-permute-done.7.near = bf16[8,2,8,1024]{3,2,1,0:T(8,128)(2,1)S(1)} collective-permute-done((bf16[8,2,8,1024]{3,2,1,0:T(8,128)(2,1)S(1)}, bf16[8,2,8,1024]{3,2,1,0:T(8,128)(2,1)S(1)}, u32[]{:S(2)}, u32[]{:S(2)}) %collective-permute-start.7) | collective-permute-done | bytes 262176 | tf_op jit(solution)/shard_map/ppermute | solution.py:267
  52.5 0.0 collective-permute-done.6.arrived
  52.5 0.2 shard_map.61
  52.7 17.3 %all_to_all.11.parts = bf16[8,2,2,8,1024]{4,3,2,1,0:T(8,128)(2,1)S(1)} all-to-all(bf16[8,2,2,8,1024]{4,3,2,1,0:T(8,128)(2,1)S(1)} %shard_map.61), channel_id=1, replica_groups=mesh['ckpt'=4,'tensor'=8] {'tensor'}, dimensions={0} | all-to-all | bytes 1048576 | tf_op jit(solution)/shard_map/all_to_all | solution.py:284
  70.0 1.3 %shard_map.62 = bf16[32,512]{1,0:T(8,128)(2,1)} custom-call(s32[2]{0:T(128)S(1)} %pad_add_fusion.place, bf16[8,2,2,8,1024]{4,3,2,1,0:T(8,128)(2,1)S(1)} %all_to_all.11.parts), custom_call_target="tpu_custom_call" | custom-call | tf_op jit(solution)/shard_map/pallas_call | solution.py:285
  (2 shorter events, 0.1 us)
Async XLA Ops:
  16.2 2.2 %collective-permute-start = (bf16[64,2048]{1,0:T(8,128)(2,1)S(1)}, bf16[64,2048]{1,0:T(8,128)(2,1)S(1)}, u32[]{:S(2)}, u32[]{:S(2)}) collective-permute-start(bf16[64,2048]{1,0:T(8,128)(2,1)S(1)} %bitcast.8), channel_id=1, source_target_pairs={{0,8},{8,0},{16,24},{24,16},{1,9},{9,1},{17,25},{25,17},{2,10},{10... | collective-permute-start | bytes 786440 | tf_op jit(solution)/shard_map/ppermute | solution.py:205
  16.2 14.7 %collective-permute-start.1 = (bf16[64,2048]{1,0:T(8,128)(2,1)S(1)}, bf16[64,2048]{1,0:T(8,128)(2,1)S(1)}, u32[]{:S(2)}, u32[]{:S(2)}) collective-permute-start(bf16[64,2048]{1,0:T(8,128)(2,1)S(1)} %bitcast.9), channel_id=1, source_target_pairs={{0,16},{8,24},{16,0},{24,8},{1,17},{9,25},{17,1},{25,9},{2,18},{10... | collective-permute-start | bytes 786440 | tf_op jit(solution)/shard_map/ppermute | solution.py:204
  18.4 7.6 %copy-start = (s32[1,2,16,16]{3,2,1,0:T(8,128)S(1)}, s32[1,2,16,16]{3,2,1,0:T(8,128)}, u32[]{:S(2)}) copy-start(s32[1,2,16,16]{3,2,1,0:T(8,128)} %param.6) | copy-start | bytes 6148
  25.7 5.6 %collective-permute-start.2 = (bf16[8,2,8,1024]{3,2,1,0:T(8,128)(2,1)S(1)}, bf16[8,2,8,1024]{3,2,1,0:T(8,128)(2,1)S(1)}, u32[]{:S(2)}, u32[]{:S(2)}) collective-permute-start(bf16[8,2,8,1024]{3,2,1,0:T(8,128)(2,1)S(1)} %get-tuple-element.22), channel_id=1, source_target_pairs={{0,8},{8,0},{16,24},{24,16},{1,9},{9,1},{17,25},{25,17},{2,10},{10... | collective-permute-start | bytes 786440 | tf_op jit(solution)/shard_map/ppermute | solution.py:228
  30.9 1.6 %collective-permute-start.3 = (bf16[64,2048]{1,0:T(8,128)(2,1)S(1)}, bf16[64,2048]{1,0:T(8,128)(2,1)S(1)}, u32[]{:S(2)}, u32[]{:S(2)}) collective-permute-start(bf16[64,2048]{1,0:T(8,128)(2,1)S(1)} %collective-permute-done.1.far_own), channel_id=1, source_target_pairs={{0,8},{8,0},{16,24},{24,16},{1,9},{9,1},{17,25},{25,17},{2,10},{10... | collective-permute-start | bytes 786440 | tf_op jit(solution)/shard_map/ppermute | solution.py:239
  32.5 9.9 %collective-permute-start.4 = (bf16[8,2,8,1024]{3,2,1,0:T(8,128)(2,1)S(1)}, bf16[8,2,8,1024]{3,2,1,0:T(8,128)(2,1)S(1)}, u32[]{:S(2)}, u32[]{:S(2)}) collective-permute-start(bf16[8,2,8,1024]{3,2,1,0:T(8,128)(2,1)S(1)} %shard_map.57), channel_id=1, source_target_pairs={{0,16},{8,24},{16,0},{24,8},{1,17},{9,25},{17,1},{25,9},{2,18},{10... | collective-permute-start | bytes 786440 | tf_op jit(solution)/shard_map/ppermute | solution.py:249
  42.4 1.6 %collective-permute-start.5 = (bf16[8,2,8,1024]{3,2,1,0:T(8,128)(2,1)S(1)}, bf16[8,2,8,1024]{3,2,1,0:T(8,128)(2,1)S(1)}, u32[]{:S(2)}, u32[]{:S(2)}) collective-permute-start(bf16[8,2,8,1024]{3,2,1,0:T(8,128)(2,1)S(1)} %get-tuple-element.28), channel_id=1, source_target_pairs={{0,8},{8,0},{16,24},{24,16},{1,9},{9,1},{17,25},{25,17},{2,10},{10... | collective-permute-start | bytes 786440 | tf_op jit(solution)/shard_map/ppermute | solution.py:264
  42.6 9.9 %collective-permute-start.6 = (bf16[8,2,2,8,1024]{4,3,2,1,0:T(8,128)(2,1)S(1)}, bf16[8,2,2,8,1024]{4,3,2,1,0:T(8,128)(2,1)S(1)}, u32[]{:S(2)}, u32[]{:S(2)}) collective-permute-start(bf16[8,2,2,8,1024]{4,3,2,1,0:T(8,128)(2,1)S(1)} %get-tuple-element.30), channel_id=1, source_target_pairs={{0,8},{8,0},{16,24},{24,16},{1,9},{9,1},{17,25},{25,17},{2,10},{10... | collective-permute-start | bytes 1572872 | tf_op jit(solution)/shard_map/ppermute | solution.py:265
  44.1 8.4 %collective-permute-start.7 = (bf16[8,2,8,1024]{3,2,1,0:T(8,128)(2,1)S(1)}, bf16[8,2,8,1024]{3,2,1,0:T(8,128)(2,1)S(1)}, u32[]{:S(2)}, u32[]{:S(2)}) collective-permute-start(bf16[8,2,8,1024]{3,2,1,0:T(8,128)(2,1)S(1)} %shard_map.59), channel_id=1, source_target_pairs={{0,16},{8,24},{16,0},{24,8},{1,17},{9,25},{17,1},{25,9},{2,18},{10... | collective-permute-start | bytes 786440 | tf_op jit(solution)/shard_map/ppermute | solution.py:267

commit v4 on v3

--- a/solution.py
+++ b/solution.py
@@ -32,17 +32,28 @@
         held[i * span : (i + 1) * span] = piece[...]
 
 
-def kept_blocks(mask_ref, weights, m, owner):
-    rows, width = weights.shape
-    strips = []
-    for i in range(rows // BLOCK):
-        strip = []
-        for j in range(width // BLOCK):
-            piece = weights[i * BLOCK : (i + 1) * BLOCK, j * BLOCK : (j + 1) * BLOCK]
-            keep = mask_ref[m, owner * (rows // BLOCK) + i, j] != 0
-            strip.append(jnp.where(keep, piece, jnp.zeros_like(piece)))
-        strips.append(jnp.concatenate(strip, axis=1))
-    return jnp.concatenate(strips, axis=0)
+def expand(mask, scale, factors):
+    blocks, width = mask.shape[-1], factors.shape[1]
+    column = lax.broadcasted_iota(jnp.int32, (blocks, width), 1) // BLOCK
+    row = lax.broadcasted_iota(jnp.int32, (blocks, width), 0)
+    spread = jnp.where(column == row, 1.0, 0.0).astype(jnp.float32)
+    kept = jnp.where(mask.reshape(-1, blocks) != 0, scale, 0.0).astype(jnp.float32)
+    factors[...] = jnp.dot(kept, spread, preferred_element_type=jnp.float32)
+
+
+def terms(factors, weights, m, owner):
+    strips = weights.shape[0] // BLOCK
+    first = m * (factors.shape[0] // 2) + owner * strips
+    scaled = []
+    for i in range(strips):
+        factor = factors[pl.ds(first + i, 1), :].astype(weights.dtype)
+        scaled.append(weights[i * BLOCK : (i + 1) * BLOCK] * factor)
+    return jnp.concatenate(scaled, axis=0)
+
+
+def chip_and_core():
+    me = lax.axis_index("ckpt")
+    return me >> 1, me & 1
 
 
 def put(view, total, core):
@@ -86,69 +97,64 @@
 
 
 def early_kernel(
-    place, scale_num, mask_hbm, own, sib, delta, theirs, kept, held, mask, sems, mask_sem
+    scale_num, mask_hbm, own, sib, delta, theirs, kept, factors, held, mask, sems, mask_sem
 ):
-    chip, core = place[0], place[1]
+    chip, core = chip_and_core()
     chunks = sems.shape[1]
     mask_copy = pltpu.make_async_copy(mask_hbm, mask, mask_sem)
     mask_copy.start()
     owners = owners_of(1 - chip, 1 - core) + owners_of(1 - chip, core)
     copies = fetch(delta, kept, sems, owners, chunks)
     gather_held(held, (own, sib))
-    scale = scale_num[0].astype(jnp.float32) / DEN
     mask_copy.wait()
+    expand(mask[...], scale_num[0].astype(jnp.float32) / DEN, factors)
     for part, (m, owner) in enumerate(owners[:2]):
         wait_for(copies, part, chunks)
-        total = scale * dot_rows(held[...], kept_blocks(mask, kept.at[part], m, owner))
+        total = dot_rows(held[...], terms(factors, kept.at[part], m, owner))
         put(half_of(theirs, m), total, core)
     for part in (2, 3):
         wait_for(copies, part, chunks)
 
 
-def early_rest_kernel(place, scale_num, mask, own, sib, kept, ours, held):
-    chip, core = place[0], place[1]
+def early_rest_kernel(factors, own, sib, kept, ours, held):
+    chip, core = chip_and_core()
     gather_held(held, (own, sib))
-    scale = scale_num[0].astype(jnp.float32) / DEN
     for part, (m, owner) in enumerate(owners_of(1 - chip, core)):
-        total = scale * dot_rows(held[...], kept_blocks(mask, kept.at[2 + part], m, owner))
+        total = dot_rows(held[...], terms(factors, kept.at[2 + part], m, owner))
         put(half_of(ours, m), total, core)
 
 
 def later_kernel(
-    place, scale_num, mask, own, sib, far_own, far_sib, kept, delta, theirs, ours, theirs_home,
-    home, held, sems,
+    factors, own, sib, far_own, far_sib, kept, delta, theirs, ours, theirs_home, home, held, sems
 ):
-    chip, core = place[0], place[1]
+    chip, core = chip_and_core()
     chunks = sems.shape[1]
     half = held.shape[0] // 2
     home_owners = owners_of(chip, 1 - core)
     copies = fetch(delta, home, sems, home_owners, chunks)
     gather_held(held, (own, sib, far_own, far_sib))
-    scale = scale_num[0].astype(jnp.float32) / DEN
     owners = owners_of(1 - chip, 1 - core) + owners_of(1 - chip, core)
     for part, (m, owner) in enumerate(owners):
-        total = scale * dot_rows(held[half:], kept_blocks(mask, kept.at[part], m, owner))
+        total = dot_rows(held[half:], terms(factors, kept.at[part], m, owner))
         put(half_of(theirs if part < 2 else ours, m), total, core)
     for part, (m, owner) in enumerate(home_owners):
         wait_for(copies, part, chunks)
-        total = scale * dot_rows(held[...], kept_blocks(mask, home.at[part], m, owner))
+        total = dot_rows(held[...], terms(factors, home.at[part], m, owner))
         put(half_of(theirs_home, m), total, core)
 
 
 def home_kernel(
-    place, scale_num, mask, own, sib, far_own, far_sib, delta, base, ours,
-    kept, kept_base, held, sems, base_sems,
+    factors, own, sib, far_own, far_sib, delta, base, ours, kept, kept_base, held, sems, base_sems
 ):
-    chip, core = place[0], place[1]
+    chip, core = chip_and_core()
     chunks = sems.shape[1]
     owners = owners_of(chip, core)
     copies = fetch(delta, kept, sems, owners, chunks)
     base_copies = fetch(base, kept_base, base_sems, [(0, 0), (1, 0)], chunks)
     gather_held(held, (own, sib, far_own, far_sib))
-    scale = scale_num[0].astype(jnp.float32) / DEN
     for part, (m, owner) in enumerate(owners):
         wait_for(copies, part, chunks)
-        total = scale * dot_rows(held[...], kept_blocks(mask, kept.at[part], m, owner))
+        total = dot_rows(held[...], terms(factors, kept.at[part], m, owner))
         wait_for(base_copies, part, chunks)
         put(half_of(ours, m), total + dot_rows(held[...], kept_base[part]), core)
 
@@ -175,8 +181,8 @@
         out[:, x] = total.astype(out.dtype)
 
 
-def last_kernel(place, parts, out, total):
-    chip, core = place[0], place[1]
+def last_kernel(parts, out, total):
+    chip, _ = chip_and_core()
     rows = parts.shape[-2]
     slab_own = out.shape[1]
     for x in range(2):
@@ -192,10 +198,7 @@
     rows, width = tokens.shape[0], tokens.shape[1] // groups
     slab_own = base.shape[1]
     f32, bf16 = jnp.float32, jnp.bfloat16
-    me = lax.axis_index("ckpt")
-    place = jnp.stack([me >> 1, me & 1]).astype(jnp.int32)
     mask, delta = drop_mask[0], delta[0]
-    mask_hbm = pltpu.with_memory_space_constraint(mask, pltpu.HBM)
     core_swap = functools.partial(lax.ppermute, axis_name="ckpt", perm=[(i, i ^ 1) for i in range(4)])
     chip_swap = functools.partial(lax.ppermute, axis_name="ckpt", perm=[(i, i ^ 2) for i in range(4)])
 
@@ -211,17 +214,17 @@
     four = (groups, 2, CORES, rows, 2 * slab_own)
     weights = (4, slab_own, width)
     size = 4 * slab_own * width
-    theirs, kept = call(
+    theirs, kept, factors = call(
         early_kernel,
-        [part(pair, bf16), part(weights, bf16)],
+        [part(pair, bf16), part(weights, bf16), part((mask.shape[0] * mask.shape[1], width), f32)],
         [
             pltpu.VMEM((half, width), bf16),
-            pltpu.SMEM(mask.shape, mask.dtype),
+            pltpu.VMEM(mask.shape, mask.dtype),
             pltpu.SemaphoreType.DMA((4, chunks)),
             pltpu.SemaphoreType.DMA(()),
         ],
-        [SMEM, SMEM, HBM, VMEM, VMEM, HBM],
-        (place, scale_num, mask_hbm, own, sib, delta),
+        [SMEM, HBM, VMEM, VMEM, HBM],
+        (scale_num, pltpu.with_memory_space_constraint(mask, pltpu.HBM), own, sib, delta),
         half * size,
         2 * size,
     )
@@ -230,8 +233,8 @@
         early_rest_kernel,
         [part(pair, f32)],
         [pltpu.VMEM((half, width), bf16)],
-        [SMEM, SMEM, SMEM, VMEM, VMEM, VMEM],
-        (place, scale_num, mask, own, sib, kept),
+        [VMEM] * 4,
+        (factors, own, sib, kept),
         half * size,
         size,
     )
@@ -255,8 +258,8 @@
             pltpu.VMEM((2 * half, width), bf16),
             pltpu.SemaphoreType.DMA((2, chunks)),
         ],
-        [SMEM, SMEM, SMEM, VMEM, VMEM, VMEM, VMEM, VMEM, HBM],
-        (place, scale_num, mask, own, sib, far_own, far_sib, kept, delta),
+        [VMEM] * 6 + [HBM],
+        (factors, own, sib, far_own, far_sib, kept, delta),
         4 * half * size,
         2 * size,
     )
@@ -275,8 +278,8 @@
             pltpu.SemaphoreType.DMA((2, chunks)),
             pltpu.SemaphoreType.DMA((2, chunks)),
         ],
-        [SMEM, SMEM, SMEM, VMEM, VMEM, VMEM, VMEM, HBM, HBM],
-        (place, scale_num, mask, own, sib, far_own, far_sib, delta, base),
+        [VMEM] * 5 + [HBM, HBM],
+        (factors, own, sib, far_own, far_sib, delta, base),
         4 * half * size,
         2 * size,
     )
@@ -285,11 +288,11 @@
     return pl.pallas_call(
         last_kernel,
         out_shape=part((2 * CORES * rows, slab_own), bf16),
-        in_specs=[SMEM, VMEM],
+        in_specs=[VMEM],
         out_specs=VMEM,
         scratch_shapes=[pltpu.VMEM((2 * CORES * rows, slab_own), f32)],
         compiler_params=pltpu.CompilerParams(vmem_limit_bytes=16 * MIB),
-    )(place, parts)
+    )(parts)
 
 
 def masked_rows(mask_ref, delta_ref, kept, m, row_block):

time: 71.6 us -> 71.5 us (level)
  no operation moved by 1% of the time
where the time goes in v4:
time: 71.5 us; the launch traced here: 71.2 us
  blocking collectives  33.5 us (47%)
  Pallas kernels  28 us (39%)
  starting transfers between devices  4.8 us (7%)
  waiting for transfers between devices  4.17 us (6%)
  between operations  0.73 us (1%)
    pallas_call x4, Pallas kernels, call(): pl.pallas_call(kernel, out_shape=outs, in_specs=in_specs, out_specs=[VMEM...  27 us
    all_to_all x1, blocking collectives, local_pair(): parts = lax.all_to_all(whole, 'tensor', 0, 0, tiled=True)  17.3 us
    all_to_all x1, blocking collectives, local_pair(): lax.all_to_all(cut, 'tensor', 0, 0, tiled=True)  16.2 us
    ppermute x1, waiting for transfers between devices, local_pair(): over_second = chip_swap(second)  1.93 us
    ppermute x1, starting transfers between devices, local_pair(): far_own = chip_swap(own)  1.49 us
  transfers between devices with their start and end apart: 8, of which 3 were waited for; matrix products, arithmetic and copies ran while one was open for 0% of the time, Pallas kernels for 38%

profile of v4, /device:TPU:0, one launch (start us, length us, event | category | flops | bytes accessed | tf_op | source)
XLA Modules:
  0.0 71.2 jit_solution(17751424296094751037)
XLA Ops:
  0.0 16.2 %all_to_all.10 = bf16[8,8,2048]{2,1,0:T(8,128)(2,1)S(1)} all-to-all(bf16[8,8,2048]{2,1,0:T(8,128)(2,1)} %bitcast.15), channel_id=1, replica_groups=mesh['ckpt'=4,'tensor'=8] {'tensor'}, dimensions={0} | all-to-all | bytes 524288 | tf_op jit(solution)/shard_map/all_to_all | solution.py:206
  16.2 0.0 collective-permute-start
  16.2 1.5 %collective-permute-start.1 = (bf16[64,2048]{1,0:T(8,128)(2,1)S(1)}, bf16[64,2048]{1,0:T(8,128)(2,1)S(1)}, u32[]{:S(2)}, u32[]{:S(2)}) collective-permute-start(bf16[64,2048]{1,0:T(8,128)(2,1)S(1)} %bitcast.7), channel_id=1, source_target_pairs={{0,16},{8,24},{16,0},{24,8},{1,17},{9,25},{17,1},{25,9},{2,18},{10... | collective-permute-start | bytes 786440 | tf_op jit(solution)/shard_map/ppermute | solution.py:207
  18.3 0.0 collective-permute-done.sib
  18.4 8.1 %shard_map.55 = (bf16[8,2,8,1024]{3,2,1,0:T(8,128)(2,1)S(1)}, bf16[4,512,2048]{2,1,0:T(8,128)(2,1)}, f32[32,2048]{1,0:T(8,128)S(1)}) custom-call(s32[1]{0:T(128)S(6)} %copy.6.scale_num, s32[2,16,16]{2,1,0:T(8,128)} %bitcast.16, bf16[64,2048]{1,0:T(8,128)(2,1)S(1)} %bitcast.8, bf16[64,2048]{1,0:T(8,128)(2,1)S(1)} %collective-permute-done.sib, ...), custom_call_target="tpu_custom_call" | custom-call | flops 67108864 | bytes 1048576 | tf_op jit(solution)/shard_map/pallas_call | solution.py:163
  26.4 0.3 collective-permute-start.2
  26.7 4.9 %shard_map.56.ours = f32[8,2,8,1024]{3,2,1,0:T(8,128)S(1)} custom-call(f32[32,2048]{1,0:T(8,128)S(1)} %get-tuple-element.20.factors, bf16[64,2048]{1,0:T(8,128)(2,1)S(1)} %bitcast.9, bf16[64,2048]{1,0:T(8,128)(2,1)S(1)} %collective-permute-done.sib, bf16[4,512,2048]{2,1,0:T(8,128)(2,1)} %get-tuple-element.21.kept), custom_call_target="tpu_custom_call" | custom-call | flops 67108864 | bytes 524288 | tf_op jit(solution)/shard_map/pallas_call | solution.py:163
  31.6 0.0 collective-permute-done.1.far_own
  31.6 0.3 collective-permute-start.3
  32.0 0.0 collective-permute-done.2.arrived
  32.0 1.2 %collective-permute-done.3.far_sib = bf16[64,2048]{1,0:T(8,128)(2,1)S(1)} collective-permute-done((bf16[64,2048]{1,0:T(8,128)(2,1)S(1)}, bf16[64,2048]{1,0:T(8,128)(2,1)S(1)}, u32[]{:S(2)}, u32[]{:S(2)}) %collective-permute-start.3) | collective-permute-done | bytes 262176 | tf_op jit(solution)/shard_map/ppermute | solution.py:242
  33.2 0.8 %collective-permute-start.4 = (bf16[8,2,8,1024]{3,2,1,0:T(8,128)(2,1)S(1)}, bf16[8,2,8,1024]{3,2,1,0:T(8,128)(2,1)S(1)}, u32[]{:S(2)}, u32[]{:S(2)}) collective-permute-start(bf16[8,2,8,1024]{3,2,1,0:T(8,128)(2,1)S(1)} %shard_map.57), channel_id=1, source_target_pairs={{0,16},{8,24},{16,0},{24,8},{1,17},{9,25},{17,1},{25,9},{2,18},{10... | collective-permute-start | bytes 786440 | tf_op jit(solution)/shard_map/ppermute | solution.py:252
  34.0 8.9 %shard_map.58 = (bf16[8,2,8,1024]{3,2,1,0:T(8,128)(2,1)S(1)}, f32[8,2,8,1024]{3,2,1,0:T(8,128)S(1)}, bf16[8,2,2,8,1024]{4,3,2,1,0:T(8,128)(2,1)S(1)}) custom-call(f32[32,2048]{1,0:T(8,128)S(1)} %get-tuple-element.20.factors, bf16[64,2048]{1,0:T(8,128)(2,1)S(1)} %bitcast.10, bf16[64,2048]{1,0:T(8,128)(2,1)S(1)} %collective-permute-done.sib, ...), custom_call_target="tpu_custom_call" | custom-call | flops 268435456 | bytes 1048576 | tf_op jit(solution)/shard_map/pallas_call | solution.py:163
  42.9 0.0 collective-permute-done.4.far
  42.9 0.1 collective-permute-start.5
  43.0 0.4 collective-permute-start.6
  43.5 1.0 %collective-permute-done.5.arrived = bf16[8,2,8,1024]{3,2,1,0:T(8,128)(2,1)S(1)} collective-permute-done((bf16[8,2,8,1024]{3,2,1,0:T(8,128)(2,1)S(1)}, bf16[8,2,8,1024]{3,2,1,0:T(8,128)(2,1)S(1)}, u32[]{:S(2)}, u32[]{:S(2)}) %collective-permute-start.5) | collective-permute-done | bytes 262176 | tf_op jit(solution)/shard_map/ppermute | solution.py:267
  44.6 1.3 %collective-permute-start.7 = (bf16[8,2,8,1024]{3,2,1,0:T(8,128)(2,1)S(1)}, bf16[8,2,8,1024]{3,2,1,0:T(8,128)(2,1)S(1)}, u32[]{:S(2)}, u32[]{:S(2)}) collective-permute-start(bf16[8,2,8,1024]{3,2,1,0:T(8,128)(2,1)S(1)} %shard_map.59), channel_id=1, source_target_pairs={{0,16},{8,24},{16,0},{24,8},{1,17},{9,25},{17,1},{25,9},{2,18},{10... | collective-permute-start | bytes 786440 | tf_op jit(solution)/shard_map/ppermute | solution.py:270
  45.9 5.2 %shard_map.60.ours = f32[8,2,2,8,1024]{4,3,2,1,0:T(8,128)S(1)} custom-call(f32[32,2048]{1,0:T(8,128)S(1)} %get-tuple-element.20.factors, bf16[64,2048]{1,0:T(8,128)(2,1)S(1)} %bitcast.11, bf16[64,2048]{1,0:T(8,128)(2,1)S(1)} %collective-permute-done.sib, bf16[64,2048]{1,0:T(8,128)(2,1)S(1)} %collective-permute-done.1.far_own, ...), custom_call_target="tpu_custom_call" | custom-call | flops 268435456 | bytes 1048576 | tf_op jit(solution)/shard_map/pallas_call | solution.py:163
  51.1 1.9 %collective-permute-done.7.near = bf16[8,2,8,1024]{3,2,1,0:T(8,128)(2,1)S(1)} collective-permute-done((bf16[8,2,8,1024]{3,2,1,0:T(8,128)(2,1)S(1)}, bf16[8,2,8,1024]{3,2,1,0:T(8,128)(2,1)S(1)}, u32[]{:S(2)}, u32[]{:S(2)}) %collective-permute-start.7) | collective-permute-done | bytes 262176 | tf_op jit(solution)/shard_map/ppermute | solution.py:270
  53.0 0.0 collective-permute-done.6.arrived
  53.0 0.2 shard_map.61
  53.1 17.3 %all_to_all.11.parts = bf16[8,2,2,8,1024]{4,3,2,1,0:T(8,128)(2,1)S(1)} all-to-all(bf16[8,2,2,8,1024]{4,3,2,1,0:T(8,128)(2,1)S(1)} %shard_map.61), channel_id=1, replica_groups=mesh['ckpt'=4,'tensor'=8] {'tensor'}, dimensions={0} | all-to-all | bytes 1048576 | tf_op jit(solution)/shard_map/all_to_all | solution.py:287
  70.5 0.7 %shard_map.62 = bf16[32,512]{1,0:T(8,128)(2,1)} custom-call(bf16[8,2,2,8,1024]{4,3,2,1,0:T(8,128)(2,1)S(1)} %all_to_all.11.parts), custom_call_target="tpu_custom_call" | custom-call | tf_op jit(solution)/shard_map/pallas_call | solution.py:288
  (2 shorter events, 0.1 us)
Async XLA Ops:
  16.2 2.1 %collective-permute-start = (bf16[64,2048]{1,0:T(8,128)(2,1)S(1)}, bf16[64,2048]{1,0:T(8,128)(2,1)S(1)}, u32[]{:S(2)}, u32[]{:S(2)}) collective-permute-start(bf16[64,2048]{1,0:T(8,128)(2,1)S(1)} %bitcast.6), channel_id=1, source_target_pairs={{0,8},{8,0},{16,24},{24,16},{1,9},{9,1},{17,25},{25,17},{2,10},{10... | collective-permute-start | bytes 786440 | tf_op jit(solution)/shard_map/ppermute | solution.py:208
  16.2 15.4 %collective-permute-start.1 = (bf16[64,2048]{1,0:T(8,128)(2,1)S(1)}, bf16[64,2048]{1,0:T(8,128)(2,1)S(1)}, u32[]{:S(2)}, u32[]{:S(2)}) collective-permute-start(bf16[64,2048]{1,0:T(8,128)(2,1)S(1)} %bitcast.7), channel_id=1, source_target_pairs={{0,16},{8,24},{16,0},{24,8},{1,17},{9,25},{17,1},{25,9},{2,18},{10... | collective-permute-start | bytes 786440 | tf_op jit(solution)/shard_map/ppermute | solution.py:207
  26.4 5.6 %collective-permute-start.2 = (bf16[8,2,8,1024]{3,2,1,0:T(8,128)(2,1)S(1)}, bf16[8,2,8,1024]{3,2,1,0:T(8,128)(2,1)S(1)}, u32[]{:S(2)}, u32[]{:S(2)}) collective-permute-start(bf16[8,2,8,1024]{3,2,1,0:T(8,128)(2,1)S(1)} %get-tuple-element.24), channel_id=1, source_target_pairs={{0,8},{8,0},{16,24},{24,16},{1,9},{9,1},{17,25},{25,17},{2,10},{10... | collective-permute-start | bytes 786440 | tf_op jit(solution)/shard_map/ppermute | solution.py:231
  31.6 1.6 %collective-permute-start.3 = (bf16[64,2048]{1,0:T(8,128)(2,1)S(1)}, bf16[64,2048]{1,0:T(8,128)(2,1)S(1)}, u32[]{:S(2)}, u32[]{:S(2)}) collective-permute-start(bf16[64,2048]{1,0:T(8,128)(2,1)S(1)} %collective-permute-done.1.far_own), channel_id=1, source_target_pairs={{0,8},{8,0},{16,24},{24,16},{1,9},{9,1},{17,25},{25,17},{2,10},{10... | collective-permute-start | bytes 786440 | tf_op jit(solution)/shard_map/ppermute | solution.py:242
  33.2 9.7 %collective-permute-start.4 = (bf16[8,2,8,1024]{3,2,1,0:T(8,128)(2,1)S(1)}, bf16[8,2,8,1024]{3,2,1,0:T(8,128)(2,1)S(1)}, u32[]{:S(2)}, u32[]{:S(2)}) collective-permute-start(bf16[8,2,8,1024]{3,2,1,0:T(8,128)(2,1)S(1)} %shard_map.57), channel_id=1, source_target_pairs={{0,16},{8,24},{16,0},{24,8},{1,17},{9,25},{17,1},{25,9},{2,18},{10... | collective-permute-start | bytes 786440 | tf_op jit(solution)/shard_map/ppermute | solution.py:252
  42.9 1.6 %collective-permute-start.5 = (bf16[8,2,8,1024]{3,2,1,0:T(8,128)(2,1)S(1)}, bf16[8,2,8,1024]{3,2,1,0:T(8,128)(2,1)S(1)}, u32[]{:S(2)}, u32[]{:S(2)}) collective-permute-start(bf16[8,2,8,1024]{3,2,1,0:T(8,128)(2,1)S(1)} %get-tuple-element.30), channel_id=1, source_target_pairs={{0,8},{8,0},{16,24},{24,16},{1,9},{9,1},{17,25},{25,17},{2,10},{10... | collective-permute-start | bytes 786440 | tf_op jit(solution)/shard_map/ppermute | solution.py:267
  43.0 9.9 %collective-permute-start.6 = (bf16[8,2,2,8,1024]{4,3,2,1,0:T(8,128)(2,1)S(1)}, bf16[8,2,2,8,1024]{4,3,2,1,0:T(8,128)(2,1)S(1)}, u32[]{:S(2)}, u32[]{:S(2)}) collective-permute-start(bf16[8,2,2,8,1024]{4,3,2,1,0:T(8,128)(2,1)S(1)} %get-tuple-element.32), channel_id=1, source_target_pairs={{0,8},{8,0},{16,24},{24,16},{1,9},{9,1},{17,25},{25,17},{2,10},{10... | collective-permute-start | bytes 1572872 | tf_op jit(solution)/shard_map/ppermute | solution.py:268
  44.6 8.4 %collective-permute-start.7 = (bf16[8,2,8,1024]{3,2,1,0:T(8,128)(2,1)S(1)}, bf16[8,2,8,1024]{3,2,1,0:T(8,128)(2,1)S(1)}, u32[]{:S(2)}, u32[]{:S(2)}) collective-permute-start(bf16[8,2,8,1024]{3,2,1,0:T(8,128)(2,1)S(1)} %shard_map.59), channel_id=1, source_target_pairs={{0,16},{8,24},{16,0},{24,8},{1,17},{9,25},{17,1},{25,9},{2,18},{10... | collective-permute-start | bytes 786440 | tf_op jit(solution)/shard_map/ppermute | solution.py:270

commit v5 on v4

--- a/solution.py
+++ b/solution.py
@@ -38,17 +38,17 @@
     row = lax.broadcasted_iota(jnp.int32, (blocks, width), 0)
     spread = jnp.where(column == row, 1.0, 0.0).astype(jnp.float32)
     kept = jnp.where(mask.reshape(-1, blocks) != 0, scale, 0.0).astype(jnp.float32)
-    factors[...] = jnp.dot(kept, spread, preferred_element_type=jnp.float32)
-
-
-def terms(factors, weights, m, owner):
-    strips = weights.shape[0] // BLOCK
-    first = m * (factors.shape[0] // 2) + owner * strips
+    rows = kept.shape[0]
+    factors[:rows] = jnp.dot(kept, spread, preferred_element_type=jnp.float32)
+    factors[rows:] = jnp.ones((factors.shape[0] - rows, width), jnp.float32)
+
+
+def product(held, factors, weights, first):
     scaled = []
-    for i in range(strips):
+    for i in range(weights.shape[0] // BLOCK):
         factor = factors[pl.ds(first + i, 1), :].astype(weights.dtype)
         scaled.append(weights[i * BLOCK : (i + 1) * BLOCK] * factor)
-    return jnp.concatenate(scaled, axis=0)
+    return dot_rows(held, jnp.concatenate(scaled, axis=0))
 
 
 def chip_and_core():
@@ -57,7 +57,7 @@
 
 
 def put(view, total, core):
-    groups, rows = view.shape[-5 if len(view.shape) == 5 else 0], view.shape[-2]
+    groups, rows = view.shape[0], view.shape[-2]
     split = total.reshape(-1, CORES, groups, rows, total.shape[-1])
     for x in range(split.shape[0]):
         for side in range(CORES):
@@ -67,96 +67,106 @@
                 view[here] = split[x, side, g].astype(view.dtype)
 
 
-def half_of(ref, m):
-    size = ref.shape[-1] // 2
-    return ref.at[(slice(None),) * (len(ref.shape) - 1) + (slice(m * size, (m + 1) * size),)]
-
-
-def fetch(delta, kept, sems, owners, chunks):
-    slab_own = kept.shape[1]
-    span = slab_own // chunks
-    copies = []
-    for part, (m, owner) in enumerate(owners):
+class Rows:
+    def __init__(self, source, kept, sems, owners, first=0):
+        self.source, self.kept, self.sems, self.owners, self.first = source, kept, sems, owners, first
+
+    def owner(self, part):
+        owner = self.owners[0]
+        return owner if len(self.owners) == 1 else jnp.where(part < 2, owner, self.owners[1])
+
+    def copies(self, part):
+        slab_own, chunks = self.kept.shape[1], self.sems.shape[1]
+        span = slab_own // chunks
+        at = self.first + part
         for h in range(chunks):
-            rows = pl.ds(pl.multiple_of(owner * slab_own + h * span, span), span)
-            copy = pltpu.make_async_copy(
-                delta.at[m, rows, :], kept.at[part, pl.ds(h * span, span), :], sems.at[part, h]
+            rows = pl.ds(pl.multiple_of(self.owner(part) * slab_own + h * span, span), span)
+            yield pltpu.make_async_copy(
+                self.source.at[part % 2, rows, :],
+                self.kept.at[at, pl.ds(h * span, span), :],
+                self.sems.at[at, h],
             )
-            copy.start()
-            copies.append(copy)
-    return copies
-
-
-def owners_of(chip, core):
-    return [(m, chip * CORES + core) for m in range(2)]
-
-
-def wait_for(copies, part, chunks):
-    for copy in copies[part * chunks : (part + 1) * chunks]:
-        copy.wait()
+
+    def start(self):
+        for part in range(2 * len(self.owners)):
+            for copy in self.copies(part):
+                copy.start()
+
+    def wait(self, part):
+        for copy in self.copies(part):
+            copy.wait()
+
+
+def first_factor(kept, factors, part, owner):
+    strips = kept.shape[1] // BLOCK
+    blocks = (factors.shape[0] - strips) // 2
+    return part % 2 * blocks + owner * strips
 
 
 def early_kernel(
-    scale_num, mask_hbm, own, sib, delta, theirs, kept, factors, held, mask, sems, mask_sem
+    scale_num, mask_hbm, own, sib, delta, theirs, ours, kept, factors, held, mask, sems, mask_sem
 ):
     chip, core = chip_and_core()
-    chunks = sems.shape[1]
     mask_copy = pltpu.make_async_copy(mask_hbm, mask, mask_sem)
     mask_copy.start()
-    owners = owners_of(1 - chip, 1 - core) + owners_of(1 - chip, core)
-    copies = fetch(delta, kept, sems, owners, chunks)
+    rows = Rows(delta, kept, sems, [(1 - chip) * CORES + at for at in (1 - core, core)])
+    rows.start()
     gather_held(held, (own, sib))
     mask_copy.wait()
     expand(mask[...], scale_num[0].astype(jnp.float32) / DEN, factors)
-    for part, (m, owner) in enumerate(owners[:2]):
-        wait_for(copies, part, chunks)
-        total = dot_rows(held[...], terms(factors, kept.at[part], m, owner))
-        put(half_of(theirs, m), total, core)
-    for part in (2, 3):
-        wait_for(copies, part, chunks)
-
-
-def early_rest_kernel(factors, own, sib, kept, ours, held):
-    chip, core = chip_and_core()
-    gather_held(held, (own, sib))
-    for part, (m, owner) in enumerate(owners_of(1 - chip, core)):
-        total = dot_rows(held[...], terms(factors, kept.at[2 + part], m, owner))
-        put(half_of(ours, m), total, core)
+
+    @pl.loop(0, 4)
+    def _(part):
+        rows.wait(part)
+        first = first_factor(kept, factors, part, rows.owner(part))
+        total = product(held[...], factors, kept.at[part], first)
+        pl.when(part < 2)(lambda: put(theirs.at[part % 2], total, core))
+        pl.when(part >= 2)(lambda: put(ours.at[part % 2], total, core))
 
 
 def later_kernel(
     factors, own, sib, far_own, far_sib, kept, delta, theirs, ours, theirs_home, home, held, sems
 ):
     chip, core = chip_and_core()
-    chunks = sems.shape[1]
     half = held.shape[0] // 2
-    home_owners = owners_of(chip, 1 - core)
-    copies = fetch(delta, home, sems, home_owners, chunks)
+    rows = Rows(delta, home, sems, [chip * CORES + 1 - core])
+    rows.start()
     gather_held(held, (own, sib, far_own, far_sib))
-    owners = owners_of(1 - chip, 1 - core) + owners_of(1 - chip, core)
-    for part, (m, owner) in enumerate(owners):
-        total = dot_rows(held[half:], terms(factors, kept.at[part], m, owner))
-        put(half_of(theirs if part < 2 else ours, m), total, core)
-    for part, (m, owner) in enumerate(home_owners):
-        wait_for(copies, part, chunks)
-        total = dot_rows(held[...], terms(factors, home.at[part], m, owner))
-        put(half_of(theirs_home, m), total, core)
-
-
-def home_kernel(
-    factors, own, sib, far_own, far_sib, delta, base, ours, kept, kept_base, held, sems, base_sems
-):
+    far = Rows(None, kept, None, [(1 - chip) * CORES + at for at in (1 - core, core)])
+
+    @pl.loop(0, 4)
+    def _(part):
+        first = first_factor(kept, factors, part, far.owner(part))
+        total = product(held[half:], factors, kept.at[part], first)
+        pl.when(part < 2)(lambda: put(theirs.at[part % 2], total, core))
+        pl.when(part >= 2)(lambda: put(ours.at[part % 2], total, core))
+
+    @pl.loop(0, 2)
+    def _(part):
+        rows.wait(part)
+        first = first_factor(home, factors, part, rows.owner(part))
+        put(theirs_home.at[part], product(held[...], factors, home.at[part], first), core)
+
+
+def home_kernel(factors, own, sib, far_own, far_sib, delta, base, ours, kept, held, total, sems):
     chip, core = chip_and_core()
-    chunks = sems.shape[1]
-    owners = owners_of(chip, core)
-    copies = fetch(delta, kept, sems, owners, chunks)
-    base_copies = fetch(base, kept_base, base_sems, [(0, 0), (1, 0)], chunks)
+    rows = Rows(delta, kept, sems, [chip * CORES + core])
+    base_rows = Rows(base, kept, sems, [0], first=2)
+    rows.start()
+    base_rows.start()
     gather_held(held, (own, sib, far_own, far_sib))
-    for part, (m, owner) in enumerate(owners):
-        wait_for(copies, part, chunks)
-        total = dot_rows(held[...], terms(factors, kept.at[part], m, owner))
-        wait_for(base_copies, part, chunks)
-        put(half_of(ours, m), total + dot_rows(held[...], kept_base[part]), core)
+    total[...] = jnp.zeros_like(total)
+    ones = factors.shape[0] - kept.shape[1] // BLOCK
+
+    @pl.loop(0, 4)
+    def _(part):
+        pl.when(part < 2)(lambda: rows.wait(part))
+        pl.when(part >= 2)(lambda: base_rows.wait(part - 2))
+        first = jnp.where(part < 2, first_factor(kept, factors, part, rows.owner(part)), ones)
+        total[part % 2] += product(held[...], factors, kept.at[part], first)
+
+    for m in range(2):
+        put(ours.at[m], total[m], core)
 
 
 def call(kernel, outs, scratch, in_specs, operands, flops, traffic):
@@ -176,9 +186,12 @@
 
 
 def join_home_kernel(ours, arrived, near, far, out):
-    for x, other in enumerate((near, far)):
-        total = ours[:, x] + arrived[:, x].astype(jnp.float32) + other[...].astype(jnp.float32)
-        out[:, x] = total.astype(out.dtype)
+    slab_own = ours.shape[-1]
+    for m in range(2):
+        for x, other in enumerate((near, far)):
+            total = ours[m, :, x] + arrived[m, :, x].astype(jnp.float32)
+            total = total + other[m].astype(jnp.float32)
+            out[:, x, :, :, m * slab_own : (m + 1) * slab_own] = total.astype(out.dtype)
 
 
 def last_kernel(parts, out, total):
@@ -210,13 +223,14 @@
     half = groups * rows * CORES
     chunks = 2
     part = jax.ShapeDtypeStruct
-    pair = (groups, CORES, rows, 2 * slab_own)
-    four = (groups, 2, CORES, rows, 2 * slab_own)
+    pair = (2, groups, CORES, rows, slab_own)
+    four = (2, groups, 2, CORES, rows, slab_own)
     weights = (4, slab_own, width)
     size = 4 * slab_own * width
-    theirs, kept, factors = call(
+    blocks = mask.shape[0] * mask.shape[1] + slab_own // BLOCK
+    theirs, ours, kept, factors = call(
         early_kernel,
-        [part(pair, bf16), part(weights, bf16), part((mask.shape[0] * mask.shape[1], width), f32)],
+        [part(pair, bf16), part(pair, f32), part(weights, bf16), part((blocks, width), f32)],
         [
             pltpu.VMEM((half, width), bf16),
             pltpu.VMEM(mask.shape, mask.dtype),
@@ -225,20 +239,11 @@
         ],
         [SMEM, HBM, VMEM, VMEM, HBM],
         (scale_num, pltpu.with_memory_space_constraint(mask, pltpu.HBM), own, sib, delta),
-        half * size,
+        2 * half * size,
         2 * size,
     )
     near = core_swap(theirs)
-    (ours,) = call(
-        early_rest_kernel,
-        [part(pair, f32)],
-        [pltpu.VMEM((half, width), bf16)],
-        [VMEM] * 4,
-        (factors, own, sib, kept),
-        half * size,
-        size,
-    )
-    far_own, ours = lax.optimization_barrier((far_own, ours))
+    far_own, theirs = lax.optimization_barrier((far_own, theirs))
     far_sib = core_swap(far_own)
     simple = lambda kernel, shape, *xs: pl.pallas_call(
         kernel,
@@ -272,18 +277,19 @@
         home_kernel,
         [part(four, f32)],
         [
-            pltpu.VMEM((2, slab_own, width), bf16),
-            pltpu.VMEM((2, slab_own, width), bf16),
+            pltpu.VMEM(weights, bf16),
             pltpu.VMEM((2 * half, width), bf16),
-            pltpu.SemaphoreType.DMA((2, chunks)),
-            pltpu.SemaphoreType.DMA((2, chunks)),
+            pltpu.VMEM((2, 2 * half, slab_own), f32),
+            pltpu.SemaphoreType.DMA((4, chunks)),
         ],
         [VMEM] * 5 + [HBM, HBM],
         (factors, own, sib, far_own, far_sib, delta, base),
         4 * half * size,
         2 * size,
     )
-    whole = simple(join_home_kernel, four, ours, near_home, over_second, over_first)
+    whole = simple(
+        join_home_kernel, (groups, 2, CORES, rows, 2 * slab_own), ours, near_home, over_second, over_first
+    )
     parts = lax.all_to_all(whole, "tensor", 0, 0, tiled=True)
     return pl.pallas_call(
         last_kernel,

time: 71.5 us -> 67.4 us (0.943)
  Pallas kernels: 28 us -> 23.4 us
    pallas_call x4 -> x3, Pallas kernels: 27 us -> 22.4 us  [call(): pl.pallas_call(kernel, out_shape=outs, in_specs=in_specs, out_specs=[VMEM...]
    ppermute x1, waiting for transfers between devices: 0.01 us -> 1.02 us  [local_pair(): near = core_swap(theirs)]
    ppermute x1, waiting for transfers between devices: 1.2 us -> 0.32 us  [local_pair(): far_sib = core_swap(far_own)]
  transfers between devices with their start and end apart: 8 -> 8, of which waited for: 3 -> 4; matrix products, arithmetic and copies ran while one was open for 0% -> 0% of each run, Pallas kernels for 38% -> 34%
where the time goes in v5:
time: 67.4 us; the launch traced here: 67.1 us
  blocking collectives  33.5 us (50%)
  Pallas kernels  23.4 us (35%)
  waiting for transfers between devices  4.78 us (7%)
  starting transfers between devices  4.73 us (7%)
  between operations  0.72 us (1%)
    pallas_call x3, Pallas kernels, call(): pl.pallas_call(kernel, out_shape=outs, in_specs=in_specs, out_specs=[VMEM...  22.4 us
    all_to_all x1, blocking collectives, local_pair(): parts = lax.all_to_all(whole, 'tensor', 0, 0, tiled=True)  17.3 us
    all_to_all x1, blocking collectives, local_pair(): lax.all_to_all(cut, 'tensor', 0, 0, tiled=True)  16.2 us
    ppermute x1, waiting for transfers between devices, local_pair(): over_second = chip_swap(second)  2.4 us
    ppermute x1, starting transfers between devices, local_pair(): far_own = chip_swap(own)  1.49 us
  transfers between devices with their start and end apart: 8, of which 4 were waited for; matrix products, arithmetic and copies ran while one was open for 0% of the time, Pallas kernels for 34%

profile of v5, /device:TPU:0, one launch (start us, length us, event | category | flops | bytes accessed | tf_op | source)
XLA Modules:
  0.0 67.1 jit_solution(6901347016594936946)
XLA Ops:
  0.0 16.2 %all_to_all.10 = bf16[8,8,2048]{2,1,0:T(8,128)(2,1)S(1)} all-to-all(bf16[8,8,2048]{2,1,0:T(8,128)(2,1)} %bitcast.14), channel_id=1, replica_groups=mesh['ckpt'=4,'tensor'=8] {'tensor'}, dimensions={0} | all-to-all | bytes 524288 | tf_op jit(solution)/shard_map/all_to_all | solution.py:219
  16.2 0.0 collective-permute-start
  16.2 1.5 %collective-permute-start.1 = (bf16[64,2048]{1,0:T(8,128)(2,1)S(1)}, bf16[64,2048]{1,0:T(8,128)(2,1)S(1)}, u32[]{:S(2)}, u32[]{:S(2)}) collective-permute-start(bf16[64,2048]{1,0:T(8,128)(2,1)S(1)} %bitcast.7), channel_id=1, source_target_pairs={{0,16},{8,24},{16,0},{24,8},{1,17},{9,25},{17,1},{25,9},{2,18},{10... | collective-permute-start | bytes 786440 | tf_op jit(solution)/shard_map/ppermute | solution.py:220
  18.3 0.0 collective-permute-done.sib
  18.4 9.2 %shard_map.55 = (bf16[2,8,2,8,512]{4,3,2,1,0:T(8,128)(2,1)S(1)}, f32[2,8,2,8,512]{4,3,2,1,0:T(8,128)S(1)}, bf16[4,512,2048]{2,1,0:T(8,128)(2,1)}, f32[36,2048]{1,0:T(8,128)S(1)}) custom-call(s32[1]{0:T(128)S(6)} %copy.6.scale_num, s32[2,16,16]{2,1,0:T(8,128)} %bitcast.15, bf16[64,2048]{1,0:T(8,128)(2,1)S(1)} %bitcast.8, ...), custom_call_target="tpu_custom_call" | custom-call | flops 134217728 | bytes 1048576 | tf_op jit(solution)/shard_map/pallas_call | solution.py:173
  27.6 0.3 collective-permute-start.2
  27.9 0.0 collective-permute-done.1.far_own
  27.9 0.3 collective-permute-start.3
  28.2 1.0 %collective-permute-done.2.arrived = bf16[2,8,2,8,512]{4,3,2,1,0:T(8,128)(2,1)S(1)} collective-permute-done((bf16[2,8,2,8,512]{4,3,2,1,0:T(8,128)(2,1)S(1)}, bf16[2,8,2,8,512]{4,3,2,1,0:T(8,128)(2,1)S(1)}, u32[]{:S(2)}, u32[]{:S(2)}) %collective-permute-start.2) | collective-permute-done | bytes 262176 | tf_op jit(solution)/shard_map/ppermute | solution.py:245
  29.2 0.3 collective-permute-done.3.far_sib
  29.5 0.9 %collective-permute-start.4 = (bf16[2,8,2,8,512]{4,3,2,1,0:T(8,128)(2,1)S(1)}, bf16[2,8,2,8,512]{4,3,2,1,0:T(8,128)(2,1)S(1)}, u32[]{:S(2)}, u32[]{:S(2)}) collective-permute-start(bf16[2,8,2,8,512]{4,3,2,1,0:T(8,128)(2,1)S(1)} %shard_map.56), channel_id=1, source_target_pairs={{0,16},{8,24},{16,0},{24,8},{1,17},{9,25},{17,1},{25,9},{2,18},{10... | collective-permute-start | bytes 786440 | tf_op jit(solution)/shard_map/ppermute | solution.py:257
  30.4 8.4 %shard_map.57 = (bf16[2,8,2,8,512]{4,3,2,1,0:T(8,128)(2,1)S(1)}, f32[2,8,2,8,512]{4,3,2,1,0:T(8,128)S(1)}, bf16[2,8,2,2,8,512]{5,4,3,2,1,0:T(8,128)(2,1)S(1)}) custom-call(f32[36,2048]{1,0:T(8,128)S(1)} %get-tuple-element.20.factors, bf16[64,2048]{1,0:T(8,128)(2,1)S(1)} %bitcast.9, bf16[64,2048]{1,0:T(8,128)(2,1)S(1)} %collective-permute-done.sib, ...), custom_call_target="tpu_custom_call" | custom-call | flops 268435456 | bytes 1048576 | tf_op jit(solution)/shard_map/pallas_call | solution.py:173
  38.8 0.0 collective-permute-done.4.far
  38.8 0.1 collective-permute-start.5
  38.9 0.5 collective-permute-start.6
  39.4 1.0 %collective-permute-done.5.arrived = bf16[2,8,2,8,512]{4,3,2,1,0:T(8,128)(2,1)S(1)} collective-permute-done((bf16[2,8,2,8,512]{4,3,2,1,0:T(8,128)(2,1)S(1)}, bf16[2,8,2,8,512]{4,3,2,1,0:T(8,128)(2,1)S(1)}, u32[]{:S(2)}, u32[]{:S(2)}) %collective-permute-start.5) | collective-permute-done | bytes 262176 | tf_op jit(solution)/shard_map/ppermute | solution.py:272
  40.5 1.2 %collective-permute-start.7 = (bf16[2,8,2,8,512]{4,3,2,1,0:T(8,128)(2,1)S(1)}, bf16[2,8,2,8,512]{4,3,2,1,0:T(8,128)(2,1)S(1)}, u32[]{:S(2)}, u32[]{:S(2)}) collective-permute-start(bf16[2,8,2,8,512]{4,3,2,1,0:T(8,128)(2,1)S(1)} %shard_map.58), channel_id=1, source_target_pairs={{0,16},{8,24},{16,0},{24,8},{1,17},{9,25},{17,1},{25,9},{2,18},{10... | collective-permute-start | bytes 786440 | tf_op jit(solution)/shard_map/ppermute | solution.py:275
  41.7 4.8 %shard_map.59.ours = f32[2,8,2,2,8,512]{5,4,3,2,1,0:T(8,128)S(1)} custom-call(f32[36,2048]{1,0:T(8,128)S(1)} %get-tuple-element.20.factors, bf16[64,2048]{1,0:T(8,128)(2,1)S(1)} %bitcast.10, bf16[64,2048]{1,0:T(8,128)(2,1)S(1)} %collective-permute-done.sib, bf16[64,2048]{1,0:T(8,128)(2,1)S(1)} %collective-permute-done.1.far_own, ...), custom_call_target="tpu_custom_call" | custom-call | flops 268435456 | bytes 1048576 | tf_op jit(solution)/shard_map/pallas_call | solution.py:173
  46.5 2.4 %collective-permute-done.7.near = bf16[2,8,2,8,512]{4,3,2,1,0:T(8,128)(2,1)S(1)} collective-permute-done((bf16[2,8,2,8,512]{4,3,2,1,0:T(8,128)(2,1)S(1)}, bf16[2,8,2,8,512]{4,3,2,1,0:T(8,128)(2,1)S(1)}, u32[]{:S(2)}, u32[]{:S(2)}) %collective-permute-start.7) | collective-permute-done | bytes 262176 | tf_op jit(solution)/shard_map/ppermute | solution.py:275
  48.9 0.0 collective-permute-done.6.arrived
  48.9 0.2 shard_map.60
  49.1 17.3 %all_to_all.11.parts = bf16[8,2,2,8,1024]{4,3,2,1,0:T(8,128)(2,1)S(1)} all-to-all(bf16[8,2,2,8,1024]{4,3,2,1,0:T(8,128)(2,1)S(1)} %shard_map.60), channel_id=1, replica_groups=mesh['ckpt'=4,'tensor'=8] {'tensor'}, dimensions={0} | all-to-all | bytes 1048576 | tf_op jit(solution)/shard_map/all_to_all | solution.py:293
  66.4 0.7 %shard_map.61 = bf16[32,512]{1,0:T(8,128)(2,1)} custom-call(bf16[8,2,2,8,1024]{4,3,2,1,0:T(8,128)(2,1)S(1)} %all_to_all.11.parts), custom_call_target="tpu_custom_call" | custom-call | tf_op jit(solution)/shard_map/pallas_call | solution.py:294
  (2 shorter events, 0.1 us)
Async XLA Ops:
  16.2 2.1 %collective-permute-start = (bf16[64,2048]{1,0:T(8,128)(2,1)S(1)}, bf16[64,2048]{1,0:T(8,128)(2,1)S(1)}, u32[]{:S(2)}, u32[]{:S(2)}) collective-permute-start(bf16[64,2048]{1,0:T(8,128)(2,1)S(1)} %bitcast.6), channel_id=1, source_target_pairs={{0,8},{8,0},{16,24},{24,16},{1,9},{9,1},{17,25},{25,17},{2,10},{10... | collective-permute-start | bytes 786440 | tf_op jit(solution)/shard_map/ppermute | solution.py:221
  16.2 11.7 %collective-permute-start.1 = (bf16[64,2048]{1,0:T(8,128)(2,1)S(1)}, bf16[64,2048]{1,0:T(8,128)(2,1)S(1)}, u32[]{:S(2)}, u32[]{:S(2)}) collective-permute-start(bf16[64,2048]{1,0:T(8,128)(2,1)S(1)} %bitcast.7), channel_id=1, source_target_pairs={{0,16},{8,24},{16,0},{24,8},{1,17},{9,25},{17,1},{25,9},{2,18},{10... | collective-permute-start | bytes 786440 | tf_op jit(solution)/shard_map/ppermute | solution.py:220
  27.6 1.6 %collective-permute-start.2 = (bf16[2,8,2,8,512]{4,3,2,1,0:T(8,128)(2,1)S(1)}, bf16[2,8,2,8,512]{4,3,2,1,0:T(8,128)(2,1)S(1)}, u32[]{:S(2)}, u32[]{:S(2)}) collective-permute-start(bf16[2,8,2,8,512]{4,3,2,1,0:T(8,128)(2,1)S(1)} %get-tuple-element.21), channel_id=1, source_target_pairs={{0,8},{8,0},{16,24},{24,16},{1,9},{9,1},{17,25},{25,17},{2,10},{10... | collective-permute-start | bytes 786440 | tf_op jit(solution)/shard_map/ppermute | solution.py:245
  27.9 1.6 %collective-permute-start.3 = (bf16[64,2048]{1,0:T(8,128)(2,1)S(1)}, bf16[64,2048]{1,0:T(8,128)(2,1)S(1)}, u32[]{:S(2)}, u32[]{:S(2)}) collective-permute-start(bf16[64,2048]{1,0:T(8,128)(2,1)S(1)} %collective-permute-done.1.far_own), channel_id=1, source_target_pairs={{0,8},{8,0},{16,24},{24,16},{1,9},{9,1},{17,25},{25,17},{2,10},{10... | collective-permute-start | bytes 786440 | tf_op jit(solution)/shard_map/ppermute | solution.py:247
  29.5 9.3 %collective-permute-start.4 = (bf16[2,8,2,8,512]{4,3,2,1,0:T(8,128)(2,1)S(1)}, bf16[2,8,2,8,512]{4,3,2,1,0:T(8,128)(2,1)S(1)}, u32[]{:S(2)}, u32[]{:S(2)}) collective-permute-start(bf16[2,8,2,8,512]{4,3,2,1,0:T(8,128)(2,1)S(1)} %shard_map.56), channel_id=1, source_target_pairs={{0,16},{8,24},{16,0},{24,8},{1,17},{9,25},{17,1},{25,9},{2,18},{10... | collective-permute-start | bytes 786440 | tf_op jit(solution)/shard_map/ppermute | solution.py:257
  38.8 1.6 %collective-permute-start.5 = (bf16[2,8,2,8,512]{4,3,2,1,0:T(8,128)(2,1)S(1)}, bf16[2,8,2,8,512]{4,3,2,1,0:T(8,128)(2,1)S(1)}, u32[]{:S(2)}, u32[]{:S(2)}) collective-permute-start(bf16[2,8,2,8,512]{4,3,2,1,0:T(8,128)(2,1)S(1)} %get-tuple-element.30), channel_id=1, source_target_pairs={{0,8},{8,0},{16,24},{24,16},{1,9},{9,1},{17,25},{25,17},{2,10},{10... | collective-permute-start | bytes 786440 | tf_op jit(solution)/shard_map/ppermute | solution.py:272
  38.9 10.0 %collective-permute-start.6 = (bf16[2,8,2,2,8,512]{5,4,3,2,1,0:T(8,128)(2,1)S(1)}, bf16[2,8,2,2,8,512]{5,4,3,2,1,0:T(8,128)(2,1)S(1)}, u32[]{:S(2)}, u32[]{:S(2)}) collective-permute-start(bf16[2,8,2,2,8,512]{5,4,3,2,1,0:T(8,128)(2,1)S(1)} %get-tuple-element.32), channel_id=1, source_target_pairs={{0,8},{8,0},{16,24},{24,16},{1,9},{9,1},{17,25},{25,17},{2,10},{10... | collective-permute-start | bytes 1572872 | tf_op jit(solution)/shard_map/ppermute | solution.py:273
  40.5 8.4 %collective-permute-start.7 = (bf16[2,8,2,8,512]{4,3,2,1,0:T(8,128)(2,1)S(1)}, bf16[2,8,2,8,512]{4,3,2,1,0:T(8,128)(2,1)S(1)}, u32[]{:S(2)}, u32[]{:S(2)}) collective-permute-start(bf16[2,8,2,8,512]{4,3,2,1,0:T(8,128)(2,1)S(1)} %shard_map.58), channel_id=1, source_target_pairs={{0,16},{8,24},{16,0},{24,8},{1,17},{9,25},{17,1},{25,9},{2,18},{10... | collective-permute-start | bytes 786440 | tf_op jit(solution)/shard_map/ppermute | solution.py:275

commit v6 on v5

--- a/solution.py
+++ b/solution.py
@@ -176,7 +176,7 @@
         in_specs=in_specs,
         out_specs=[VMEM] * len(outs),
         scratch_shapes=scratch,
-        compiler_params=pltpu.CompilerParams(vmem_limit_bytes=50 * MIB),
+        compiler_params=pltpu.CompilerParams(vmem_limit_bytes=20 * MIB),
         cost_estimate=pl.CostEstimate(flops=flops // 8, bytes_accessed=traffic // 8, transcendentals=0),
     )(*operands)
 
@@ -211,7 +211,8 @@
     rows, width = tokens.shape[0], tokens.shape[1] // groups
     slab_own = base.shape[1]
     f32, bf16 = jnp.float32, jnp.bfloat16
-    mask, delta = drop_mask[0], delta[0]
+    in_hbm = lambda x: pltpu.with_memory_space_constraint(x, pltpu.HBM)
+    mask, delta, base = in_hbm(drop_mask[0]), in_hbm(delta[0]), in_hbm(base)
     core_swap = functools.partial(lax.ppermute, axis_name="ckpt", perm=[(i, i ^ 1) for i in range(4)])
     chip_swap = functools.partial(lax.ppermute, axis_name="ckpt", perm=[(i, i ^ 2) for i in range(4)])
 
@@ -238,7 +239,7 @@
             pltpu.SemaphoreType.DMA(()),
         ],
         [SMEM, HBM, VMEM, VMEM, HBM],
-        (scale_num, pltpu.with_memory_space_constraint(mask, pltpu.HBM), own, sib, delta),
+        (scale_num, mask, own, sib, delta),
         2 * half * size,
         2 * size,
     )

time: 67.4 us -> 63.3 us (0.939)
  Pallas kernels: 23.4 us -> 16.7 us
  waiting for transfers between devices: 4.78 us -> 6.65 us
    pallas_call x3, Pallas kernels: 22.4 us -> 15.8 us  [call(): pl.pallas_call(kernel, out_shape=outs, in_specs=in_specs, out_specs=[VMEM...]
    ppermute x1, waiting for transfers between devices: 0.01 us -> 1.82 us  [local_pair(): over_first = chip_swap(first)]
  transfers between devices with their start and end apart: 8 -> 8, of which waited for: 4 -> 6; matrix products, arithmetic and copies ran while one was open for 0% -> 0% of each run, Pallas kernels for 34% -> 25%
where the time goes in v6:
time: 63.3 us; the launch traced here: 63 us
  blocking collectives  33.5 us (53%)
  Pallas kernels  16.7 us (26%)
  waiting for transfers between devices  6.65 us (11%)
  starting transfers between devices  5.39 us (9%)
  between operations  0.7 us (1%)
    all_to_all x1, blocking collectives, local_pair(): parts = lax.all_to_all(whole, 'tensor', 0, 0, tiled=True)  17.3 us
    all_to_all x1, blocking collectives, local_pair(): lax.all_to_all(cut, 'tensor', 0, 0, tiled=True)  16.2 us
    pallas_call x3, Pallas kernels, call(): pl.pallas_call(kernel, out_shape=outs, in_specs=in_specs, out_specs=[VMEM...  15.8 us
    ppermute x1, waiting for transfers between devices, local_pair(): over_second = chip_swap(second)  2.07 us
    ppermute x1, waiting for transfers between devices, local_pair(): over_first = chip_swap(first)  1.82 us
    ppermute x1, starting transfers between devices, local_pair(): over_second = chip_swap(second)  1.56 us
    ppermute x1, starting transfers between devices, local_pair(): far_own = chip_swap(own)  1.49 us
    ppermute x1, starting transfers between devices, local_pair(): over_first = chip_swap(first)  1.49 us
  transfers between devices with their start and end apart: 8, of which 6 were waited for; matrix products, arithmetic and copies ran while one was open for 0% of the time, Pallas kernels for 25%

profile of v6, /device:TPU:0, one launch (start us, length us, event | category | flops | bytes accessed | tf_op | source)
XLA Modules:
  0.0 63.0 jit_solution(8829959634581521178)
XLA Ops:
  0.0 16.2 %all_to_all.10 = bf16[8,8,2048]{2,1,0:T(8,128)(2,1)S(1)} all-to-all(bf16[8,8,2048]{2,1,0:T(8,128)(2,1)} %bitcast.14), channel_id=1, replica_groups=mesh['ckpt'=4,'tensor'=8] {'tensor'}, dimensions={0} | all-to-all | bytes 524288 | tf_op jit(solution)/shard_map/all_to_all | solution.py:220
  16.2 0.0 collective-permute-start
  16.2 1.5 %collective-permute-start.1 = (bf16[64,2048]{1,0:T(8,128)(2,1)S(1)}, bf16[64,2048]{1,0:T(8,128)(2,1)S(1)}, u32[]{:S(2)}, u32[]{:S(2)}) collective-permute-start(bf16[64,2048]{1,0:T(8,128)(2,1)S(1)} %bitcast.7), channel_id=1, source_target_pairs={{0,16},{8,24},{16,0},{24,8},{1,17},{9,25},{17,1},{25,9},{2,18},{10... | collective-permute-start | bytes 786440 | tf_op jit(solution)/shard_map/ppermute | solution.py:221
  18.3 0.0 collective-permute-done.sib
  18.4 6.0 %shard_map.55 = (bf16[2,8,2,8,512]{4,3,2,1,0:T(8,128)(2,1)S(1)}, f32[2,8,2,8,512]{4,3,2,1,0:T(8,128)S(1)}, bf16[4,512,2048]{2,1,0:T(8,128)(2,1)S(1)}, f32[36,2048]{1,0:T(8,128)S(1)}) custom-call(s32[1]{0:T(128)S(6)} %copy.6.scale_num, s32[2,16,16]{2,1,0:T(8,128)} %bitcast.15, bf16[64,2048]{1,0:T(8,128)(2,1)S(1)} %bitcast.8, ...), custom_call_target="tpu_custom_call" | custom-call | flops 134217728 | bytes 1048576 | tf_op jit(solution)/shard_map/pallas_call | solution.py:173
  24.3 0.3 collective-permute-start.2
  24.7 0.2 collective-permute-done.1.far_own
  24.9 0.0 collective-permute-start.3
  24.9 1.0 %collective-permute-done.2.arrived = bf16[2,8,2,8,512]{4,3,2,1,0:T(8,128)(2,1)S(1)} collective-permute-done((bf16[2,8,2,8,512]{4,3,2,1,0:T(8,128)(2,1)S(1)}, bf16[2,8,2,8,512]{4,3,2,1,0:T(8,128)(2,1)S(1)}, u32[]{:S(2)}, u32[]{:S(2)}) %collective-permute-start.2) | collective-permute-done | bytes 262176 | tf_op jit(solution)/shard_map/ppermute | solution.py:246
  26.0 0.5 collective-permute-done.3.far_sib
  26.5 1.5 %collective-permute-start.4 = (bf16[2,8,2,8,512]{4,3,2,1,0:T(8,128)(2,1)S(1)}, bf16[2,8,2,8,512]{4,3,2,1,0:T(8,128)(2,1)S(1)}, u32[]{:S(2)}, u32[]{:S(2)}) collective-permute-start(bf16[2,8,2,8,512]{4,3,2,1,0:T(8,128)(2,1)S(1)} %shard_map.56), channel_id=1, source_target_pairs={{0,16},{8,24},{16,0},{24,8},{1,17},{9,25},{17,1},{25,9},{2,18},{10... | collective-permute-start | bytes 786440 | tf_op jit(solution)/shard_map/ppermute | solution.py:258
  27.9 5.0 %shard_map.57 = (bf16[2,8,2,8,512]{4,3,2,1,0:T(8,128)(2,1)S(1)}, f32[2,8,2,8,512]{4,3,2,1,0:T(8,128)S(1)}, bf16[2,8,2,2,8,512]{5,4,3,2,1,0:T(8,128)(2,1)S(1)}) custom-call(f32[36,2048]{1,0:T(8,128)S(1)} %get-tuple-element.20.factors, bf16[64,2048]{1,0:T(8,128)(2,1)S(1)} %bitcast.9, bf16[64,2048]{1,0:T(8,128)(2,1)S(1)} %collective-permute-done.sib, ...), custom_call_target="tpu_custom_call" | custom-call | flops 268435456 | bytes 1048576 | tf_op jit(solution)/shard_map/pallas_call | solution.py:173
  33.0 1.8 %collective-permute-done.4.far = bf16[2,8,2,8,512]{4,3,2,1,0:T(8,128)(2,1)S(1)} collective-permute-done((bf16[2,8,2,8,512]{4,3,2,1,0:T(8,128)(2,1)S(1)}, bf16[2,8,2,8,512]{4,3,2,1,0:T(8,128)(2,1)S(1)}, u32[]{:S(2)}, u32[]{:S(2)}) %collective-permute-start.4) | collective-permute-done | bytes 262176 | tf_op jit(solution)/shard_map/ppermute | solution.py:258
  34.8 0.0 collective-permute-start.5
  34.8 0.5 collective-permute-start.6
  35.3 1.0 %collective-permute-done.5.arrived = bf16[2,8,2,8,512]{4,3,2,1,0:T(8,128)(2,1)S(1)} collective-permute-done((bf16[2,8,2,8,512]{4,3,2,1,0:T(8,128)(2,1)S(1)}, bf16[2,8,2,8,512]{4,3,2,1,0:T(8,128)(2,1)S(1)}, u32[]{:S(2)}, u32[]{:S(2)}) %collective-permute-start.5) | collective-permute-done | bytes 262176 | tf_op jit(solution)/shard_map/ppermute | solution.py:273
  36.4 1.6 %collective-permute-start.7 = (bf16[2,8,2,8,512]{4,3,2,1,0:T(8,128)(2,1)S(1)}, bf16[2,8,2,8,512]{4,3,2,1,0:T(8,128)(2,1)S(1)}, u32[]{:S(2)}, u32[]{:S(2)}) collective-permute-start(bf16[2,8,2,8,512]{4,3,2,1,0:T(8,128)(2,1)S(1)} %shard_map.58), channel_id=1, source_target_pairs={{0,16},{8,24},{16,0},{24,8},{1,17},{9,25},{17,1},{25,9},{2,18},{10... | collective-permute-start | bytes 786440 | tf_op jit(solution)/shard_map/ppermute | solution.py:276
  37.9 4.8 %shard_map.59.ours = f32[2,8,2,2,8,512]{5,4,3,2,1,0:T(8,128)S(1)} custom-call(f32[36,2048]{1,0:T(8,128)S(1)} %get-tuple-element.20.factors, bf16[64,2048]{1,0:T(8,128)(2,1)S(1)} %bitcast.10, bf16[64,2048]{1,0:T(8,128)(2,1)S(1)} %collective-permute-done.sib, bf16[64,2048]{1,0:T(8,128)(2,1)S(1)} %collective-permute-done.1.far_own, ...), custom_call_target="tpu_custom_call" | custom-call | flops 268435456 | bytes 1048576 | tf_op jit(solution)/shard_map/pallas_call | solution.py:173
  42.7 2.1 %collective-permute-done.7.near = bf16[2,8,2,8,512]{4,3,2,1,0:T(8,128)(2,1)S(1)} collective-permute-done((bf16[2,8,2,8,512]{4,3,2,1,0:T(8,128)(2,1)S(1)}, bf16[2,8,2,8,512]{4,3,2,1,0:T(8,128)(2,1)S(1)}, u32[]{:S(2)}, u32[]{:S(2)}) %collective-permute-start.7) | collective-permute-done | bytes 262176 | tf_op jit(solution)/shard_map/ppermute | solution.py:276
  44.8 0.0 collective-permute-done.6.arrived
  44.8 0.2 shard_map.60
  45.0 17.3 %all_to_all.11.parts = bf16[8,2,2,8,1024]{4,3,2,1,0:T(8,128)(2,1)S(1)} all-to-all(bf16[8,2,2,8,1024]{4,3,2,1,0:T(8,128)(2,1)S(1)} %shard_map.60), channel_id=1, replica_groups=mesh['ckpt'=4,'tensor'=8] {'tensor'}, dimensions={0} | all-to-all | bytes 1048576 | tf_op jit(solution)/shard_map/all_to_all | solution.py:294
  62.3 0.7 %shard_map.61 = bf16[32,512]{1,0:T(8,128)(2,1)} custom-call(bf16[8,2,2,8,1024]{4,3,2,1,0:T(8,128)(2,1)S(1)} %all_to_all.11.parts), custom_call_target="tpu_custom_call" | custom-call | tf_op jit(solution)/shard_map/pallas_call | solution.py:295
  (2 shorter events, 0.1 us)
Async XLA Ops:
  16.2 2.1 %collective-permute-start = (bf16[64,2048]{1,0:T(8,128)(2,1)S(1)}, bf16[64,2048]{1,0:T(8,128)(2,1)S(1)}, u32[]{:S(2)}, u32[]{:S(2)}) collective-permute-start(bf16[64,2048]{1,0:T(8,128)(2,1)S(1)} %bitcast.6), channel_id=1, source_target_pairs={{0,8},{8,0},{16,24},{24,16},{1,9},{9,1},{17,25},{25,17},{2,10},{10... | collective-permute-start | bytes 786440 | tf_op jit(solution)/shard_map/ppermute | solution.py:222
  16.2 8.7 %collective-permute-start.1 = (bf16[64,2048]{1,0:T(8,128)(2,1)S(1)}, bf16[64,2048]{1,0:T(8,128)(2,1)S(1)}, u32[]{:S(2)}, u32[]{:S(2)}) collective-permute-start(bf16[64,2048]{1,0:T(8,128)(2,1)S(1)} %bitcast.7), channel_id=1, source_target_pairs={{0,16},{8,24},{16,0},{24,8},{1,17},{9,25},{17,1},{25,9},{2,18},{10... | collective-permute-start | bytes 786440 | tf_op jit(solution)/shard_map/ppermute | solution.py:221
  24.3 1.6 %collective-permute-start.2 = (bf16[2,8,2,8,512]{4,3,2,1,0:T(8,128)(2,1)S(1)}, bf16[2,8,2,8,512]{4,3,2,1,0:T(8,128)(2,1)S(1)}, u32[]{:S(2)}, u32[]{:S(2)}) collective-permute-start(bf16[2,8,2,8,512]{4,3,2,1,0:T(8,128)(2,1)S(1)} %get-tuple-element.21), channel_id=1, source_target_pairs={{0,8},{8,0},{16,24},{24,16},{1,9},{9,1},{17,25},{25,17},{2,10},{10... | collective-permute-start | bytes 786440 | tf_op jit(solution)/shard_map/ppermute | solution.py:246
  24.9 1.5 %collective-permute-start.3 = (bf16[64,2048]{1,0:T(8,128)(2,1)S(1)}, bf16[64,2048]{1,0:T(8,128)(2,1)S(1)}, u32[]{:S(2)}, u32[]{:S(2)}) collective-permute-start(bf16[64,2048]{1,0:T(8,128)(2,1)S(1)} %collective-permute-done.1.far_own), channel_id=1, source_target_pairs={{0,8},{8,0},{16,24},{24,16},{1,9},{9,1},{17,25},{25,17},{2,10},{10... | collective-permute-start | bytes 786440 | tf_op jit(solution)/shard_map/ppermute | solution.py:248
  26.5 8.3 %collective-permute-start.4 = (bf16[2,8,2,8,512]{4,3,2,1,0:T(8,128)(2,1)S(1)}, bf16[2,8,2,8,512]{4,3,2,1,0:T(8,128)(2,1)S(1)}, u32[]{:S(2)}, u32[]{:S(2)}) collective-permute-start(bf16[2,8,2,8,512]{4,3,2,1,0:T(8,128)(2,1)S(1)} %shard_map.56), channel_id=1, source_target_pairs={{0,16},{8,24},{16,0},{24,8},{1,17},{9,25},{17,1},{25,9},{2,18},{10... | collective-permute-start | bytes 786440 | tf_op jit(solution)/shard_map/ppermute | solution.py:258
  34.8 1.5 %collective-permute-start.5 = (bf16[2,8,2,8,512]{4,3,2,1,0:T(8,128)(2,1)S(1)}, bf16[2,8,2,8,512]{4,3,2,1,0:T(8,128)(2,1)S(1)}, u32[]{:S(2)}, u32[]{:S(2)}) collective-permute-start(bf16[2,8,2,8,512]{4,3,2,1,0:T(8,128)(2,1)S(1)} %get-tuple-element.30), channel_id=1, source_target_pairs={{0,8},{8,0},{16,24},{24,16},{1,9},{9,1},{17,25},{25,17},{2,10},{10... | collective-permute-start | bytes 786440 | tf_op jit(solution)/shard_map/ppermute | solution.py:273
  34.8 10.0 %collective-permute-start.6 = (bf16[2,8,2,2,8,512]{5,4,3,2,1,0:T(8,128)(2,1)S(1)}, bf16[2,8,2,2,8,512]{5,4,3,2,1,0:T(8,128)(2,1)S(1)}, u32[]{:S(2)}, u32[]{:S(2)}) collective-permute-start(bf16[2,8,2,2,8,512]{5,4,3,2,1,0:T(8,128)(2,1)S(1)} %get-tuple-element.32), channel_id=1, source_target_pairs={{0,8},{8,0},{16,24},{24,16},{1,9},{9,1},{17,25},{25,17},{2,10},{10... | collective-permute-start | bytes 1572872 | tf_op jit(solution)/shard_map/ppermute | solution.py:274
  36.4 8.4 %collective-permute-start.7 = (bf16[2,8,2,8,512]{4,3,2,1,0:T(8,128)(2,1)S(1)}, bf16[2,8,2,8,512]{4,3,2,1,0:T(8,128)(2,1)S(1)}, u32[]{:S(2)}, u32[]{:S(2)}) collective-permute-start(bf16[2,8,2,8,512]{4,3,2,1,0:T(8,128)(2,1)S(1)} %shard_map.58), channel_id=1, source_target_pairs={{0,16},{8,24},{16,0},{24,8},{1,17},{9,25},{17,1},{25,9},{2,18},{10... | collective-permute-start | bytes 786440 | tf_op jit(solution)/shard_map/ppermute | solution.py:276

commit v7 on v6

--- a/solution.py
+++ b/solution.py
@@ -104,7 +104,7 @@
 
 
 def early_kernel(
-    scale_num, mask_hbm, own, sib, delta, theirs, ours, kept, factors, held, mask, sems, mask_sem
+    scale_num, mask_hbm, own, sib, delta, theirs, kept, factors, held, mask, sems, mask_sem
 ):
     chip, core = chip_and_core()
     mask_copy = pltpu.make_async_copy(mask_hbm, mask, mask_sem)
@@ -115,13 +115,24 @@
     mask_copy.wait()
     expand(mask[...], scale_num[0].astype(jnp.float32) / DEN, factors)
 
-    @pl.loop(0, 4)
+    @pl.loop(0, 2)
     def _(part):
         rows.wait(part)
         first = first_factor(kept, factors, part, rows.owner(part))
-        total = product(held[...], factors, kept.at[part], first)
-        pl.when(part < 2)(lambda: put(theirs.at[part % 2], total, core))
-        pl.when(part >= 2)(lambda: put(ours.at[part % 2], total, core))
+        put(theirs.at[part], product(held[...], factors, kept.at[part], first), core)
+
+    for part in (2, 3):
+        rows.wait(part)
+
+
+def early_rest_kernel(factors, own, sib, kept, ours, held):
+    chip, core = chip_and_core()
+    gather_held(held, (own, sib))
+
+    @pl.loop(0, 2)
+    def _(part):
+        first = first_factor(kept, factors, part, (1 - chip) * CORES + core)
+        put(ours.at[part], product(held[...], factors, kept.at[2 + part], first), core)
 
 
 def later_kernel(
@@ -181,7 +192,13 @@
     )(*operands)
 
 
-def join_kernel(ours, arrived, out):
+def meet_kernel(arrived, out):
+    first = (0,) * (len(arrived.shape) - 2)
+    out[...] = arrived[first + (slice(0, out.shape[0]), slice(0, out.shape[1]))]
+
+
+def join_kernel(ours, arrived, *rest):
+    out = rest[-1]
     out[...] = (ours[...] + arrived[...].astype(jnp.float32)).astype(out.dtype)
 
 
@@ -229,9 +246,9 @@
     weights = (4, slab_own, width)
     size = 4 * slab_own * width
     blocks = mask.shape[0] * mask.shape[1] + slab_own // BLOCK
-    theirs, ours, kept, factors = call(
+    theirs, kept, factors = call(
         early_kernel,
-        [part(pair, bf16), part(pair, f32), part(weights, bf16), part((blocks, width), f32)],
+        [part(pair, bf16), part(weights, bf16), part((blocks, width), f32)],
         [
             pltpu.VMEM((half, width), bf16),
             pltpu.VMEM(mask.shape, mask.dtype),
@@ -240,12 +257,19 @@
         ],
         [SMEM, HBM, VMEM, VMEM, HBM],
         (scale_num, mask, own, sib, delta),
-        2 * half * size,
+        half * size,
         2 * size,
     )
     near = core_swap(theirs)
-    far_own, theirs = lax.optimization_barrier((far_own, theirs))
-    far_sib = core_swap(far_own)
+    (ours,) = call(
+        early_rest_kernel,
+        [part(pair, f32)],
+        [pltpu.VMEM((half, width), bf16)],
+        [VMEM] * 4,
+        (factors, own, sib, kept),
+        8,
+        8,
+    )
     simple = lambda kernel, shape, *xs: pl.pallas_call(
         kernel,
         out_shape=part(shape, bf16),
@@ -254,8 +278,10 @@
         compiler_params=pltpu.CompilerParams(vmem_limit_bytes=16 * MIB),
         cost_estimate=pl.CostEstimate(flops=xs[0].size, bytes_accessed=8 * xs[0].size, transcendentals=0),
     )(*xs)
-    first, far_sib = lax.optimization_barrier((simple(join_kernel, pair, ours, near), far_sib))
-    over_first = chip_swap(first)
+    far_own, ours = lax.optimization_barrier((far_own, ours))
+    met = simple(meet_kernel, (rows, BLOCK), far_own)
+    over_first = chip_swap(simple(join_kernel, pair, ours, near, met))
+    far_sib = core_swap(far_own)
     theirs, ours, theirs_home = call(
         later_kernel,
         [part(pair, bf16), part(pair, f32), part(four, bf16)],
@@ -269,8 +295,8 @@
         4 * half * size,
         2 * size,
     )
-    theirs, theirs_home, over_first = lax.optimization_barrier((theirs, theirs_home, over_first))
-    second = simple(join_kernel, pair, ours, core_swap(theirs))
+    met = simple(meet_kernel, (rows, BLOCK), over_first)
+    second = simple(join_kernel, pair, ours, core_swap(theirs), met)
     near_home = core_swap(theirs_home)
     second, own = lax.optimization_barrier((second, own))
     over_second = chip_swap(second)

time: 63.3 us -> 59.8 us (0.945)
  waiting for transfers between devices: 6.65 us -> 4.31 us
  Pallas kernels: 16.7 us -> 16 us
    ppermute x2, waiting for transfers between devices: 2.85 us -> 1.61 us  [the longest x1 1.6 us: local_pair(): over_first = chip_swap(simple(join_kernel, pair, ours, near, met))]
    ppermute x1, waiting for transfers between devices: 1.02 us -> 0.01 us  [local_pair(): near = core_swap(theirs)]
    ppermute x1, waiting for transfers between devices: 0.24 us -> 1.04 us  [local_pair(): far_own = chip_swap(own)]
    pallas_call x3 -> x4, Pallas kernels: 15.8 us -> 15 us  [call(): pl.pallas_call(kernel, out_shape=outs, in_specs=in_specs, out_specs=[VMEM...]
  transfers between devices with their start and end apart: 8 -> 8, of which waited for: 6 -> 3; matrix products, arithmetic and copies ran while one was open for 0% -> 0% of each run, Pallas kernels for 25% -> 25%
where the time goes in v7:
time: 59.8 us; the launch traced here: 59.6 us
  blocking collectives  33.1 us (55%)
  Pallas kernels  16 us (27%)
  starting transfers between devices  5.48 us (9%)
  waiting for transfers between devices  4.31 us (7%)
  between operations  0.72 us (1%)
    all_to_all x1, blocking collectives, local_pair(): parts = lax.all_to_all(whole, 'tensor', 0, 0, tiled=True)  16.9 us
    all_to_all x1, blocking collectives, local_pair(): lax.all_to_all(cut, 'tensor', 0, 0, tiled=True)  16.2 us
    pallas_call x4, Pallas kernels, call(): pl.pallas_call(kernel, out_shape=outs, in_specs=in_specs, out_specs=[VMEM...  15 us
    ppermute x1, waiting for transfers between devices, local_pair(): over_second = chip_swap(second)  1.65 us
    ppermute x1, waiting for transfers between devices, local_pair(): over_first = chip_swap(simple(join_kernel, pair, ours, near, met))  1.6 us
    ppermute x1, starting transfers between devices, local_pair(): over_first = chip_swap(simple(join_kernel, pair, ours, near, met))  1.56 us
    ppermute x1, starting transfers between devices, local_pair(): over_second = chip_swap(second)  1.56 us
    ppermute x1, starting transfers between devices, local_pair(): far_own = chip_swap(own)  1.49 us
  transfers between devices with their start and end apart: 8, of which 3 were waited for; matrix products, arithmetic and copies ran while one was open for 0% of the time, Pallas kernels for 25%

profile of v7, /device:TPU:0, one launch (start us, length us, event | category | flops | bytes accessed | tf_op | source)
XLA Modules:
  0.0 59.6 jit_solution(2685108991931679262)
XLA Ops:
  0.0 16.2 %all_to_all.10 = bf16[8,8,2048]{2,1,0:T(8,128)(2,1)S(1)} all-to-all(bf16[8,8,2048]{2,1,0:T(8,128)(2,1)} %bitcast.15), channel_id=1, replica_groups=mesh['ckpt'=4,'tensor'=8] {'tensor'}, dimensions={0} | all-to-all | bytes 524288 | tf_op jit(solution)/shard_map/all_to_all | solution.py:237
  16.2 0.0 collective-permute-start
  16.2 1.5 %collective-permute-start.1 = (bf16[64,2048]{1,0:T(8,128)(2,1)S(1)}, bf16[64,2048]{1,0:T(8,128)(2,1)S(1)}, u32[]{:S(2)}, u32[]{:S(2)}) collective-permute-start(bf16[64,2048]{1,0:T(8,128)(2,1)S(1)} %bitcast.7), channel_id=1, source_target_pairs={{0,16},{8,24},{16,0},{24,8},{1,17},{9,25},{17,1},{25,9},{2,18},{10... | collective-permute-start | bytes 786440 | tf_op jit(solution)/shard_map/ppermute | solution.py:238
  18.3 0.0 collective-permute-done.sib
  18.4 3.5 %shard_map.55 = (bf16[2,8,2,8,512]{4,3,2,1,0:T(8,128)(2,1)S(1)}, bf16[4,512,2048]{2,1,0:T(8,128)(2,1)S(1)}, f32[36,2048]{1,0:T(8,128)S(1)}) custom-call(s32[1]{0:T(128)S(6)} %copy.6.scale_num, s32[2,16,16]{2,1,0:T(8,128)} %bitcast.16, bf16[64,2048]{1,0:T(8,128)(2,1)S(1)} %bitcast.8, bf16[64,2048]{1,0:T(8,128)(2,1)S(1)} %collective-permute-done.sib, ...), custom_call_target="tpu_custom_call" | custom-call | flops 67108864 | bytes 1048576 | tf_op jit(solution)/shard_map/pallas_call | solution.py:184
  21.9 0.3 collective-permute-start.4
  22.2 1.7 %shard_map.56.ours = f32[2,8,2,8,512]{4,3,2,1,0:T(8,128)S(1)} custom-call(f32[36,2048]{1,0:T(8,128)S(1)} %get-tuple-element.15.factors, bf16[64,2048]{1,0:T(8,128)(2,1)S(1)} %bitcast.9, bf16[64,2048]{1,0:T(8,128)(2,1)S(1)} %collective-permute-done.sib, bf16[4,512,2048]{2,1,0:T(8,128)(2,1)S(1)} %get-tuple-element.16.kept), custom_call_target="tpu_custom_call" | custom-call | flops 1 | bytes 1 | tf_op jit(solution)/shard_map/pallas_call | solution.py:184
  23.9 1.0 %collective-permute-done.1.far_own.arrived = bf16[64,2048]{1,0:T(8,128)(2,1)S(1)} collective-permute-done((bf16[64,2048]{1,0:T(8,128)(2,1)S(1)}, bf16[64,2048]{1,0:T(8,128)(2,1)S(1)}, u32[]{:S(2)}, u32[]{:S(2)}) %collective-permute-start.1) | collective-permute-done | bytes 262176 | tf_op jit(solution)/shard_map/ppermute | solution.py:238
  24.9 0.0 collective-permute-start.2
  24.9 0.0 collective-permute-done.4.arrived
  25.0 1.6 %collective-permute-start.5 = (bf16[2,8,2,8,512]{4,3,2,1,0:T(8,128)(2,1)S(1)}, bf16[2,8,2,8,512]{4,3,2,1,0:T(8,128)(2,1)S(1)}, u32[]{:S(2)}, u32[]{:S(2)}) collective-permute-start(bf16[2,8,2,8,512]{4,3,2,1,0:T(8,128)(2,1)S(1)} %shard_map.59), channel_id=1, source_target_pairs={{0,16},{8,24},{16,0},{24,8},{1,17},{9,25},{17,1},{25,9},{2,18},{10... | collective-permute-start | bytes 786440 | tf_op jit(solution)/shard_map/ppermute | solution.py:283
  26.5 0.0 collective-permute-done.2.far_sib
  26.5 5.0 %shard_map.57 = (bf16[2,8,2,8,512]{4,3,2,1,0:T(8,128)(2,1)S(1)}, f32[2,8,2,8,512]{4,3,2,1,0:T(8,128)S(1)}, bf16[2,8,2,2,8,512]{5,4,3,2,1,0:T(8,128)(2,1)S(1)}) custom-call(f32[36,2048]{1,0:T(8,128)S(1)} %get-tuple-element.15.factors, bf16[64,2048]{1,0:T(8,128)(2,1)S(1)} %bitcast.10, bf16[64,2048]{1,0:T(8,128)(2,1)S(1)} %collective-permute-done.sib, ...), custom_call_target="tpu_custom_call" | custom-call | flops 268435456 | bytes 1048576 | tf_op jit(solution)/shard_map/pallas_call | solution.py:184
  31.6 0.3 collective-permute-start.3
  31.9 0.3 collective-permute-start.6
  32.2 1.6 %collective-permute-done.5.arrived.far = bf16[2,8,2,8,512]{4,3,2,1,0:T(8,128)(2,1)S(1)} collective-permute-done((bf16[2,8,2,8,512]{4,3,2,1,0:T(8,128)(2,1)S(1)}, bf16[2,8,2,8,512]{4,3,2,1,0:T(8,128)(2,1)S(1)}, u32[]{:S(2)}, u32[]{:S(2)}) %collective-permute-start.5) | collective-permute-done | bytes 262176 | tf_op jit(solution)/shard_map/ppermute | solution.py:283
  33.8 0.0 collective-permute-done.3.arrived
  33.8 1.6 %collective-permute-start.7 = (bf16[2,8,2,8,512]{4,3,2,1,0:T(8,128)(2,1)S(1)}, bf16[2,8,2,8,512]{4,3,2,1,0:T(8,128)(2,1)S(1)}, u32[]{:S(2)}, u32[]{:S(2)}) collective-permute-start(bf16[2,8,2,8,512]{4,3,2,1,0:T(8,128)(2,1)S(1)} %shard_map.61), channel_id=1, source_target_pairs={{0,16},{8,24},{16,0},{24,8},{1,17},{9,25},{17,1},{25,9},{2,18},{10... | collective-permute-start | bytes 786440 | tf_op jit(solution)/shard_map/ppermute | solution.py:302
  35.4 4.8 %shard_map.62.ours = f32[2,8,2,2,8,512]{5,4,3,2,1,0:T(8,128)S(1)} custom-call(f32[36,2048]{1,0:T(8,128)S(1)} %get-tuple-element.15.factors, bf16[64,2048]{1,0:T(8,128)(2,1)S(1)} %bitcast.11, bf16[64,2048]{1,0:T(8,128)(2,1)S(1)} %collective-permute-done.sib, bf16[64,2048]{1,0:T(8,128)(2,1)S(1)} %collective-permute-done.1.far_own.arrived, ...), custom_call_target="tpu_custom_call" | custom-call | flops 268435456 | bytes 1048576 | tf_op jit(solution)/shard_map/pallas_call | solution.py:184
  40.2 1.7 %collective-permute-done.7.near = bf16[2,8,2,8,512]{4,3,2,1,0:T(8,128)(2,1)S(1)} collective-permute-done((bf16[2,8,2,8,512]{4,3,2,1,0:T(8,128)(2,1)S(1)}, bf16[2,8,2,8,512]{4,3,2,1,0:T(8,128)(2,1)S(1)}, u32[]{:S(2)}, u32[]{:S(2)}) %collective-permute-start.7) | collective-permute-done | bytes 262176 | tf_op jit(solution)/shard_map/ppermute | solution.py:302
  41.8 0.0 collective-permute-done.6.arrived
  41.8 0.2 shard_map.63
  42.0 16.9 %all_to_all.11.parts = bf16[8,2,2,8,1024]{4,3,2,1,0:T(8,128)(2,1)S(1)} all-to-all(bf16[8,2,2,8,1024]{4,3,2,1,0:T(8,128)(2,1)S(1)} %shard_map.63), channel_id=1, replica_groups=mesh['ckpt'=4,'tensor'=8] {'tensor'}, dimensions={0} | all-to-all | bytes 1048576 | tf_op jit(solution)/shard_map/all_to_all | solution.py:320
  58.8 0.7 %shard_map.64 = bf16[32,512]{1,0:T(8,128)(2,1)} custom-call(bf16[8,2,2,8,1024]{4,3,2,1,0:T(8,128)(2,1)S(1)} %all_to_all.11.parts), custom_call_target="tpu_custom_call" | custom-call | tf_op jit(solution)/shard_map/pallas_call | solution.py:321
  (4 shorter events, 0.1 us)
Async XLA Ops:
  16.2 2.1 %collective-permute-start = (bf16[64,2048]{1,0:T(8,128)(2,1)S(1)}, bf16[64,2048]{1,0:T(8,128)(2,1)S(1)}, u32[]{:S(2)}, u32[]{:S(2)}) collective-permute-start(bf16[64,2048]{1,0:T(8,128)(2,1)S(1)} %bitcast.6), channel_id=1, source_target_pairs={{0,8},{8,0},{16,24},{24,16},{1,9},{9,1},{17,25},{25,17},{2,10},{10... | collective-permute-start | bytes 786440 | tf_op jit(solution)/shard_map/ppermute | solution.py:239
  16.2 8.7 %collective-permute-start.1 = (bf16[64,2048]{1,0:T(8,128)(2,1)S(1)}, bf16[64,2048]{1,0:T(8,128)(2,1)S(1)}, u32[]{:S(2)}, u32[]{:S(2)}) collective-permute-start(bf16[64,2048]{1,0:T(8,128)(2,1)S(1)} %bitcast.7), channel_id=1, source_target_pairs={{0,16},{8,24},{16,0},{24,8},{1,17},{9,25},{17,1},{25,9},{2,18},{10... | collective-permute-start | bytes 786440 | tf_op jit(solution)/shard_map/ppermute | solution.py:238
  21.9 3.1 %collective-permute-start.4 = (bf16[2,8,2,8,512]{4,3,2,1,0:T(8,128)(2,1)S(1)}, bf16[2,8,2,8,512]{4,3,2,1,0:T(8,128)(2,1)S(1)}, u32[]{:S(2)}, u32[]{:S(2)}) collective-permute-start(bf16[2,8,2,8,512]{4,3,2,1,0:T(8,128)(2,1)S(1)} %get-tuple-element.21), channel_id=1, source_target_pairs={{0,8},{8,0},{16,24},{24,16},{1,9},{9,1},{17,25},{25,17},{2,10},{10... | collective-permute-start | bytes 786440 | tf_op jit(solution)/shard_map/ppermute | solution.py:263
  24.9 1.6 %collective-permute-start.2 = (bf16[64,2048]{1,0:T(8,128)(2,1)S(1)}, bf16[64,2048]{1,0:T(8,128)(2,1)S(1)}, u32[]{:S(2)}, u32[]{:S(2)}) collective-permute-start(bf16[64,2048]{1,0:T(8,128)(2,1)S(1)} %collective-permute-done.1.far_own.arrived), channel_id=1, source_target_pairs={{0,8},{8,0},{16,24},{24,16},{1,9},{9,1},{17,25},{25,17},{2,10},{10... | collective-permute-start | bytes 786440 | tf_op jit(solution)/shard_map/ppermute | solution.py:284
  25.0 8.8 %collective-permute-start.5 = (bf16[2,8,2,8,512]{4,3,2,1,0:T(8,128)(2,1)S(1)}, bf16[2,8,2,8,512]{4,3,2,1,0:T(8,128)(2,1)S(1)}, u32[]{:S(2)}, u32[]{:S(2)}) collective-permute-start(bf16[2,8,2,8,512]{4,3,2,1,0:T(8,128)(2,1)S(1)} %shard_map.59), channel_id=1, source_target_pairs={{0,16},{8,24},{16,0},{24,8},{1,17},{9,25},{17,1},{25,9},{2,18},{10... | collective-permute-start | bytes 786440 | tf_op jit(solution)/shard_map/ppermute | solution.py:283
  31.6 2.2 %collective-permute-start.3 = (bf16[2,8,2,8,512]{4,3,2,1,0:T(8,128)(2,1)S(1)}, bf16[2,8,2,8,512]{4,3,2,1,0:T(8,128)(2,1)S(1)}, u32[]{:S(2)}, u32[]{:S(2)}) collective-permute-start(bf16[2,8,2,8,512]{4,3,2,1,0:T(8,128)(2,1)S(1)} %get-tuple-element.19), channel_id=1, source_target_pairs={{0,8},{8,0},{16,24},{24,16},{1,9},{9,1},{17,25},{25,17},{2,10},{10... | collective-permute-start | bytes 786440 | tf_op jit(solution)/shard_map/ppermute | solution.py:299
  31.9 9.9 %collective-permute-start.6 = (bf16[2,8,2,2,8,512]{5,4,3,2,1,0:T(8,128)(2,1)S(1)}, bf16[2,8,2,2,8,512]{5,4,3,2,1,0:T(8,128)(2,1)S(1)}, u32[]{:S(2)}, u32[]{:S(2)}) collective-permute-start(bf16[2,8,2,2,8,512]{5,4,3,2,1,0:T(8,128)(2,1)S(1)} %get-tuple-element.23), channel_id=1, source_target_pairs={{0,8},{8,0},{16,24},{24,16},{1,9},{9,1},{17,25},{25,17},{2,10},{10... | collective-permute-start | bytes 1572872 | tf_op jit(solution)/shard_map/ppermute | solution.py:300
  33.8 8.0 %collective-permute-start.7 = (bf16[2,8,2,8,512]{4,3,2,1,0:T(8,128)(2,1)S(1)}, bf16[2,8,2,8,512]{4,3,2,1,0:T(8,128)(2,1)S(1)}, u32[]{:S(2)}, u32[]{:S(2)}) collective-permute-start(bf16[2,8,2,8,512]{4,3,2,1,0:T(8,128)(2,1)S(1)} %shard_map.61), channel_id=1, source_target_pairs={{0,16},{8,24},{16,0},{24,8},{1,17},{9,25},{17,1},{25,9},{2,18},{10... | collective-permute-start | bytes 786440 | tf_op jit(solution)/shard_map/ppermute | solution.py:302

commit v8 on v7

--- a/solution.py
+++ b/solution.py
@@ -104,7 +104,7 @@
 
 
 def early_kernel(
-    scale_num, mask_hbm, own, sib, delta, theirs, kept, factors, held, mask, sems, mask_sem
+    scale_num, mask_hbm, own, sib, delta, gate, up, kept, factors, held, mask, sems, mask_sem
 ):
     chip, core = chip_and_core()
     mask_copy = pltpu.make_async_copy(mask_hbm, mask, mask_sem)
@@ -119,7 +119,9 @@
     def _(part):
         rows.wait(part)
         first = first_factor(kept, factors, part, rows.owner(part))
-        put(theirs.at[part], product(held[...], factors, kept.at[part], first), core)
+        total = product(held[...], factors, kept.at[part], first)
+        pl.when(part == 0)(lambda: put(gate, total, core))
+        pl.when(part == 1)(lambda: put(up, total, core))
 
     for part in (2, 3):
         rows.wait(part)
@@ -135,28 +137,30 @@
         put(ours.at[part], product(held[...], factors, kept.at[2 + part], first), core)
 
 
-def later_kernel(
-    factors, own, sib, far_own, far_sib, kept, delta, theirs, ours, theirs_home, home, held, sems
-):
+def later_kernel(factors, far_own, far_sib, kept, after, theirs, ours, held):
     chip, core = chip_and_core()
-    half = held.shape[0] // 2
+    gather_held(held, (far_own, far_sib))
+    far = Rows(None, kept, None, [(1 - chip) * CORES + at for at in (1 - core, core)])
+
+    @pl.loop(0, 4)
+    def _(part):
+        first = first_factor(kept, factors, part, far.owner(part))
+        total = product(held[...], factors, kept.at[part], first)
+        pl.when(part < 2)(lambda: put(theirs.at[part % 2], total, core))
+        pl.when(part >= 2)(lambda: put(ours.at[part % 2], total, core))
+
+
+def home_sib_kernel(factors, own, sib, far_own, far_sib, delta, theirs, home, held, sems):
+    chip, core = chip_and_core()
     rows = Rows(delta, home, sems, [chip * CORES + 1 - core])
     rows.start()
     gather_held(held, (own, sib, far_own, far_sib))
-    far = Rows(None, kept, None, [(1 - chip) * CORES + at for at in (1 - core, core)])
-
-    @pl.loop(0, 4)
-    def _(part):
-        first = first_factor(kept, factors, part, far.owner(part))
-        total = product(held[half:], factors, kept.at[part], first)
-        pl.when(part < 2)(lambda: put(theirs.at[part % 2], total, core))
-        pl.when(part >= 2)(lambda: put(ours.at[part % 2], total, core))
 
     @pl.loop(0, 2)
     def _(part):
         rows.wait(part)
         first = first_factor(home, factors, part, rows.owner(part))
-        put(theirs_home.at[part], product(held[...], factors, home.at[part], first), core)
+        put(theirs.at[part], product(held[...], factors, home.at[part], first), core)
 
 
 def home_kernel(factors, own, sib, far_own, far_sib, delta, base, ours, kept, held, total, sems):
@@ -195,6 +199,11 @@
 def meet_kernel(arrived, out):
     first = (0,) * (len(arrived.shape) - 2)
     out[...] = arrived[first + (slice(0, out.shape[0]), slice(0, out.shape[1]))]
+
+
+def join_halves_kernel(ours, gate, up, out):
+    for m, arrived in enumerate((gate, up)):
+        out[m] = (ours[m] + arrived[...].astype(jnp.float32)).astype(out.dtype)
 
 
 def join_kernel(ours, arrived, *rest):
@@ -246,9 +255,9 @@
     weights = (4, slab_own, width)
     size = 4 * slab_own * width
     blocks = mask.shape[0] * mask.shape[1] + slab_own // BLOCK
-    theirs, kept, factors = call(
+    gate, up, kept, factors = call(
         early_kernel,
-        [part(pair, bf16), part(weights, bf16), part((blocks, width), f32)],
+        [part(pair[1:], bf16), part(pair[1:], bf16), part(weights, bf16), part((blocks, width), f32)],
         [
             pltpu.VMEM((half, width), bf16),
             pltpu.VMEM(mask.shape, mask.dtype),
@@ -260,7 +269,7 @@
         half * size,
         2 * size,
     )
-    near = core_swap(theirs)
+    near = [core_swap(gate), core_swap(up)]
     (ours,) = call(
         early_rest_kernel,
         [part(pair, f32)],
@@ -278,25 +287,36 @@
         compiler_params=pltpu.CompilerParams(vmem_limit_bytes=16 * MIB),
         cost_estimate=pl.CostEstimate(flops=xs[0].size, bytes_accessed=8 * xs[0].size, transcendentals=0),
     )(*xs)
-    far_own, ours = lax.optimization_barrier((far_own, ours))
-    met = simple(meet_kernel, (rows, BLOCK), far_own)
-    over_first = chip_swap(simple(join_kernel, pair, ours, near, met))
+    first = simple(join_halves_kernel, pair, ours, *near)
+    over_first = chip_swap(first)
+    far_own, first = lax.optimization_barrier((far_own, first))
     far_sib = core_swap(far_own)
-    theirs, ours, theirs_home = call(
+    theirs, ours = call(
         later_kernel,
-        [part(pair, bf16), part(pair, f32), part(four, bf16)],
+        [part(pair, bf16), part(pair, f32)],
+        [pltpu.VMEM((half, width), bf16)],
+        [VMEM] * 4 + [pl.BlockSpec(memory_space=pl.ANY)],
+        (factors, far_own, far_sib, kept, first),
+        2 * half * size,
+        2 * size,
+    )
+    near = core_swap(theirs)
+    (theirs_home,) = call(
+        home_sib_kernel,
+        [part(four, bf16)],
         [
             pltpu.VMEM((2, slab_own, width), bf16),
             pltpu.VMEM((2 * half, width), bf16),
             pltpu.SemaphoreType.DMA((2, chunks)),
         ],
-        [VMEM] * 6 + [HBM],
-        (factors, own, sib, far_own, far_sib, kept, delta),
-        4 * half * size,
-        2 * size,
+        [VMEM] * 5 + [HBM],
+        (factors, own, sib, far_own, far_sib, delta),
+        size,
+        size,
     )
     met = simple(meet_kernel, (rows, BLOCK), over_first)
-    second = simple(join_kernel, pair, ours, core_swap(theirs), met)
+    ours, theirs_home = lax.optimization_barrier((ours, theirs_home))
+    second = simple(join_kernel, pair, ours, near, met)
     near_home = core_swap(theirs_home)
     second, own = lax.optimization_barrier((second, own))
     over_second = chip_swap(second)

time: 59.8 us -> 61 us (1.020)
  Pallas kernels: 16 us -> 18.3 us
  waiting for transfers between devices: 4.31 us -> 2.54 us
    pallas_call x4 -> x5, Pallas kernels: 15 us -> 17.3 us  [call(): pl.pallas_call(kernel, out_shape=outs, in_specs=in_specs, out_specs=[VMEM...]
    ppermute x2 -> x3, waiting for transfers between devices: 1.61 us -> 0.01 us  [the longest x2 0.01 us: local_pair(): near = [core_swap(gate), core_swap(up)]]
    ppermute x1, waiting for transfers between devices: 1.04 us -> 0.01 us  [local_pair(): far_own = chip_swap(own)]
    ppermute x1, waiting for transfers between devices: 1.65 us -> 2.34 us  [local_pair(): over_second = chip_swap(second)]
    all_to_all x1, blocking collectives: 16.9 us -> 17.5 us  [local_pair(): parts = lax.all_to_all(whole, 'tensor', 0, 0, tiled=True)]
    ppermute x2 -> x3, starting transfers between devices: 1.84 us -> 1.67 us  [the longest x1 1.09 us: local_pair(): over_first = chip_swap(first)]
  transfers between devices with their start and end apart: 8 -> 9, of which waited for: 3 -> 2; matrix products, arithmetic and copies ran while one was open for 0% -> 0% of each run, Pallas kernels for 25% -> 29%
where the time goes in v8:
time: 61 us; the launch traced here: 60.8 us
  blocking collectives  33.7 us (55%)
  Pallas kernels  18.3 us (30%)
  starting transfers between devices  5.53 us (9%)
  waiting for transfers between devices  2.54 us (4%)
  between operations  0.75 us (1%)
    all_to_all x1, blocking collectives, local_pair(): parts = lax.all_to_all(whole, 'tensor', 0, 0, tiled=True)  17.5 us
    pallas_call x5, Pallas kernels, call(): pl.pallas_call(kernel, out_shape=outs, in_specs=in_specs, out_specs=[VMEM...  17.3 us
    all_to_all x1, blocking collectives, local_pair(): lax.all_to_all(cut, 'tensor', 0, 0, tiled=True)  16.2 us
    ppermute x1, waiting for transfers between devices, local_pair(): over_second = chip_swap(second)  2.34 us
    ppermute x1, starting transfers between devices, local_pair(): far_own = chip_swap(own)  1.49 us
    ppermute x1, starting transfers between devices, local_pair(): over_second = chip_swap(second)  1.41 us
  transfers between devices with their start and end apart: 9, of which 2 were waited for; matrix products, arithmetic and copies ran while one was open for 0% of the time, Pallas kernels for 29%

profile of v8, /device:TPU:0, one launch (start us, length us, event | category | flops | bytes accessed | tf_op | source)
XLA Modules:
  0.0 60.8 jit_solution(4437531396139133260)
XLA Ops:
  0.0 16.2 %all_to_all.10 = bf16[8,8,2048]{2,1,0:T(8,128)(2,1)S(1)} all-to-all(bf16[8,8,2048]{2,1,0:T(8,128)(2,1)} %bitcast.15), channel_id=1, replica_groups=mesh['ckpt'=4,'tensor'=8] {'tensor'}, dimensions={0} | all-to-all | bytes 524288 | tf_op jit(solution)/shard_map/all_to_all | solution.py:246
  16.2 0.0 collective-permute-start
  16.2 1.5 %collective-permute-start.1 = (bf16[64,2048]{1,0:T(8,128)(2,1)S(1)}, bf16[64,2048]{1,0:T(8,128)(2,1)S(1)}, u32[]{:S(2)}, u32[]{:S(2)}) collective-permute-start(bf16[64,2048]{1,0:T(8,128)(2,1)S(1)} %bitcast.7), channel_id=1, source_target_pairs={{0,16},{8,24},{16,0},{24,8},{1,17},{9,25},{17,1},{25,9},{2,18},{10... | collective-permute-start | bytes 786440 | tf_op jit(solution)/shard_map/ppermute | solution.py:247
  18.3 0.0 collective-permute-done.sib
  18.4 4.3 %shard_map.55 = (bf16[8,2,8,512]{3,2,1,0:T(8,128)(2,1)S(1)}, bf16[8,2,8,512]{3,2,1,0:T(8,128)(2,1)S(1)}, bf16[4,512,2048]{2,1,0:T(8,128)(2,1)S(1)}, f32[36,2048]{1,0:T(8,128)S(1)}) custom-call(s32[1]{0:T(128)S(6)} %copy.6.scale_num, s32[2,16,16]{2,1,0:T(8,128)} %bitcast.16, bf16[64,2048]{1,0:T(8,128)(2,1)S(1)} %bitcast.8, ...), custom_call_target="tpu_custom_call" | custom-call | flops 67108864 | bytes 1048576 | tf_op jit(solution)/shard_map/pallas_call | solution.py:188
  22.6 0.3 collective-permute-start.2
  22.9 0.3 collective-permute-start.3
  23.2 1.7 %shard_map.56.ours = f32[2,8,2,8,512]{4,3,2,1,0:T(8,128)S(1)} custom-call(f32[36,2048]{1,0:T(8,128)S(1)} %get-tuple-element.17.factors, bf16[64,2048]{1,0:T(8,128)(2,1)S(1)} %bitcast.9, bf16[64,2048]{1,0:T(8,128)(2,1)S(1)} %collective-permute-done.sib, bf16[4,512,2048]{2,1,0:T(8,128)(2,1)S(1)} %get-tuple-element.18.kept), custom_call_target="tpu_custom_call" | custom-call | flops 1 | bytes 1 | tf_op jit(solution)/shard_map/pallas_call | solution.py:188
  24.9 0.0 collective-permute-done.2.gate
  24.9 0.0 collective-permute-done.3.up
  25.0 0.0 collective-permute-done.1.far_own
  25.0 0.3 collective-permute-start.4
  25.3 1.1 %collective-permute-start.6 = (bf16[2,8,2,8,512]{4,3,2,1,0:T(8,128)(2,1)S(1)}, bf16[2,8,2,8,512]{4,3,2,1,0:T(8,128)(2,1)S(1)}, u32[]{:S(2)}, u32[]{:S(2)}) collective-permute-start(bf16[2,8,2,8,512]{4,3,2,1,0:T(8,128)(2,1)S(1)} %shard_map.57.after), channel_id=1, source_target_pairs={{0,16},{8,24},{16,0},{24,8},{1,17},{9,25},{17,1},{25,9},{2,18},{10... | collective-permute-start | bytes 786440 | tf_op jit(solution)/shard_map/ppermute | solution.py:291
  26.4 0.2 collective-permute-done.4.far_sib
  26.6 3.4 %shard_map.58 = (bf16[2,8,2,8,512]{4,3,2,1,0:T(8,128)(2,1)S(1)}, f32[2,8,2,8,512]{4,3,2,1,0:T(8,128)S(1)}) custom-call(f32[36,2048]{1,0:T(8,128)S(1)} %get-tuple-element.17.factors, bf16[64,2048]{1,0:T(8,128)(2,1)S(1)} %collective-permute-done.1.far_own, bf16[64,2048]{1,0:T(8,128)(2,1)S(1)} %collective-permute-done.4.far_sib, ...), custom_call_target="tpu_custom_call" | custom-call | flops 134217728 | bytes 1048576 | tf_op jit(solution)/shard_map/pallas_call | solution.py:188
  30.1 0.3 collective-permute-start.5
  30.4 3.1 %shard_map.59 = bf16[2,8,2,2,8,512]{5,4,3,2,1,0:T(8,128)(2,1)S(1)} custom-call(f32[36,2048]{1,0:T(8,128)S(1)} %get-tuple-element.17.factors, bf16[64,2048]{1,0:T(8,128)(2,1)S(1)} %bitcast.10, bf16[64,2048]{1,0:T(8,128)(2,1)S(1)} %collective-permute-done.sib, bf16[64,2048]{1,0:T(8,128)(2,1)S(1)} %collective-permute-done.1.far_own, ...), custom_call_target="tpu_custom_call" | custom-call | flops 524288 | bytes 524288 | tf_op jit(solution)/shard_map/pallas_call | solution.py:188
  33.5 0.3 collective-permute-start.7
  33.8 0.0 collective-permute-done.6.arrived.far
  33.8 0.0 collective-permute-done.5.arrived
  33.9 1.4 %collective-permute-start.8 = (bf16[2,8,2,8,512]{4,3,2,1,0:T(8,128)(2,1)S(1)}, bf16[2,8,2,8,512]{4,3,2,1,0:T(8,128)(2,1)S(1)}, u32[]{:S(2)}, u32[]{:S(2)}) collective-permute-start(bf16[2,8,2,8,512]{4,3,2,1,0:T(8,128)(2,1)S(1)} %shard_map.61), channel_id=1, source_target_pairs={{0,16},{8,24},{16,0},{24,8},{1,17},{9,25},{17,1},{25,9},{2,18},{10... | collective-permute-start | bytes 786440 | tf_op jit(solution)/shard_map/ppermute | solution.py:322
  35.3 4.8 %shard_map.62.ours = f32[2,8,2,2,8,512]{5,4,3,2,1,0:T(8,128)S(1)} custom-call(f32[36,2048]{1,0:T(8,128)S(1)} %get-tuple-element.17.factors, bf16[64,2048]{1,0:T(8,128)(2,1)S(1)} %bitcast.11, bf16[64,2048]{1,0:T(8,128)(2,1)S(1)} %collective-permute-done.sib, bf16[64,2048]{1,0:T(8,128)(2,1)S(1)} %collective-permute-done.1.far_own, ...), custom_call_target="tpu_custom_call" | custom-call | flops 268435456 | bytes 1048576 | tf_op jit(solution)/shard_map/pallas_call | solution.py:188
  40.1 2.3 %collective-permute-done.8.near = bf16[2,8,2,8,512]{4,3,2,1,0:T(8,128)(2,1)S(1)} collective-permute-done((bf16[2,8,2,8,512]{4,3,2,1,0:T(8,128)(2,1)S(1)}, bf16[2,8,2,8,512]{4,3,2,1,0:T(8,128)(2,1)S(1)}, u32[]{:S(2)}, u32[]{:S(2)}) %collective-permute-start.8) | collective-permute-done | bytes 262176 | tf_op jit(solution)/shard_map/ppermute | solution.py:322
  42.4 0.0 collective-permute-done.7.arrived
  42.4 0.2 shard_map.63
  42.6 17.5 %all_to_all.11.parts = bf16[8,2,2,8,1024]{4,3,2,1,0:T(8,128)(2,1)S(1)} all-to-all(bf16[8,2,2,8,1024]{4,3,2,1,0:T(8,128)(2,1)S(1)} %shard_map.63), channel_id=1, replica_groups=mesh['ckpt'=4,'tensor'=8] {'tensor'}, dimensions={0} | all-to-all | bytes 1048576 | tf_op jit(solution)/shard_map/all_to_all | solution.py:340
  60.1 0.7 %shard_map.64 = bf16[32,512]{1,0:T(8,128)(2,1)} custom-call(bf16[8,2,2,8,1024]{4,3,2,1,0:T(8,128)(2,1)S(1)} %all_to_all.11.parts), custom_call_target="tpu_custom_call" | custom-call | tf_op jit(solution)/shard_map/pallas_call | solution.py:341
  (3 shorter events, 0.1 us)
Async XLA Ops:
  16.2 2.1 %collective-permute-start = (bf16[64,2048]{1,0:T(8,128)(2,1)S(1)}, bf16[64,2048]{1,0:T(8,128)(2,1)S(1)}, u32[]{:S(2)}, u32[]{:S(2)}) collective-permute-start(bf16[64,2048]{1,0:T(8,128)(2,1)S(1)} %bitcast.6), channel_id=1, source_target_pairs={{0,8},{8,0},{16,24},{24,16},{1,9},{9,1},{17,25},{25,17},{2,10},{10... | collective-permute-start | bytes 786440 | tf_op jit(solution)/shard_map/ppermute | solution.py:248
  16.2 8.8 %collective-permute-start.1 = (bf16[64,2048]{1,0:T(8,128)(2,1)S(1)}, bf16[64,2048]{1,0:T(8,128)(2,1)S(1)}, u32[]{:S(2)}, u32[]{:S(2)}) collective-permute-start(bf16[64,2048]{1,0:T(8,128)(2,1)S(1)} %bitcast.7), channel_id=1, source_target_pairs={{0,16},{8,24},{16,0},{24,8},{1,17},{9,25},{17,1},{25,9},{2,18},{10... | collective-permute-start | bytes 786440 | tf_op jit(solution)/shard_map/ppermute | solution.py:247
  22.6 2.3 %collective-permute-start.2 = (bf16[8,2,8,512]{3,2,1,0:T(8,128)(2,1)S(1)}, bf16[8,2,8,512]{3,2,1,0:T(8,128)(2,1)S(1)}, u32[]{:S(2)}, u32[]{:S(2)}) collective-permute-start(bf16[8,2,8,512]{3,2,1,0:T(8,128)(2,1)S(1)} %get-tuple-element.19), channel_id=1, source_target_pairs={{0,8},{8,0},{16,24},{24,16},{1,9},{9,1},{17,25},{25,17},{2,10},{10... | collective-permute-start | bytes 393224 | tf_op jit(solution)/shard_map/ppermute | solution.py:272
  22.9 2.0 %collective-permute-start.3 = (bf16[8,2,8,512]{3,2,1,0:T(8,128)(2,1)S(1)}, bf16[8,2,8,512]{3,2,1,0:T(8,128)(2,1)S(1)}, u32[]{:S(2)}, u32[]{:S(2)}) collective-permute-start(bf16[8,2,8,512]{3,2,1,0:T(8,128)(2,1)S(1)} %get-tuple-element.20), channel_id=1, source_target_pairs={{0,8},{8,0},{16,24},{24,16},{1,9},{9,1},{17,25},{25,17},{2,10},{10... | collective-permute-start | bytes 393224 | tf_op jit(solution)/shard_map/ppermute | solution.py:272
  25.0 1.6 %collective-permute-start.4 = (bf16[64,2048]{1,0:T(8,128)(2,1)S(1)}, bf16[64,2048]{1,0:T(8,128)(2,1)S(1)}, u32[]{:S(2)}, u32[]{:S(2)}) collective-permute-start(bf16[64,2048]{1,0:T(8,128)(2,1)S(1)} %collective-permute-done.1.far_own), channel_id=1, source_target_pairs={{0,8},{8,0},{16,24},{24,16},{1,9},{9,1},{17,25},{25,17},{2,10},{10... | collective-permute-start | bytes 786440 | tf_op jit(solution)/shard_map/ppermute | solution.py:293
  25.3 8.5 %collective-permute-start.6 = (bf16[2,8,2,8,512]{4,3,2,1,0:T(8,128)(2,1)S(1)}, bf16[2,8,2,8,512]{4,3,2,1,0:T(8,128)(2,1)S(1)}, u32[]{:S(2)}, u32[]{:S(2)}) collective-permute-start(bf16[2,8,2,8,512]{4,3,2,1,0:T(8,128)(2,1)S(1)} %shard_map.57.after), channel_id=1, source_target_pairs={{0,16},{8,24},{16,0},{24,8},{1,17},{9,25},{17,1},{25,9},{2,18},{10... | collective-permute-start | bytes 786440 | tf_op jit(solution)/shard_map/ppermute | solution.py:291
  30.1 3.8 %collective-permute-start.5 = (bf16[2,8,2,8,512]{4,3,2,1,0:T(8,128)(2,1)S(1)}, bf16[2,8,2,8,512]{4,3,2,1,0:T(8,128)(2,1)S(1)}, u32[]{:S(2)}, u32[]{:S(2)}) collective-permute-start(bf16[2,8,2,8,512]{4,3,2,1,0:T(8,128)(2,1)S(1)} %get-tuple-element.25), channel_id=1, source_target_pairs={{0,8},{8,0},{16,24},{24,16},{1,9},{9,1},{17,25},{25,17},{2,10},{10... | collective-permute-start | bytes 786440 | tf_op jit(solution)/shard_map/ppermute | solution.py:303
  33.5 8.9 %collective-permute-start.7 = (bf16[2,8,2,2,8,512]{5,4,3,2,1,0:T(8,128)(2,1)S(1)}, bf16[2,8,2,2,8,512]{5,4,3,2,1,0:T(8,128)(2,1)S(1)}, u32[]{:S(2)}, u32[]{:S(2)}) collective-permute-start(bf16[2,8,2,2,8,512]{5,4,3,2,1,0:T(8,128)(2,1)S(1)} %shard_map.59), channel_id=1, source_target_pairs={{0,8},{8,0},{16,24},{24,16},{1,9},{9,1},{17,25},{25,17},{2,10},{10... | collective-permute-start | bytes 1572872 | tf_op jit(solution)/shard_map/ppermute | solution.py:320
  33.9 8.5 %collective-permute-start.8 = (bf16[2,8,2,8,512]{4,3,2,1,0:T(8,128)(2,1)S(1)}, bf16[2,8,2,8,512]{4,3,2,1,0:T(8,128)(2,1)S(1)}, u32[]{:S(2)}, u32[]{:S(2)}) collective-permute-start(bf16[2,8,2,8,512]{4,3,2,1,0:T(8,128)(2,1)S(1)} %shard_map.61), channel_id=1, source_target_pairs={{0,16},{8,24},{16,0},{24,8},{1,17},{9,25},{17,1},{25,9},{2,18},{10... | collective-permute-start | bytes 786440 | tf_op jit(solution)/shard_map/ppermute | solution.py:322

commit v9 on v8

--- a/solution.py
+++ b/solution.py
@@ -27,9 +27,10 @@
 
 
 def gather_held(held, pieces):
-    for i, piece in enumerate(pieces):
-        span = piece.shape[0]
-        held[i * span : (i + 1) * span] = piece[...]
+    at = 0
+    for piece in pieces:
+        held[at : at + piece.shape[0]] = piece[...]
+        at += piece.shape[0]
 
 
 def expand(mask, scale, factors):
@@ -115,13 +116,10 @@
     mask_copy.wait()
     expand(mask[...], scale_num[0].astype(jnp.float32) / DEN, factors)
 
-    @pl.loop(0, 2)
-    def _(part):
+    for part, view in enumerate((gate, up)):
         rows.wait(part)
-        first = first_factor(kept, factors, part, rows.owner(part))
-        total = product(held[...], factors, kept.at[part], first)
-        pl.when(part == 0)(lambda: put(gate, total, core))
-        pl.when(part == 1)(lambda: put(up, total, core))
+        first = first_factor(kept, factors, part, (1 - chip) * CORES + 1 - core)
+        put(view, product(held[...], factors, kept.at[part], first), core)
 
     for part in (2, 3):
         rows.wait(part)
@@ -137,9 +135,11 @@
         put(ours.at[part], product(held[...], factors, kept.at[2 + part], first), core)
 
 
-def later_kernel(factors, far_own, far_sib, kept, after, theirs, ours, held):
+def later_kernel(factors, far_own, far_sib_0, far_sib_1, kept, after, delta, theirs, ours, home, held, sems):
     chip, core = chip_and_core()
-    gather_held(held, (far_own, far_sib))
+    rows = Rows(delta, home, sems, [chip * CORES + 1 - core])
+    rows.start()
+    gather_held(held, (far_own, far_sib_0, far_sib_1))
     far = Rows(None, kept, None, [(1 - chip) * CORES + at for at in (1 - core, core)])
 
     @pl.loop(0, 4)
@@ -149,27 +149,29 @@
         pl.when(part < 2)(lambda: put(theirs.at[part % 2], total, core))
         pl.when(part >= 2)(lambda: put(ours.at[part % 2], total, core))
 
-
-def home_sib_kernel(factors, own, sib, far_own, far_sib, delta, theirs, home, held, sems):
+    for part in range(2):
+        rows.wait(part)
+
+
+def home_sib_kernel(factors, own, sib, far_own, far_sib_0, far_sib_1, home, theirs, held):
     chip, core = chip_and_core()
-    rows = Rows(delta, home, sems, [chip * CORES + 1 - core])
-    rows.start()
-    gather_held(held, (own, sib, far_own, far_sib))
+    gather_held(held, (own, sib, far_own, far_sib_0, far_sib_1))
 
     @pl.loop(0, 2)
     def _(part):
-        rows.wait(part)
-        first = first_factor(home, factors, part, rows.owner(part))
+        first = first_factor(home, factors, part, chip * CORES + 1 - core)
         put(theirs.at[part], product(held[...], factors, home.at[part], first), core)
 
 
-def home_kernel(factors, own, sib, far_own, far_sib, delta, base, ours, kept, held, total, sems):
+def home_kernel(
+    factors, own, sib, far_own, far_sib_0, far_sib_1, delta, base, ours, kept, held, total, sems
+):
     chip, core = chip_and_core()
     rows = Rows(delta, kept, sems, [chip * CORES + core])
     base_rows = Rows(base, kept, sems, [0], first=2)
     rows.start()
     base_rows.start()
-    gather_held(held, (own, sib, far_own, far_sib))
+    gather_held(held, (own, sib, far_own, far_sib_0, far_sib_1))
     total[...] = jnp.zeros_like(total)
     ones = factors.shape[0] - kept.shape[1] // BLOCK
 
@@ -290,27 +292,23 @@
     first = simple(join_halves_kernel, pair, ours, *near)
     over_first = chip_swap(first)
     far_own, first = lax.optimization_barrier((far_own, first))
-    far_sib = core_swap(far_own)
-    theirs, ours = call(
+    far_sib = [core_swap(far_own[: half // 4]), core_swap(far_own[half // 4 :])]
+    theirs, ours, home = call(
         later_kernel,
-        [part(pair, bf16), part(pair, f32)],
-        [pltpu.VMEM((half, width), bf16)],
-        [VMEM] * 4 + [pl.BlockSpec(memory_space=pl.ANY)],
-        (factors, far_own, far_sib, kept, first),
-        2 * half * size,
-        2 * size,
+        [part(pair, bf16), part(pair, f32), part((2, slab_own, width), bf16)],
+        [pltpu.VMEM((half, width), bf16), pltpu.SemaphoreType.DMA((2, chunks))],
+        [VMEM] * 5 + [pl.BlockSpec(memory_space=pl.ANY), HBM],
+        (factors, far_own, *far_sib, kept, first, delta),
+        size,
+        size,
     )
     near = core_swap(theirs)
     (theirs_home,) = call(
         home_sib_kernel,
         [part(four, bf16)],
-        [
-            pltpu.VMEM((2, slab_own, width), bf16),
-            pltpu.VMEM((2 * half, width), bf16),
-            pltpu.SemaphoreType.DMA((2, chunks)),
-        ],
-        [VMEM] * 5 + [HBM],
-        (factors, own, sib, far_own, far_sib, delta),
+        [pltpu.VMEM((2 * half, width), bf16)],
+        [VMEM] * 7,
+        (factors, own, sib, far_own, *far_sib, home),
         size,
         size,
     )
@@ -329,8 +327,8 @@
             pltpu.VMEM((2, 2 * half, slab_own), f32),
             pltpu.SemaphoreType.DMA((4, chunks)),
         ],
-        [VMEM] * 5 + [HBM, HBM],
-        (factors, own, sib, far_own, far_sib, delta, base),
+        [VMEM] * 6 + [HBM, HBM],
+        (factors, own, sib, far_own, *far_sib, delta, base),
         4 * half * size,
         2 * size,
     )

time: 61 us -> 58.9 us (0.966)
  Pallas kernels: 18.3 us -> 16 us
  blocking collectives: 33.7 us -> 32.5 us
  starting transfers between devices: 5.53 us -> 6.32 us
    pallas_call x5, Pallas kernels: 17.3 us -> 15.1 us  [call(): pl.pallas_call(kernel, out_shape=outs, in_specs=in_specs, out_specs=[VMEM...]
    ppermute x1, waiting for transfers between devices: 2.34 us -> 1.17 us  [local_pair(): over_second = chip_swap(second)]
    all_to_all x1, blocking collectives: 17.5 us -> 16.4 us  [local_pair(): parts = lax.all_to_all(whole, 'tensor', 0, 0, tiled=True)]
    ppermute x1, waiting for transfers between devices: 0.01 us -> 1.05 us  [local_pair(): over_first = chip_swap(first)]
    ppermute x1, waiting for transfers between devices: 0.01 us -> 0.68 us  [local_pair(): far_own = chip_swap(own)]
  transfers between devices with their start and end apart: 9 -> 10, of which waited for: 2 -> 3; matrix products, arithmetic and copies ran while one was open for 0% -> 0% of each run, Pallas kernels for 29% -> 26%
where the time goes in v9:
time: 58.9 us; the launch traced here: 58.6 us
  blocking collectives  32.5 us (55%)
  Pallas kernels  16 us (27%)
  starting transfers between devices  6.32 us (11%)
  waiting for transfers between devices  2.92 us (5%)
  between operations  0.77 us (1%)
    all_to_all x1, blocking collectives, local_pair(): parts = lax.all_to_all(whole, 'tensor', 0, 0, tiled=True)  16.4 us
    all_to_all x1, blocking collectives, local_pair(): lax.all_to_all(cut, 'tensor', 0, 0, tiled=True)  16.2 us
    pallas_call x5, Pallas kernels, call(): pl.pallas_call(kernel, out_shape=outs, in_specs=in_specs, out_specs=[VMEM...  15.1 us
    ppermute x1, starting transfers between devices, local_pair(): over_second = chip_swap(second)  1.56 us
    ppermute x1, starting transfers between devices, local_pair(): far_own = chip_swap(own)  1.49 us
    ppermute x1, starting transfers between devices, local_pair(): over_first = chip_swap(first)  1.49 us
  transfers between devices with their start and end apart: 10, of which 3 were waited for; matrix products, arithmetic and copies ran while one was open for 0% of the time, Pallas kernels for 26%

profile of v9, /device:TPU:0, one launch (start us, length us, event | category | flops | bytes accessed | tf_op | source)
XLA Modules:
  0.0 58.6 jit_solution(2831043472437188116)
XLA Ops:
  0.0 16.2 %all_to_all.10 = bf16[8,8,2048]{2,1,0:T(8,128)(2,1)S(1)} all-to-all(bf16[8,8,2048]{2,1,0:T(8,128)(2,1)} %bitcast.15), channel_id=1, replica_groups=mesh['ckpt'=4,'tensor'=8] {'tensor'}, dimensions={0} | all-to-all | bytes 524288 | tf_op jit(solution)/shard_map/all_to_all | solution.py:248
  16.2 0.0 collective-permute-start
  16.2 1.5 %collective-permute-start.1 = (bf16[64,2048]{1,0:T(8,128)(2,1)S(1)}, bf16[64,2048]{1,0:T(8,128)(2,1)S(1)}, u32[]{:S(2)}, u32[]{:S(2)}) collective-permute-start(bf16[64,2048]{1,0:T(8,128)(2,1)S(1)} %bitcast.7), channel_id=1, source_target_pairs={{0,16},{8,24},{16,0},{24,8},{1,17},{9,25},{17,1},{25,9},{2,18},{10... | collective-permute-start | bytes 786440 | tf_op jit(solution)/shard_map/ppermute | solution.py:249
  18.3 0.0 collective-permute-done.sib
  18.4 3.5 %shard_map.55 = (bf16[8,2,8,512]{3,2,1,0:T(8,128)(2,1)S(1)}, bf16[8,2,8,512]{3,2,1,0:T(8,128)(2,1)S(1)}, bf16[4,512,2048]{2,1,0:T(8,128)(2,1)S(1)}, f32[36,2048]{1,0:T(8,128)S(1)}) custom-call(s32[1]{0:T(128)S(6)} %copy.6.scale_num, s32[2,16,16]{2,1,0:T(8,128)} %bitcast.16, bf16[64,2048]{1,0:T(8,128)(2,1)S(1)} %bitcast.8, ...), custom_call_target="tpu_custom_call" | custom-call | flops 67108864 | bytes 1048576 | tf_op jit(solution)/shard_map/pallas_call | solution.py:190
  21.9 0.3 collective-permute-start.2
  22.2 0.3 collective-permute-start.3
  22.4 1.7 %shard_map.56.ours = f32[2,8,2,8,512]{4,3,2,1,0:T(8,128)S(1)} custom-call(f32[36,2048]{1,0:T(8,128)S(1)} %get-tuple-element.18.factors, bf16[64,2048]{1,0:T(8,128)(2,1)S(1)} %bitcast.9, bf16[64,2048]{1,0:T(8,128)(2,1)S(1)} %collective-permute-done.sib, bf16[4,512,2048]{2,1,0:T(8,128)(2,1)S(1)} %get-tuple-element.19.kept), custom_call_target="tpu_custom_call" | custom-call | flops 1 | bytes 1 | tf_op jit(solution)/shard_map/pallas_call | solution.py:190
  24.2 0.0 collective-permute-done.2.gate
  24.2 0.0 collective-permute-done.3.up
  24.2 0.7 %collective-permute-done.1.far_own = bf16[64,2048]{1,0:T(8,128)(2,1)S(1)} collective-permute-done((bf16[64,2048]{1,0:T(8,128)(2,1)S(1)}, bf16[64,2048]{1,0:T(8,128)(2,1)S(1)}, u32[]{:S(2)}, u32[]{:S(2)}) %collective-permute-start.1) | collective-permute-done | bytes 262176 | tf_op jit(solution)/shard_map/ppermute | solution.py:249
  24.9 0.1 collective-permute-start.5
  25.0 0.5 collective-permute-start.4
  25.5 1.5 %collective-permute-start.7 = (bf16[2,8,2,8,512]{4,3,2,1,0:T(8,128)(2,1)S(1)}, bf16[2,8,2,8,512]{4,3,2,1,0:T(8,128)(2,1)S(1)}, u32[]{:S(2)}, u32[]{:S(2)}) collective-permute-start(bf16[2,8,2,8,512]{4,3,2,1,0:T(8,128)(2,1)S(1)} %shard_map.57.after), channel_id=1, source_target_pairs={{0,16},{8,24},{16,0},{24,8},{1,17},{9,25},{17,1},{25,9},{2,18},{10... | collective-permute-start | bytes 786440 | tf_op jit(solution)/shard_map/ppermute | solution.py:293
  27.0 0.0 collective-permute-done.5.far_sib_1
  27.0 0.0 collective-permute-done.4.far_sib_0
  27.0 3.5 %shard_map.58 = (bf16[2,8,2,8,512]{4,3,2,1,0:T(8,128)(2,1)S(1)}, f32[2,8,2,8,512]{4,3,2,1,0:T(8,128)S(1)}, bf16[2,512,2048]{2,1,0:T(8,128)(2,1)S(1)}) custom-call(f32[36,2048]{1,0:T(8,128)S(1)} %get-tuple-element.18.factors, bf16[64,2048]{1,0:T(8,128)(2,1)S(1)} %collective-permute-done.1.far_own, bf16[32,2048]{1,0:T(8,128)(2,1)S(1)} %collective-permute-done.4.far_sib_0, ...), custom_call_target="tpu_custom_call" | custom-call | flops 524288 | bytes 524288 | tf_op jit(solution)/shard_map/pallas_call | solution.py:190
  30.5 0.1 collective-permute-start.6
  30.6 1.6 %shard_map.59 = bf16[2,8,2,2,8,512]{5,4,3,2,1,0:T(8,128)(2,1)S(1)} custom-call(f32[36,2048]{1,0:T(8,128)S(1)} %get-tuple-element.18.factors, bf16[64,2048]{1,0:T(8,128)(2,1)S(1)} %bitcast.10, bf16[64,2048]{1,0:T(8,128)(2,1)S(1)} %collective-permute-done.sib, bf16[64,2048]{1,0:T(8,128)(2,1)S(1)} %collective-permute-done.1.far_own, ...), custom_call_target="tpu_custom_call" | custom-call | flops 524288 | bytes 524288 | tf_op jit(solution)/shard_map/pallas_call | solution.py:190
  32.2 0.6 collective-permute-start.8
  32.8 1.0 %collective-permute-done.7.arrived.far = bf16[2,8,2,8,512]{4,3,2,1,0:T(8,128)(2,1)S(1)} collective-permute-done((bf16[2,8,2,8,512]{4,3,2,1,0:T(8,128)(2,1)S(1)}, bf16[2,8,2,8,512]{4,3,2,1,0:T(8,128)(2,1)S(1)}, u32[]{:S(2)}, u32[]{:S(2)}) %collective-permute-start.7) | collective-permute-done | bytes 262176 | tf_op jit(solution)/shard_map/ppermute | solution.py:293
  33.8 0.0 collective-permute-done.6.arrived
  33.9 1.6 %collective-permute-start.9 = (bf16[2,8,2,8,512]{4,3,2,1,0:T(8,128)(2,1)S(1)}, bf16[2,8,2,8,512]{4,3,2,1,0:T(8,128)(2,1)S(1)}, u32[]{:S(2)}, u32[]{:S(2)}) collective-permute-start(bf16[2,8,2,8,512]{4,3,2,1,0:T(8,128)(2,1)S(1)} %shard_map.61), channel_id=1, source_target_pairs={{0,16},{8,24},{16,0},{24,8},{1,17},{9,25},{17,1},{25,9},{2,18},{10... | collective-permute-start | bytes 786440 | tf_op jit(solution)/shard_map/ppermute | solution.py:320
  35.4 4.8 %shard_map.62.ours = f32[2,8,2,2,8,512]{5,4,3,2,1,0:T(8,128)S(1)} custom-call(f32[36,2048]{1,0:T(8,128)S(1)} %get-tuple-element.18.factors, bf16[64,2048]{1,0:T(8,128)(2,1)S(1)} %bitcast.11, bf16[64,2048]{1,0:T(8,128)(2,1)S(1)} %collective-permute-done.sib, bf16[64,2048]{1,0:T(8,128)(2,1)S(1)} %collective-permute-done.1.far_own, ...), custom_call_target="tpu_custom_call" | custom-call | flops 268435456 | bytes 1048576 | tf_op jit(solution)/shard_map/pallas_call | solution.py:190
  40.2 0.0 collective-permute-done.8.arrived
  40.2 1.2 %collective-permute-done.9.near = bf16[2,8,2,8,512]{4,3,2,1,0:T(8,128)(2,1)S(1)} collective-permute-done((bf16[2,8,2,8,512]{4,3,2,1,0:T(8,128)(2,1)S(1)}, bf16[2,8,2,8,512]{4,3,2,1,0:T(8,128)(2,1)S(1)}, u32[]{:S(2)}, u32[]{:S(2)}) %collective-permute-start.9) | collective-permute-done | bytes 262176 | tf_op jit(solution)/shard_map/ppermute | solution.py:320
  41.4 0.2 shard_map.63
  41.5 16.4 %all_to_all.11.parts = bf16[8,2,2,8,1024]{4,3,2,1,0:T(8,128)(2,1)S(1)} all-to-all(bf16[8,2,2,8,1024]{4,3,2,1,0:T(8,128)(2,1)S(1)} %shard_map.63), channel_id=1, replica_groups=mesh['ckpt'=4,'tensor'=8] {'tensor'}, dimensions={0} | all-to-all | bytes 1048576 | tf_op jit(solution)/shard_map/all_to_all | solution.py:338
  57.9 0.7 %shard_map.64 = bf16[32,512]{1,0:T(8,128)(2,1)} custom-call(bf16[8,2,2,8,1024]{4,3,2,1,0:T(8,128)(2,1)S(1)} %all_to_all.11.parts), custom_call_target="tpu_custom_call" | custom-call | tf_op jit(solution)/shard_map/pallas_call | solution.py:339
  (4 shorter events, 0.1 us)
Async XLA Ops:
  16.2 2.1 %collective-permute-start = (bf16[64,2048]{1,0:T(8,128)(2,1)S(1)}, bf16[64,2048]{1,0:T(8,128)(2,1)S(1)}, u32[]{:S(2)}, u32[]{:S(2)}) collective-permute-start(bf16[64,2048]{1,0:T(8,128)(2,1)S(1)} %bitcast.6), channel_id=1, source_target_pairs={{0,8},{8,0},{16,24},{24,16},{1,9},{9,1},{17,25},{25,17},{2,10},{10... | collective-permute-start | bytes 786440 | tf_op jit(solution)/shard_map/ppermute | solution.py:250
  16.2 8.7 %collective-permute-start.1 = (bf16[64,2048]{1,0:T(8,128)(2,1)S(1)}, bf16[64,2048]{1,0:T(8,128)(2,1)S(1)}, u32[]{:S(2)}, u32[]{:S(2)}) collective-permute-start(bf16[64,2048]{1,0:T(8,128)(2,1)S(1)} %bitcast.7), channel_id=1, source_target_pairs={{0,16},{8,24},{16,0},{24,8},{1,17},{9,25},{17,1},{25,9},{2,18},{10... | collective-permute-start | bytes 786440 | tf_op jit(solution)/shard_map/ppermute | solution.py:249
  21.9 2.3 %collective-permute-start.2 = (bf16[8,2,8,512]{3,2,1,0:T(8,128)(2,1)S(1)}, bf16[8,2,8,512]{3,2,1,0:T(8,128)(2,1)S(1)}, u32[]{:S(2)}, u32[]{:S(2)}) collective-permute-start(bf16[8,2,8,512]{3,2,1,0:T(8,128)(2,1)S(1)} %get-tuple-element.20), channel_id=1, source_target_pairs={{0,8},{8,0},{16,24},{24,16},{1,9},{9,1},{17,25},{25,17},{2,10},{10... | collective-permute-start | bytes 393224 | tf_op jit(solution)/shard_map/ppermute | solution.py:274
  22.2 2.0 %collective-permute-start.3 = (bf16[8,2,8,512]{3,2,1,0:T(8,128)(2,1)S(1)}, bf16[8,2,8,512]{3,2,1,0:T(8,128)(2,1)S(1)}, u32[]{:S(2)}, u32[]{:S(2)}) collective-permute-start(bf16[8,2,8,512]{3,2,1,0:T(8,128)(2,1)S(1)} %get-tuple-element.21), channel_id=1, source_target_pairs={{0,8},{8,0},{16,24},{24,16},{1,9},{9,1},{17,25},{25,17},{2,10},{10... | collective-permute-start | bytes 393224 | tf_op jit(solution)/shard_map/ppermute | solution.py:274
  24.9 2.1 %collective-permute-start.5 = (bf16[32,2048]{1,0:T(8,128)(2,1)S(1)}, bf16[32,2048]{1,0:T(8,128)(2,1)S(1)}, u32[]{:S(2)}, u32[]{:S(2)}) collective-permute-start(bf16[32,2048]{1,0:T(8,128)(2,1)S(1)} %get-tuple-element.31), channel_id=1, source_target_pairs={{0,8},{8,0},{16,24},{24,16},{1,9},{9,1},{17,25},{25,17},{2,10},{10... | collective-permute-start | bytes 393224 | tf_op jit(solution)/shard_map/ppermute | solution.py:295
  25.0 2.0 %collective-permute-start.4 = (bf16[32,2048]{1,0:T(8,128)(2,1)S(1)}, bf16[32,2048]{1,0:T(8,128)(2,1)S(1)}, u32[]{:S(2)}, u32[]{:S(2)}) collective-permute-start(bf16[32,2048]{1,0:T(8,128)(2,1)S(1)} %get-tuple-element.32), channel_id=1, source_target_pairs={{0,8},{8,0},{16,24},{24,16},{1,9},{9,1},{17,25},{25,17},{2,10},{10... | collective-permute-start | bytes 393224 | tf_op jit(solution)/shard_map/ppermute | solution.py:295
  25.5 8.3 %collective-permute-start.7 = (bf16[2,8,2,8,512]{4,3,2,1,0:T(8,128)(2,1)S(1)}, bf16[2,8,2,8,512]{4,3,2,1,0:T(8,128)(2,1)S(1)}, u32[]{:S(2)}, u32[]{:S(2)}) collective-permute-start(bf16[2,8,2,8,512]{4,3,2,1,0:T(8,128)(2,1)S(1)} %shard_map.57.after), channel_id=1, source_target_pairs={{0,16},{8,24},{16,0},{24,8},{1,17},{9,25},{17,1},{25,9},{2,18},{10... | collective-permute-start | bytes 786440 | tf_op jit(solution)/shard_map/ppermute | solution.py:293
  30.5 3.3 %collective-permute-start.6 = (bf16[2,8,2,8,512]{4,3,2,1,0:T(8,128)(2,1)S(1)}, bf16[2,8,2,8,512]{4,3,2,1,0:T(8,128)(2,1)S(1)}, u32[]{:S(2)}, u32[]{:S(2)}) collective-permute-start(bf16[2,8,2,8,512]{4,3,2,1,0:T(8,128)(2,1)S(1)} %get-tuple-element.27), channel_id=1, source_target_pairs={{0,8},{8,0},{16,24},{24,16},{1,9},{9,1},{17,25},{25,17},{2,10},{10... | collective-permute-start | bytes 786440 | tf_op jit(solution)/shard_map/ppermute | solution.py:305
  32.2 8.0 %collective-permute-start.8 = (bf16[2,8,2,2,8,512]{5,4,3,2,1,0:T(8,128)(2,1)S(1)}, bf16[2,8,2,2,8,512]{5,4,3,2,1,0:T(8,128)(2,1)S(1)}, u32[]{:S(2)}, u32[]{:S(2)}) collective-permute-start(bf16[2,8,2,2,8,512]{5,4,3,2,1,0:T(8,128)(2,1)S(1)} %shard_map.59), channel_id=1, source_target_pairs={{0,8},{8,0},{16,24},{24,16},{1,9},{9,1},{17,25},{25,17},{2,10},{10... | collective-permute-start | bytes 1572872 | tf_op jit(solution)/shard_map/ppermute | solution.py:318
  33.9 7.5 %collective-permute-start.9 = (bf16[2,8,2,8,512]{4,3,2,1,0:T(8,128)(2,1)S(1)}, bf16[2,8,2,8,512]{4,3,2,1,0:T(8,128)(2,1)S(1)}, u32[]{:S(2)}, u32[]{:S(2)}) collective-permute-start(bf16[2,8,2,8,512]{4,3,2,1,0:T(8,128)(2,1)S(1)} %shard_map.61), channel_id=1, source_target_pairs={{0,16},{8,24},{16,0},{24,8},{1,17},{9,25},{17,1},{25,9},{2,18},{10... | collective-permute-start | bytes 786440 | tf_op jit(solution)/shard_map/ppermute | solution.py:320
